TPU v7x, 32 devices: a whole 2x2x4 slice. The times are simulated.
32 devices in a mesh: fsdp: 8 (over z, x), seq: 4 (over y, core).
Axes of the slice: x: 2, y: 2, z: 4, core: 2. Of those that a mesh axis runs over, the one named last changes fastest.
Arguments:
- tokens: bfloat16 [16, 1024, 1024], P('fsdp', 'seq'), may hold values from -6 to 6
- w_query: bfloat16 [1024, 1024], P('fsdp'), may hold values from -0.1875 to 0.1875
- w_key: bfloat16 [1024, 512], P('fsdp'), may hold values from -0.1875 to 0.1875
- w_value: bfloat16 [1024, 512], P('fsdp'), may hold values from -0.1875 to 0.1875
- w_out: bfloat16 [1024, 1024], P('fsdp'), may hold values from -0.75 to 0.75
- w_gate: bfloat16 [1024, 4608], P('fsdp'), may hold values from -0.1875 to 0.1875
- w_up: bfloat16 [1024, 4608], P('fsdp'), may hold values from -0.1875 to 0.1875
- w_down: bfloat16 [4608, 1024], P('fsdp'), may hold values from -0.125 to 0.125
- attn_gain: bfloat16 [1024], P('fsdp'), may hold values from 0.099609375 to 1.8984375
- ffn_gain: bfloat16 [1024], P('fsdp'), may hold values from 0.099609375 to 1.8984375
- qk_gain: bfloat16 [2, 64], replicated, may hold values from 0.099609375 to 1.8984375
- cotangent: bfloat16 [16, 1024, 1024], P('fsdp', 'seq'), may hold values from -6 to 6
Outputs:
- out: bfloat16 [16, 1024, 1024], P('fsdp', 'seq')
- grad_tokens: float32 [16, 1024, 1024], P('fsdp', 'seq')
- grad_query: float32 [1024, 1024], P('fsdp')
- grad_key: float32 [1024, 512], P('fsdp')
- grad_value: float32 [1024, 512], P('fsdp')
- grad_out: float32 [1024, 1024], P('fsdp')
- grad_gate: float32 [1024, 4608], P('fsdp')
- grad_up: float32 [1024, 4608], P('fsdp')
- grad_down: float32 [4608, 1024], P('fsdp')
- grad_attn_gain: float32 [1024], P('fsdp')
- grad_ffn_gain: float32 [1024], P('fsdp')
- grad_qk_gain: float32 [2, 64], replicated
All inputs are finite; a program needn't handle non-finite values.
Results may differ from a plain program's by a relative error of at most 0.022.
Values may be sent and summed in bfloat16 or wider, within the bound.
No kernel may reach another device: no remote copies, remote signals or barrier semaphores. Data moves between devices by JAX's collectives and lax.ppermute only.
A program may use at most 192 MiB of HBM per device.

v0:
```python
import jax
import jax.numpy as jnp
from jax import lax
from jax.sharding import PartitionSpec as P

HD = 64


RMS_EPSILON = 1e-05
ROPE_THETA = 1000000.0
NEG_LARGE = -1e30


def rms_scale(values):
    return lax.rsqrt(jnp.mean(values * values, axis=-1, keepdims=True) + RMS_EPSILON)


def rope_tables(positions, head_size):
    half_size = head_size // 2
    freqs = ROPE_THETA ** (-(jnp.arange(half_size, dtype=jnp.float32) * 2.0) / head_size)
    angles = positions.astype(jnp.float32)[:, None] * freqs[None, :]
    angles = jnp.concatenate([angles, angles], axis=-1)
    return (jnp.cos(angles), jnp.sin(angles))


def rotate(values):
    half_size = values.shape[-1] // 2
    return jnp.concatenate([-values[..., half_size:], values[..., :half_size]], axis=-1)


def rotate_back(values):
    half_size = values.shape[-1] // 2
    return jnp.concatenate([values[..., half_size:], -values[..., :half_size]], axis=-1)


def head_rope(flat, gain, cosine, sine):
    shaped = flat.reshape(flat.shape[:-1] + (-1, HD))
    scale = rms_scale(shaped)
    normed = shaped * scale * gain
    turned = normed * cosine[:, None, :] + rotate(normed) * sine[:, None, :]
    return (turned.reshape(flat.shape), scale)


def head_rope_back(grad_flat, flat, scale, gain, cosine, sine):
    shaped = flat.reshape(flat.shape[:-1] + (-1, HD))
    grad_turned = grad_flat.reshape(shaped.shape)
    grad_normed = grad_turned * cosine[:, None, :] + rotate_back(grad_turned * sine[:, None, :])
    grad_gain = jnp.sum(grad_normed * shaped * scale, axis=(0, 1, 2))
    weighted = grad_normed * gain
    grad_shaped = scale * weighted - shaped * scale**3 * jnp.mean(
        weighted * shaped, axis=-1, keepdims=True
    )
    return (grad_shaped.reshape(flat.shape), grad_gain)


def norm_back(grad, values, scale, gain):
    weighted = grad * gain
    grad_values = scale * weighted - values * scale**3 * jnp.mean(
        weighted * values, axis=-1, keepdims=True
    )
    grad_gain = jnp.sum(grad * values * scale, axis=(0, 1))
    return (grad_values, grad_gain)


def to_blocks(flat, count, kv_heads):
    batch, length, width = flat.shape
    group = width // (kv_heads * HD)
    shaped = flat.reshape(batch, count, length // count, kv_heads, group, HD)
    return jnp.moveaxis(shaped, 1, 0)


def split_heads(query_flat, key_flat, value_flat):
    batch, length, width = query_flat.shape
    kv_heads = key_flat.shape[2] // HD
    block_rows = min(512, length)
    count = length // block_rows
    query_blocks = to_blocks(query_flat, count, kv_heads)
    key_heads = key_flat.reshape(batch, length, kv_heads, HD)
    value_heads = value_flat.reshape(batch, length, kv_heads, HD)
    starts = jnp.arange(count) * block_rows
    return (query_blocks, key_heads, value_heads, starts)


def block_scores(query_block, key_heads, start):
    block_rows = query_block.shape[1]
    scores = jnp.einsum(
        "bqkgd,bskd->bkgqs", query_block, key_heads, preferred_element_type=jnp.float32
    ) * HD ** (-0.5)
    rows = start + jnp.arange(block_rows)
    columns = jnp.arange(key_heads.shape[1])
    causal = rows[:, None] >= columns[None, :]
    return (scores, causal)


def attend(parts):
    query_flat, key_flat, value_flat = parts
    batch, length, width = query_flat.shape
    query_blocks, key_heads, value_heads, starts = split_heads(query_flat, key_flat, value_flat)

    def one_block(pieces):
        query_block, start = pieces
        scores, causal = block_scores(query_block, key_heads, start)
        scores = jnp.where(causal, scores, NEG_LARGE)
        row_max = jnp.max(scores, axis=-1, keepdims=True)
        exp_part = jnp.exp(scores - row_max)
        row_sum = jnp.sum(exp_part, axis=-1, keepdims=True)
        probs = (exp_part / row_sum).astype(jnp.bfloat16)
        mixed = jnp.einsum(
            "bkgqs,bskd->bqkgd", probs, value_heads, preferred_element_type=jnp.float32
        )
        return (mixed.astype(jnp.bfloat16), (row_max + jnp.log(row_sum))[..., 0])

    mixed, log_sums = lax.map(one_block, (query_blocks, starts))
    mixed = jnp.moveaxis(mixed, 0, 1).reshape(batch, length, width)
    kv_heads = log_sums.shape[2]
    group = log_sums.shape[3]
    log_sums = jnp.moveaxis(log_sums, 0, 3).reshape(batch, kv_heads, group, length)
    return (mixed, log_sums, query_flat, key_flat, value_flat)


def attend_back(query_flat, key_flat, value_flat, log_sums, grad_mixed):
    batch, length, width = query_flat.shape
    query_blocks, key_heads, value_heads, starts = split_heads(query_flat, key_flat, value_flat)
    count = starts.shape[0]
    kv_heads = key_heads.shape[2]
    grad_blocks = to_blocks(grad_mixed, count, kv_heads)
    sum_blocks = jnp.moveaxis(log_sums.reshape(log_sums.shape[:3] + (count, length // count)), 3, 0)
    head_scale = HD ** (-0.5)

    def one_block(carry, pieces):
        grad_keys, grad_values = carry
        query_block, grad_block, sums_block, start = pieces
        scores, causal = block_scores(query_block, key_heads, start)
        probs = jnp.where(causal, jnp.exp(scores - sums_block[..., None]), 0.0)
        grad_values = grad_values + jnp.einsum(
            "bkgqs,bqkgd->bskd",
            probs.astype(jnp.bfloat16),
            grad_block,
            preferred_element_type=jnp.float32,
        )
        grad_probs = jnp.einsum(
            "bqkgd,bskd->bkgqs", grad_block, value_heads, preferred_element_type=jnp.float32
        )
        inner = jnp.sum(probs * grad_probs, axis=-1, keepdims=True)
        grad_scores = (probs * (grad_probs - inner)).astype(jnp.bfloat16)
        grad_query = (
            jnp.einsum(
                "bkgqs,bskd->bqkgd", grad_scores, key_heads, preferred_element_type=jnp.float32
            )
            * head_scale
        )
        grad_keys = (
            grad_keys
            + jnp.einsum(
                "bkgqs,bqkgd->bskd", grad_scores, query_block, preferred_element_type=jnp.float32
            )
            * head_scale
        )
        return ((grad_keys, grad_values), grad_query.astype(jnp.bfloat16))

    zero_heads = jnp.zeros(key_heads.shape, jnp.float32)
    (grad_keys, grad_values), grad_query = lax.scan(
        one_block, (zero_heads, zero_heads), (query_blocks, grad_blocks, sum_blocks, starts)
    )
    grad_query = jnp.moveaxis(grad_query, 0, 1).reshape(batch, length, width)
    grad_keys = grad_keys.reshape(key_flat.shape).astype(jnp.bfloat16)
    grad_values = grad_values.reshape(value_flat.shape).astype(jnp.bfloat16)
    return (grad_query, grad_keys, grad_values)


def per_device(
    tokens,
    w_query,
    w_key,
    w_value,
    w_out,
    w_gate,
    w_up,
    w_down,
    attn_gain,
    ffn_gain,
    qk_gain,
    cotangent,
):
    forward_weights = (
        lax.all_gather(w_query, "fsdp", axis=0, tiled=True),
        lax.all_gather(w_key, "fsdp", axis=0, tiled=True),
        lax.all_gather(w_value, "fsdp", axis=0, tiled=True),
        lax.all_gather(w_out, "fsdp", axis=0, tiled=True),
        lax.all_gather(w_gate, "fsdp", axis=0, tiled=True),
        lax.all_gather(w_up, "fsdp", axis=0, tiled=True),
        lax.all_gather(w_down, "fsdp", axis=0, tiled=True),
        lax.all_gather(attn_gain, "fsdp", axis=0, tiled=True),
        lax.all_gather(ffn_gain, "fsdp", axis=0, tiled=True),
    )
    query_all, key_all, value_all, out_all, gate_all, up_all, down_all, attn_all, ffn_all = (
        forward_weights
    )
    seq_rows = tokens.shape[1]
    positions = lax.axis_index("seq") * seq_rows + jnp.arange(seq_rows, dtype=jnp.int32)
    cosine, sine = rope_tables(positions, HD)
    query_gain = qk_gain[0].astype(jnp.float32)
    key_gain = qk_gain[1].astype(jnp.float32)
    inputs = tokens.astype(jnp.float32)
    scale_one = rms_scale(inputs)
    attn_full = attn_all.astype(jnp.float32)
    normed = (inputs * scale_one * attn_full).astype(jnp.bfloat16)
    query_raw = jnp.dot(normed, query_all, preferred_element_type=jnp.float32)
    key_raw = jnp.dot(normed, key_all, preferred_element_type=jnp.float32)
    value_raw = jnp.dot(normed, value_all, preferred_element_type=jnp.float32)
    query_turned, query_scale = head_rope(query_raw, query_gain, cosine, sine)
    key_turned, key_scale = head_rope(key_raw, key_gain, cosine, sine)
    query_send = query_turned.astype(jnp.bfloat16)
    key_send = key_turned.astype(jnp.bfloat16)
    value_send = value_raw.astype(jnp.bfloat16)
    mixed_heads, log_sums, query_heads, key_heads, value_heads = attend(
        (
            lax.all_to_all(query_send, "seq", split_axis=2, concat_axis=1, tiled=True),
            lax.all_to_all(key_send, "seq", split_axis=2, concat_axis=1, tiled=True),
            lax.all_to_all(value_send, "seq", split_axis=2, concat_axis=1, tiled=True),
        )
    )
    mixed = lax.all_to_all(mixed_heads, "seq", split_axis=1, concat_axis=2, tiled=True)
    middle = inputs + jnp.dot(mixed, out_all, preferred_element_type=jnp.float32)
    scale_two = rms_scale(middle)
    ffn_full = ffn_all.astype(jnp.float32)
    normed_two = (middle * scale_two * ffn_full).astype(jnp.bfloat16)
    gate = jnp.dot(normed_two, gate_all, preferred_element_type=jnp.float32)
    upward = jnp.dot(normed_two, up_all, preferred_element_type=jnp.float32)
    sigma = jax.nn.sigmoid(gate)
    activated = gate * sigma
    hidden = (activated * upward).astype(jnp.bfloat16)
    result = (middle + jnp.dot(hidden, down_all, preferred_element_type=jnp.float32)).astype(
        jnp.bfloat16
    )
    (
        query_back,
        key_back,
        value_back,
        out_back,
        gate_back,
        up_back,
        down_back,
        attn_back,
        ffn_back,
    ) = forward_weights
    grad_down = jnp.einsum("btf,btd->fd", hidden, cotangent, preferred_element_type=jnp.float32)
    grad_hidden = jnp.einsum(
        "btd,fd->btf", cotangent, down_back, preferred_element_type=jnp.float32
    )
    grad_gate_act = (grad_hidden * upward * sigma * (1.0 + gate * (1.0 - sigma))).astype(
        jnp.bfloat16
    )
    grad_upward = (grad_hidden * activated).astype(jnp.bfloat16)
    grad_gate = jnp.einsum(
        "btd,btf->df", normed_two, grad_gate_act, preferred_element_type=jnp.float32
    )
    grad_up = jnp.einsum("btd,btf->df", normed_two, grad_upward, preferred_element_type=jnp.float32)
    grad_normed_two = jnp.einsum(
        "btf,df->btd", grad_gate_act, gate_back, preferred_element_type=jnp.float32
    ) + jnp.einsum("btf,df->btd", grad_upward, up_back, preferred_element_type=jnp.float32)
    grad_middle_norm, grad_ffn_gain = norm_back(
        grad_normed_two, middle, scale_two, ffn_back.astype(jnp.float32)
    )
    grad_middle = cotangent.astype(jnp.float32) + grad_middle_norm
    grad_branch = grad_middle.astype(jnp.bfloat16)
    grad_out = jnp.einsum("btc,btd->cd", mixed, grad_branch, preferred_element_type=jnp.float32)
    grad_mixed = jnp.einsum(
        "btd,cd->btc", grad_branch, out_back, preferred_element_type=jnp.float32
    ).astype(jnp.bfloat16)
    grad_mixed_heads = lax.all_to_all(grad_mixed, "seq", split_axis=2, concat_axis=1, tiled=True)
    grad_query_heads, grad_key_heads, grad_value_heads = attend_back(
        query_heads, key_heads, value_heads, log_sums, grad_mixed_heads
    )
    grad_query_tok, grad_key_tok, grad_value_tok = (
        lax.all_to_all(grad_query_heads, "seq", split_axis=1, concat_axis=2, tiled=True),
        lax.all_to_all(grad_key_heads, "seq", split_axis=1, concat_axis=2, tiled=True),
        lax.all_to_all(grad_value_heads, "seq", split_axis=1, concat_axis=2, tiled=True),
    )
    grad_query_raw, grad_query_gain = head_rope_back(
        grad_query_tok.astype(jnp.float32), query_raw, query_scale, query_gain, cosine, sine
    )
    grad_key_raw, grad_key_gain = head_rope_back(
        grad_key_tok.astype(jnp.float32), key_raw, key_scale, key_gain, cosine, sine
    )
    grad_query_low = grad_query_raw.astype(jnp.bfloat16)
    grad_key_low = grad_key_raw.astype(jnp.bfloat16)
    grad_query = jnp.einsum(
        "btd,btc->dc", normed, grad_query_low, preferred_element_type=jnp.float32
    )
    grad_key = jnp.einsum("btd,btc->dc", normed, grad_key_low, preferred_element_type=jnp.float32)
    grad_value = jnp.einsum(
        "btd,btc->dc", normed, grad_value_tok, preferred_element_type=jnp.float32
    )
    grad_normed = (
        jnp.einsum("btc,dc->btd", grad_query_low, query_back, preferred_element_type=jnp.float32)
        + jnp.einsum("btc,dc->btd", grad_key_low, key_back, preferred_element_type=jnp.float32)
        + jnp.einsum("btc,dc->btd", grad_value_tok, value_back, preferred_element_type=jnp.float32)
    )
    grad_inputs_norm, grad_attn_gain = norm_back(
        grad_normed, inputs, scale_one, attn_back.astype(jnp.float32)
    )
    grad_tokens = grad_middle + grad_inputs_norm
    gain_total = lax.psum(jnp.stack([grad_query_gain, grad_key_gain]), ("fsdp", "seq"))
    owned = (
        lax.psum_scatter(
            grad_query.astype(jnp.bfloat16), "fsdp", scatter_dimension=0, tiled=True
        ).astype(jnp.float32),
        lax.psum_scatter(
            grad_key.astype(jnp.bfloat16), "fsdp", scatter_dimension=0, tiled=True
        ).astype(jnp.float32),
        lax.psum_scatter(
            grad_value.astype(jnp.bfloat16), "fsdp", scatter_dimension=0, tiled=True
        ).astype(jnp.float32),
        lax.psum_scatter(
            grad_out.astype(jnp.bfloat16), "fsdp", scatter_dimension=0, tiled=True
        ).astype(jnp.float32),
        lax.psum_scatter(
            grad_gate.astype(jnp.bfloat16), "fsdp", scatter_dimension=0, tiled=True
        ).astype(jnp.float32),
        lax.psum_scatter(
            grad_up.astype(jnp.bfloat16), "fsdp", scatter_dimension=0, tiled=True
        ).astype(jnp.float32),
        lax.psum_scatter(
            grad_down.astype(jnp.bfloat16), "fsdp", scatter_dimension=0, tiled=True
        ).astype(jnp.float32),
        lax.psum_scatter(
            grad_attn_gain.astype(jnp.bfloat16), "fsdp", scatter_dimension=0, tiled=True
        ).astype(jnp.float32),
        lax.psum_scatter(
            grad_ffn_gain.astype(jnp.bfloat16), "fsdp", scatter_dimension=0, tiled=True
        ).astype(jnp.float32),
    )
    (
        owned_query,
        owned_key,
        owned_value,
        owned_out,
        owned_gate,
        owned_up,
        owned_down,
        owned_attn,
        owned_ffn,
    ) = owned
    shards = (
        lax.psum(owned_query.astype(jnp.bfloat16), "seq").astype(jnp.float32),
        lax.psum(owned_key.astype(jnp.bfloat16), "seq").astype(jnp.float32),
        lax.psum(owned_value.astype(jnp.bfloat16), "seq").astype(jnp.float32),
        lax.psum(owned_out.astype(jnp.bfloat16), "seq").astype(jnp.float32),
        lax.psum(owned_gate.astype(jnp.bfloat16), "seq").astype(jnp.float32),
        lax.psum(owned_up.astype(jnp.bfloat16), "seq").astype(jnp.float32),
        lax.psum(owned_down.astype(jnp.bfloat16), "seq").astype(jnp.float32),
        lax.psum(owned_attn.astype(jnp.bfloat16), "seq").astype(jnp.float32),
        lax.psum(owned_ffn.astype(jnp.bfloat16), "seq").astype(jnp.float32),
    )
    (
        shard_query,
        shard_key,
        shard_value,
        shard_out,
        shard_gate,
        shard_up,
        shard_down,
        shard_attn,
        shard_ffn,
    ) = shards
    return (
        result,
        grad_tokens,
        shard_query,
        shard_key,
        shard_value,
        shard_out,
        shard_gate,
        shard_up,
        shard_down,
        shard_attn,
        shard_ffn,
        gain_total,
    )


def solution(mesh):
    placed = (
        P("fsdp", "seq", None),
        P("fsdp", None),
        P("fsdp", None),
        P("fsdp", None),
        P("fsdp", None),
        P("fsdp", None),
        P("fsdp", None),
        P("fsdp", None),
        P("fsdp"),
        P("fsdp"),
        P(),
        P("fsdp", "seq", None),
    )
    return jax.shard_map(
        per_device,
        mesh=mesh,
        in_specs=placed,
        out_specs=(
            P("fsdp", "seq", None),
            P("fsdp", "seq", None),
            P("fsdp", None),
            P("fsdp", None),
            P("fsdp", None),
            P("fsdp", None),
            P("fsdp", None),
            P("fsdp", None),
            P("fsdp", None),
            P("fsdp"),
            P("fsdp"),
            P(),
        ),
        check_vma=False,
    )
```

profile of v0, /device:TPU:0, one launch (start us, length us, event | category | flops | bytes accessed | tf_op | source)
XLA Modules:
  0.0 1667.1 jit_solution(14253296848511540375)
XLA Ops:
  12.0 22.3 %all-gather = bf16[8,1,128]{2,1,0:T(2,128)(2,1)S(1)} all-gather(bf16[1,1,128]{2,1,0:T(2,128)(2,1)S(1)} %bitcast.423), channel_id=1, replica_groups=mesh['fsdp'=8,'seq'=4] {'fsdp'}, dimensions={0}, use_global_device_ids=true | all-gather | bytes 2304 | tf_op jit(solution)/shard_map/all_gather | solution.py:193
  39.5 13.6 all-gather.12.cloned.1.call-done
  66.1 4.2 all-to-all-start.1
  70.2 24.0 %all-gather.14.cloned.1.call-done = bf16[1024,512]{1,0:T(8,128)(2,1)} async-done(((bf16[128,512]{1,0:T(8,128)(2,1)}), bf16[1024,512]{1,0:T(8,128)(2,1)}) %all-gather.14.cloned.1.call-update) | async-done | bytes 1048592 | tf_op jit(solution)/shard_map/all_gather | solution.py:188
  97.4 46.9 %all-gather.10.cloned.1.call-done = bf16[1024,1024]{1,0:T(8,128)(2,1)} async-done(((bf16[128,1024]{1,0:T(8,128)(2,1)}), bf16[1024,1024]{1,0:T(8,128)(2,1)}) %all-gather.10.cloned.1.call-update) | async-done | bytes 2097168 | tf_op jit(solution)/shard_map/all_gather | solution.py:186
  144.3 4.2 fusion.82
  158.7 4.1 all-to-all-start.2
  162.9 4.5 add_convert_fusion.1
  167.4 3.7 copy.184
  171.7 4.0 all-to-all-start
  179.4 10.7 all-to-all-done
  192.9 30.1 %while.27 = (s32[]{:T(128)}, bf16[2,2,512,2,2,64]{2,5,4,3,1,0:T(8,128)(2,1)S(1)}, f32[2,2,2,2,512]{4,3,2,1,0:T(2,128)S(1)}, s32[2]{0:T(128)S(1)}, bf16[2,2,512,2...) while((s32[]{:T(128)}, ...), condition=%wide.region_6.7_spmd, body=%wide.region_3.6_spmd.sunk | while | flops 1124856320 | bytes 54661240 | solution.py:113
  194.5 4.0 bitcast_reduce_fusion.2
  198.5 4.3 fusion.155
  202.8 5.1 fusion.156
  209.6 3.9 bitcast_reduce_fusion.2
  213.5 4.3 fusion.155
  217.9 5.1 fusion.156
  224.0 4.6 copy.246
  230.7 3.5 all-to-all-start.3
  234.2 18.9 %all-gather.1 = bf16[8,1,128]{2,1,0:T(2,128)(2,1)S(1)} all-gather(bf16[1,1,128]{2,1,0:T(2,128)(2,1)S(1)} %bitcast.424), channel_id=1, replica_groups=mesh['fsdp'=8,'seq'=4] {'fsdp'}, dimensions={0}, use_global_device_ids=true | all-gather | bytes 2304 | tf_op jit(solution)/shard_map/all_gather | solution.py:194
  258.8 72.9 %all-gather.22.cloned.1.call-done = bf16[4608,1024]{1,0:T(8,128)(2,1)} async-done(((bf16[576,1024]{1,0:T(8,128)(2,1)}), bf16[4608,1024]{1,0:T(8,128)(2,1)}) %all-gather.22.cloned.1.call-update) | async-done | bytes 9437200 | tf_op jit(solution)/shard_map/all_gather | solution.py:192
  331.8 11.2 fusion.54
  342.9 126.3 %all-gather.20.cloned.1.call-done = bf16[1024,4608]{1,0:T(8,128)(2,1)} async-done(((bf16[128,4608]{1,0:T(8,128)(2,1)}), bf16[1024,4608]{1,0:T(8,128)(2,1)}) %all-gather.20.cloned.1.call-update) | async-done | bytes 9437200 | tf_op jit(solution)/shard_map/all_gather | solution.py:191
  469.2 11.0 fusion.60
  480.3 126.6 %all-gather.18.cloned.1.call-done = bf16[1024,4608]{1,0:T(8,128)(2,1)} async-done(((bf16[128,4608]{1,0:T(8,128)(2,1)}), bf16[1024,4608]{1,0:T(8,128)(2,1)}) %all-gather.18.cloned.1.call-update) | async-done | bytes 9437200 | tf_op jit(solution)/shard_map/all_gather | solution.py:190
  606.9 17.8 %multiply_convert_fusion.1 = (bf16[2,256,4608]{2,1,0:T(8,128)(2,1)}, bf16[2,256,4608]{2,1,0:T(8,128)(2,1)}, bf16[2,256,4608]{2,1,0:T(8,128)(2,1)}) fusion(f32[2,256,4608]{2,1,0:T(8,128)} %fusion.54, f32[2,256,4608]{2,1,0:T(8,128)} %fusion.60, bf16[2,256,1024]{2,1,0:T(8,128)(2,1)S(1)} %multiply_convert_fusion.3, ...), kind=kOutput, calls=%fused_computation.80 | convolution fusion | flops 4867227648 | bytes 43515904 | tf_op jit(solution)/shard_map/dot_general | solution.py:228
  624.7 9.4 fusion.58
  634.5 5.8 multiply_reduce_fusion.1
  644.2 3.6 copy.200
  647.8 3.5 all-to-all-start.4
  651.4 14.4 all-to-all-done.4
  669.5 96.2 %while.28 = (s32[]{:T(128)}, f32[2,1024,2,64]{1,3,2,0:T(8,128)}, f32[2,1024,2,64]{1,3,2,0:T(8,128)}, bf16[2,2,512,2,2,64]{2,5,4,3,1,0:T(8,128)(2,1)}, bf16[2,2,5...) while((s32[]{:T(128)}, f32[2,1024,2,64]{1,3,2,0:T(8,128)}, ...), condition=%wide.region_11.12_spmd.clone, body=%wide.region_9.11_spmd.clone.sunk | while | flops 2749624832 | bytes 254202448 | solution.py:162
  670.7 3.4 fusion.165
  676.8 11.9 fusion.166
  688.7 11.1 fusion.167
  699.8 6.2 fusion.168
  706.1 7.9 fusion.169
  724.6 11.9 fusion.166
  736.5 11.1 fusion.167
  747.6 6.5 fusion.168
  754.1 7.9 fusion.169
  768.2 3.5 all-to-all-start.6
  773.3 7.2 all-to-all-done.6
  793.2 11.2 all_to_all.114
  807.2 3.8 bitcast_convert_fusion.3
  816.0 3.5 all-to-all-start.5
  821.9 12.1 all-to-all-done.5
  851.4 5.9 multiply_reduce_fusion
  862.3 10.0 bitcast_convert_fusion.2
  872.3 9.8 bitcast_convert_fusion.1
  883.4 9.9 bitcast_convert_fusion
  895.2 25.7 %reduce-scatter.12.cloned.1.call-done = bf16[128,512]{1,0:T(8,128)(2,1)} async-done(((bf16[1024,512]{1,0:T(8,128)(2,1)}), bf16[128,512]{1,0:T(8,128)(2,1)}) %reduce-scatter.12.cloned.1.call-update) | async-done | bytes 131088 | tf_op jit(solution)/shard_map/reduce_scatter | solution.py:312
  920.9 70.8 %reduce-scatter.14.cloned.1.call-done = bf16[128,1024]{1,0:T(8,128)(2,1)} async-done(((bf16[1024,1024]{1,0:T(8,128)(2,1)}), bf16[128,1024]{1,0:T(8,128)(2,1)}) %reduce-scatter.14.cloned.1.call-update) | async-done | bytes 262160 | tf_op jit(solution)/shard_map/reduce_scatter | solution.py:315
  991.7 71.5 %reduce-scatter.8.cloned.1.call-done = bf16[128,1024]{1,0:T(8,128)(2,1)} async-done(((bf16[1024,1024]{1,0:T(8,128)(2,1)}), bf16[128,1024]{1,0:T(8,128)(2,1)}) %reduce-scatter.8.cloned.1.call-update) | async-done | bytes 262160 | tf_op jit(solution)/shard_map/reduce_scatter | solution.py:306
  1063.3 164.7 %reduce-scatter.16.cloned.1.call-done = bf16[128,4608]{1,0:T(8,128)(2,1)} async-done(((bf16[1024,4608]{1,0:T(8,128)(2,1)}), bf16[128,4608]{1,0:T(8,128)(2,1)}) %reduce-scatter.16.cloned.1.call-update) | async-done | bytes 1179664 | tf_op jit(solution)/shard_map/reduce_scatter | solution.py:318
  1227.9 164.8 %reduce-scatter.18.cloned.1.call-done = bf16[128,4608]{1,0:T(8,128)(2,1)} async-done(((bf16[1024,4608]{1,0:T(8,128)(2,1)}), bf16[128,4608]{1,0:T(8,128)(2,1)}) %reduce-scatter.18.cloned.1.call-update) | async-done | bytes 1179664 | tf_op jit(solution)/shard_map/reduce_scatter | solution.py:321
  1392.8 164.7 %reduce-scatter.20.cloned.1.call-done = bf16[576,1024]{1,0:T(8,128)(2,1)} async-done(((bf16[4608,1024]{1,0:T(8,128)(2,1)}), bf16[576,1024]{1,0:T(8,128)(2,1)}) %reduce-scatter.20.cloned.1.call-update) | async-done | bytes 1179664 | tf_op jit(solution)/shard_map/reduce_scatter | solution.py:324
  1559.1 9.8 add_convert_fusion
  1575.3 19.4 %all-reduce.2 = (bf16[1024]{0:T(1024)(128)(2,1)S(1)}, bf16[1024]{0:T(1024)(128)(2,1)S(1)}) all-reduce(bf16[1024]{0:T(1024)(128)(2,1)S(1)} %get-tuple-element.212, bf16[1024]{0:T(1024)(128)(2,1)S(1)} %copy-done.74), channel_id=9, replica_groups=mesh['fsdp'=8,'seq'=4] {'fsdp'}, use_global_device_ids=true, to_apply=%region_30.31.clone | all-reduce | flops 2048 | bytes 8192
  1594.9 6.4 all-reduce.3
  1602.5 37.7 %psum.79 = f32[2,64]{1,0:T(2,128)} all-reduce(f32[2,64]{1,0:T(2,128)S(1)} %pad_maximum_fusion.5), channel_id=1, replica_groups=mesh['fsdp'=8,'seq'=4] {'fsdp','seq'}, use_global_device_ids=true, to_apply=%region_39.40 | all-reduce | flops 128 | bytes 1024 | tf_op jit(solution)/shard_map/psum | solution.py:304
  1640.2 3.5 fusion.72
  1643.7 4.4 all-reduce.7.cloned.1.call-done
  (378 shorter events, 153.4 us)
Async XLA Ops:
  7.2 46.0 %all-gather.12.cloned.1.call-start = ((), (), s32[]{:S(2)}) async-start(), calls=%async_computation.16 | async-start | bytes 1179648 | tf_op jit(solution)/shard_map/all_gather | solution.py:187
  7.9 4.1 copy-start.76
  7.9 26.3 %copy-start.16 = (bf16[2,256,1024]{2,1,0:T(8,128)(2,1)S(1)}, bf16[2,256,1024]{2,1,0:T(8,128)(2,1)}, u32[]{:S(2)}) copy-start(bf16[2,256,1024]{2,1,0:T(8,128)(2,1)} %param.16) | copy-start | bytes 3145732
  7.9 86.3 %all-gather.14.cloned.1.call-start = ((), (), s32[]{:S(2)}) async-start(), calls=%async_computation.17 | async-start | bytes 1179648 | tf_op jit(solution)/shard_map/all_gather | solution.py:188
  8.7 135.6 %all-gather.10.cloned.1.call-start = ((), (), s32[]{:S(2)}) async-start(), calls=%async_computation.15 | async-start | bytes 2359296 | tf_op jit(solution)/shard_map/all_gather | solution.py:186
  9.4 243.9 %all-gather.16.cloned.1.call-start = ((), (), s32[]{:S(2)}) async-start(), calls=%async_computation.18 | async-start | bytes 2359296 | tf_op jit(solution)/shard_map/all_gather | solution.py:189
  10.0 321.7 %all-gather.22.cloned.1.call-start = ((), (), s32[]{:S(2)}) async-start(), calls=%async_computation.21 | async-start | bytes 10616832 | tf_op jit(solution)/shard_map/all_gather | solution.py:192
  10.6 458.6 %all-gather.20.cloned.1.call-start = ((), (), s32[]{:S(2)}) async-start(), calls=%async_computation.20 | async-start | bytes 10616832 | tf_op jit(solution)/shard_map/all_gather | solution.py:191
  11.2 595.7 %all-gather.18.cloned.1.call-start = ((), (), s32[]{:S(2)}) async-start(), calls=%async_computation.19 | async-start | bytes 10616832 | tf_op jit(solution)/shard_map/all_gather | solution.py:190
  12.0 44.4 %copy-start.72 = (f32[64]{0:T(128)}, f32[64]{0:T(128)S(1)}, u32[]{:S(2)}) copy-start(f32[64]{0:T(128)S(1)} %get-tuple-element.296) | copy-start | bytes 772
  12.0 139.6 %copy-start.70 = (f32[64]{0:T(128)}, f32[64]{0:T(128)S(1)}, u32[]{:S(2)}) copy-start(f32[64]{0:T(128)S(1)} %get-tuple-element.297) | copy-start | bytes 772
  34.3 110.0 %copy-start.61 = (f32[8,1,128]{2,1,0:T(1,128)}, f32[8,1,128]{2,1,0:T(1,128)S(1)}, u32[]{:S(2)}) copy-start(f32[8,1,128]{2,1,0:T(1,128)S(1)} %convert_element_type.299) | copy-start | bytes 12292
  35.2 109.1 %copy-start.67 = (f32[2,256]{1,0:T(2,128)}, f32[2,256]{1,0:T(2,128)S(1)}, u32[]{:S(2)}) copy-start(f32[2,256]{1,0:T(2,128)S(1)} %get-tuple-element.293) | copy-start | bytes 6148
  37.3 125.6 %copy-start.10 = (f32[256,1024]{1,0:T(8,128)}, f32[256,1024]{1,0:T(8,128)S(1)}, u32[]{:S(2)}) copy-start(f32[256,1024]{1,0:T(8,128)S(1)} %copy.181) | copy-start | bytes 3145732
  37.3 125.5 %copy-start.63 = (f32[1024]{0:T(1024)}, f32[1024]{0:T(1024)S(1)}, u32[]{:S(2)}) copy-start(f32[1024]{0:T(1024)S(1)} %mul.475) | copy-start | bytes 12292
  39.5 21.2 %copy-start.65 = (f32[512]{0:T(512)}, f32[512]{0:T(512)S(1)}, u32[]{:S(2)}) copy-start(f32[512]{0:T(512)S(1)} %mul.500) | copy-start | bytes 6148
  55.1 5.6 copy-start.12
  64.0 30.3 %copy-start.17 = (bf16[2,256,1024]{2,1,0:T(8,128)(2,1)S(1)}, bf16[2,256,1024]{2,1,0:T(8,128)(2,1)}, u32[]{:S(2)}) copy-start(bf16[2,256,1024]{2,1,0:T(8,128)(2,1)} %param.16) | copy-start | bytes 3145732
  66.1 92.6 %all-to-all-start.1 = ((bf16[2,256,512]{1,0,2:T(2,128)(2,1)}), bf16[2,256,512]{1,0,2:T(2,128)(2,1)}, u32[]{:S(2)}, u32[]{:S(2)}) async-start(bf16[2,256,512]{1,0,2:T(2,128)(2,1)} %copy.191), calls=%async_computation.1 | async-start | bytes 1048576 | tf_op jit(solution)/shard_map/all_to_all | solution.py:219
  155.7 7.2 copy-start.5
  158.7 13.0 all-to-all-start.2
  171.7 18.4 %all-to-all-start = ((bf16[2,256,1024]{1,0,2:T(2,128)(2,1)}), bf16[2,256,1024]{1,0,2:T(2,128)(2,1)S(1)}, u32[]{:S(2)}, u32[]{:S(2)}) async-start(bf16[2,256,1024]{1,0,2:T(2,128)(2,1)} %copy.184), calls=%async_computation | async-start | bytes 2097152 | tf_op jit(solution)/shard_map/all_to_all | solution.py:218
  228.5 5.6 copy-start.77
  230.7 22.4 %all-to-all-start.3 = ((bf16[2,1024,256]{2,0,1:T(2,128)(2,1)}), bf16[2,1024,256]{2,0,1:T(2,128)(2,1)S(1)}, u32[]{:S(2)}, u32[]{:S(2)}) async-start(bf16[2,1024,256]{2,0,1:T(2,128)(2,1)} %reshape.349), calls=%async_computation.3 | async-start | bytes 2097152 | tf_op jit(solution)/shard_map/all_to_all | solution.py:223
  257.2 74.5 %copy-start.45 = (bf16[2,256,1024]{2,1,0:T(8,128)(2,1)S(1)}, bf16[2,256,1024]{2,1,0:T(8,128)(2,1)}, u32[]{:S(2)}) copy-start(bf16[2,256,1024]{2,1,0:T(8,128)(2,1)} %param.27) | copy-start | bytes 3145732
  258.8 348.1 %copy-start.53 = (bf16[2,256,1024]{2,1,0:T(8,128)(2,1)}, bf16[2,256,1024]{2,1,0:T(8,128)(2,1)S(1)}, u32[]{:S(2)}) copy-start(bf16[2,256,1024]{2,1,0:T(8,128)(2,1)S(1)} %multiply_convert_fusion.3) | copy-start | bytes 3145732
  624.7 9.4 copy-start.26
  624.7 9.4 copy-start.78
  624.7 9.8 copy-start.82
  634.5 5.8 copy-start.46
  647.8 17.9 %all-to-all-start.4 = ((bf16[2,256,1024]{1,0,2:T(2,128)(2,1)}), bf16[2,256,1024]{1,0,2:T(2,128)(2,1)S(1)}, u32[]{:S(2)}, u32[]{:S(2)}) async-start(bf16[2,256,1024]{1,0,2:T(2,128)(2,1)} %copy.200), calls=%async_computation.4 | async-start | bytes 2097152 | tf_op jit(solution)/shard_map/all_to_all | solution.py:271
  669.9 4.2 copy-start.57
  674.1 14.6 copy-start
  699.8 6.3 copy-start.9
  699.8 6.3 copy-start.33
  699.8 6.3 copy-start.50
  699.8 14.2 slice-start
  706.0 8.0 slice-start.1
  706.1 8.0 copy-start.29
  717.7 4.2 copy-start.57
  721.9 14.6 copy-start
  747.6 6.5 copy-start.9
  747.6 6.5 copy-start.33
  747.6 6.5 copy-start.50
  747.6 14.5 slice-start
  754.1 8.0 slice-start.1
  754.1 8.0 copy-start.29
  765.7 6.1 copy-start.60
  768.2 12.3 all-to-all-start.6
  771.6 123.5 %reduce-scatter.10.cloned.1.call-start = ((), (), s32[]{:S(2)}) async-start(), calls=%async_computation.23 | async-start | bytes 1179648 | tf_op jit(solution)/shard_map/reduce_scatter | solution.py:309
  792.6 128.3 %reduce-scatter.12.cloned.1.call-start = ((), (), s32[]{:S(2)}) async-start(), calls=%async_computation.24 | async-start | bytes 1179648 | tf_op jit(solution)/shard_map/reduce_scatter | solution.py:312
  807.1 184.6 %reduce-scatter.14.cloned.1.call-start = ((), (), s32[]{:S(2)}) async-start(), calls=%async_computation.25 | async-start | bytes 2359296 | tf_op jit(solution)/shard_map/reduce_scatter | solution.py:315
  813.9 5.9 copy-start.59
  816.0 17.9 %all-to-all-start.5 = ((bf16[2,1024,256]{2,0,1:T(2,128)(2,1)}), bf16[2,1024,256]{2,0,1:T(2,128)(2,1)S(1)}, u32[]{:S(2)}, u32[]{:S(2)}) async-start(bf16[2,1024,256]{2,0,1:T(2,128)(2,1)} %reshape.350), calls=%async_computation.5 | async-start | bytes 2097152 | tf_op jit(solution)/shard_map/all_to_all | solution.py:276
  819.6 243.7 %reduce-scatter.8.cloned.1.call-start = ((), (), s32[]{:S(2)}) async-start(), calls=%async_computation.22 | async-start | bytes 2359296 | tf_op jit(solution)/shard_map/reduce_scatter | solution.py:306
  851.4 6.9 copy-start.20
  861.1 366.8 %reduce-scatter.16.cloned.1.call-start = ((), (), s32[]{:S(2)}) async-start(), calls=%async_computation.26 | async-start | bytes 10616832 | tf_op jit(solution)/shard_map/reduce_scatter | solution.py:318
  872.3 520.5 %reduce-scatter.18.cloned.1.call-start = ((), (), s32[]{:S(2)}) async-start(), calls=%async_computation.27 | async-start | bytes 10616832 | tf_op jit(solution)/shard_map/reduce_scatter | solution.py:321
  882.2 675.3 %reduce-scatter.20.cloned.1.call-start = ((), (), s32[]{:S(2)}) async-start(), calls=%async_computation.28 | async-start | bytes 10616832 | tf_op jit(solution)/shard_map/reduce_scatter | solution.py:324
  893.3 754.8 %all-reduce.7.cloned.1.call-start = ((), (), s32[]{:S(2)}) async-start(), calls=%async_computation.29 | async-start | bytes 8650752 | tf_op jit(solution)/shard_map/psum | solution.py:346
  1559.0 9.9 copy-start.35
  1572.9 67.3 %copy-start.24 = (f32[2,256,1024]{2,1,0:T(8,128)S(1)}, f32[2,256,1024]{2,1,0:T(8,128)}, u32[]{:S(2)}) copy-start(f32[2,256,1024]{2,1,0:T(8,128)} %copy-done.22) | copy-start | bytes 6291460
  1572.9 67.3 %copy-start.69 = (f32[2,256]{1,0:T(2,128)S(1)}, f32[2,256]{1,0:T(2,128)}, u32[]{:S(2)}) copy-start(f32[2,256]{1,0:T(2,128)} %get-tuple-element.292) | copy-start | bytes 6148
  1648.1 7.0 copy-start.44
  (56 other events, 115.8 us)
Sparse Core Ops, SparseCore 0:
  10.1 42.9 all-gather.11
  55.3 38.9 all-gather.13
  96.4 47.7 all-gather.9
  146.2 47.6 all-gather.15
  195.9 135.7 all-gather.21
  333.8 135.4 all-gather.19
  471.4 135.4 all-gather.17
  792.8 61.4 reduce-scatter.9
  857.7 63.1 reduce-scatter.11
  924.3 67.4 reduce-scatter.13
  995.9 67.3 reduce-scatter.7
  1066.7 161.1 reduce-scatter.15
  1231.5 161.1 reduce-scatter.17
  1396.2 161.1 reduce-scatter.19
  1560.2 87.8 all-reduce.6
where the time goes:
time: 1680 us; the launch traced here: 1670 us
  waiting for transfers between devices  1130 us (67%)
  matrix products  207 us (12%)
  blocking collectives  116 us (7%)
  local copies, waits for them, and re-layouts  92.3 us (5%)
  other arithmetic  81.1 us (5%)
  starting transfers between devices  27.5 us (2%)
    reduce_scatter x1, waiting for transfers between devices, per_device(): lax.psum_scatter(grad_up.astype(jnp.bfloat16), 'fsdp', scatter_dimension=...  165 us
    reduce_scatter x1, waiting for transfers between devices, per_device(): lax.psum_scatter(grad_down.astype(jnp.bfloat16), 'fsdp', scatter_dimensio...  165 us
    reduce_scatter x1, waiting for transfers between devices, per_device(): lax.psum_scatter(grad_gate.astype(jnp.bfloat16), 'fsdp', scatter_dimensio...  165 us
    all_gather x1, waiting for transfers between devices, per_device(): lax.all_gather(w_gate, 'fsdp', axis=0, tiled=True)  127 us
    all_gather x1, waiting for transfers between devices, per_device(): lax.all_gather(w_up, 'fsdp', axis=0, tiled=True)  126 us
    all_gather x1, waiting for transfers between devices, per_device(): lax.all_gather(w_down, 'fsdp', axis=0, tiled=True)  72.9 us
    reduce_scatter x1, waiting for transfers between devices, per_device(): lax.psum_scatter(grad_query.astype(jnp.bfloat16), 'fsdp', scatter_dimensi...  71.5 us
    reduce_scatter x1, waiting for transfers between devices, per_device(): lax.psum_scatter(grad_out.astype(jnp.bfloat16), 'fsdp', scatter_dimension...  70.8 us
  transfers between devices with their start and end apart: 22, of which 18 were waited for; matrix products, arithmetic and copies ran while one was open for 12% of the time, Pallas kernels for 0%

commit v1 on v0

v1 whole, which is shorter than its diff:
```python
import functools

import jax
import jax.numpy as jnp
from jax import lax
from jax.sharding import PartitionSpec as P

HD = 64


RMS_EPSILON = 1e-05
ROPE_THETA = 1000000.0
NEG_LARGE = -1e30


def rms_scale(values):
    return lax.rsqrt(jnp.mean(values * values, axis=-1, keepdims=True) + RMS_EPSILON)


def rope_tables(positions, head_size):
    half_size = head_size // 2
    freqs = ROPE_THETA ** (-(jnp.arange(half_size, dtype=jnp.float32) * 2.0) / head_size)
    angles = positions.astype(jnp.float32)[:, None] * freqs[None, :]
    angles = jnp.concatenate([angles, angles], axis=-1)
    return (jnp.cos(angles), jnp.sin(angles))


def rotate(values):
    half_size = values.shape[-1] // 2
    return jnp.concatenate([-values[..., half_size:], values[..., :half_size]], axis=-1)


def rotate_back(values):
    half_size = values.shape[-1] // 2
    return jnp.concatenate([values[..., half_size:], -values[..., :half_size]], axis=-1)


def head_rope(flat, gain, cosine, sine):
    shaped = flat.reshape(flat.shape[:-1] + (-1, HD))
    scale = rms_scale(shaped)
    normed = shaped * scale * gain
    turned = normed * cosine[:, None, :] + rotate(normed) * sine[:, None, :]
    return (turned.reshape(flat.shape), scale)


def head_rope_back(grad_flat, flat, scale, gain, cosine, sine):
    shaped = flat.reshape(flat.shape[:-1] + (-1, HD))
    grad_turned = grad_flat.reshape(shaped.shape)
    grad_normed = grad_turned * cosine[:, None, :] + rotate_back(grad_turned * sine[:, None, :])
    grad_gain = jnp.sum(grad_normed * shaped * scale, axis=(0, 1, 2))
    weighted = grad_normed * gain
    grad_shaped = scale * weighted - shaped * scale**3 * jnp.mean(
        weighted * shaped, axis=-1, keepdims=True
    )
    return (grad_shaped.reshape(flat.shape), grad_gain)


def norm_back(grad, values, scale, gain):
    weighted = grad * gain
    grad_values = scale * weighted - values * scale**3 * jnp.mean(
        weighted * values, axis=-1, keepdims=True
    )
    grad_gain = jnp.sum(grad * values * scale, axis=(0, 1))
    return (grad_values, grad_gain)


def to_blocks(flat, count, kv_heads):
    batch, length, width = flat.shape
    group = width // (kv_heads * HD)
    shaped = flat.reshape(batch, count, length // count, kv_heads, group, HD)
    return jnp.moveaxis(shaped, 1, 0)


def split_heads(query_flat, key_flat, value_flat):
    batch, length, width = query_flat.shape
    kv_heads = key_flat.shape[2] // HD
    block_rows = min(512, length)
    count = length // block_rows
    query_blocks = to_blocks(query_flat, count, kv_heads)
    key_heads = key_flat.reshape(batch, length, kv_heads, HD)
    value_heads = value_flat.reshape(batch, length, kv_heads, HD)
    starts = jnp.arange(count) * block_rows
    return (query_blocks, key_heads, value_heads, starts)


def block_scores(query_block, key_heads, start):
    block_rows = query_block.shape[1]
    scores = jnp.einsum(
        "bqkgd,bskd->bkgqs", query_block, key_heads, preferred_element_type=jnp.float32
    ) * HD ** (-0.5)
    rows = start + jnp.arange(block_rows)
    columns = jnp.arange(key_heads.shape[1])
    causal = rows[:, None] >= columns[None, :]
    return (scores, causal)


def attend(parts):
    query_flat, key_flat, value_flat = parts
    batch, length, width = query_flat.shape
    query_blocks, key_heads, value_heads, starts = split_heads(query_flat, key_flat, value_flat)

    def one_block(pieces):
        query_block, start = pieces
        scores, causal = block_scores(query_block, key_heads, start)
        scores = jnp.where(causal, scores, NEG_LARGE)
        row_max = jnp.max(scores, axis=-1, keepdims=True)
        exp_part = jnp.exp(scores - row_max)
        row_sum = jnp.sum(exp_part, axis=-1, keepdims=True)
        probs = (exp_part / row_sum).astype(jnp.bfloat16)
        mixed = jnp.einsum(
            "bkgqs,bskd->bqkgd", probs, value_heads, preferred_element_type=jnp.float32
        )
        return (mixed.astype(jnp.bfloat16), (row_max + jnp.log(row_sum))[..., 0])

    mixed, log_sums = lax.map(one_block, (query_blocks, starts))
    mixed = jnp.moveaxis(mixed, 0, 1).reshape(batch, length, width)
    kv_heads = log_sums.shape[2]
    group = log_sums.shape[3]
    log_sums = jnp.moveaxis(log_sums, 0, 3).reshape(batch, kv_heads, group, length)
    return (mixed, log_sums, query_flat, key_flat, value_flat)


def attend_back(query_flat, key_flat, value_flat, log_sums, grad_mixed):
    batch, length, width = query_flat.shape
    query_blocks, key_heads, value_heads, starts = split_heads(query_flat, key_flat, value_flat)
    count = starts.shape[0]
    kv_heads = key_heads.shape[2]
    grad_blocks = to_blocks(grad_mixed, count, kv_heads)
    sum_blocks = jnp.moveaxis(log_sums.reshape(log_sums.shape[:3] + (count, length // count)), 3, 0)
    head_scale = HD ** (-0.5)

    def one_block(carry, pieces):
        grad_keys, grad_values = carry
        query_block, grad_block, sums_block, start = pieces
        scores, causal = block_scores(query_block, key_heads, start)
        probs = jnp.where(causal, jnp.exp(scores - sums_block[..., None]), 0.0)
        grad_values = grad_values + jnp.einsum(
            "bkgqs,bqkgd->bskd",
            probs.astype(jnp.bfloat16),
            grad_block,
            preferred_element_type=jnp.float32,
        )
        grad_probs = jnp.einsum(
            "bqkgd,bskd->bkgqs", grad_block, value_heads, preferred_element_type=jnp.float32
        )
        inner = jnp.sum(probs * grad_probs, axis=-1, keepdims=True)
        grad_scores = (probs * (grad_probs - inner)).astype(jnp.bfloat16)
        grad_query = (
            jnp.einsum(
                "bkgqs,bskd->bqkgd", grad_scores, key_heads, preferred_element_type=jnp.float32
            )
            * head_scale
        )
        grad_keys = (
            grad_keys
            + jnp.einsum(
                "bkgqs,bqkgd->bskd", grad_scores, query_block, preferred_element_type=jnp.float32
            )
            * head_scale
        )
        return ((grad_keys, grad_values), grad_query.astype(jnp.bfloat16))

    zero_heads = jnp.zeros(key_heads.shape, jnp.float32)
    (grad_keys, grad_values), grad_query = lax.scan(
        one_block, (zero_heads, zero_heads), (query_blocks, grad_blocks, sum_blocks, starts)
    )
    grad_query = jnp.moveaxis(grad_query, 0, 1).reshape(batch, length, width)
    grad_keys = grad_keys.reshape(key_flat.shape).astype(jnp.bfloat16)
    grad_values = grad_values.reshape(value_flat.shape).astype(jnp.bfloat16)
    return (grad_query, grad_keys, grad_values)


def bits_of(count):
    return [1 << i for i in range(count.bit_length() - 1)]


def swap(values, bit, count):
    return lax.ppermute(values, "seq", [(i, i ^ bit) for i in range(count)])


def gather_blocks(block, count):
    blocks = {0: block}
    for bit in reversed(bits_of(count)):
        for at in list(blocks):
            blocks[at | bit] = swap(blocks[at], bit, count)
    return blocks


def scatter_blocks(blocks, count):
    blocks = dict(blocks)
    for bit in bits_of(count):
        kept = {}
        for at in blocks:
            if not at & bit:
                arrived = swap(blocks[at | bit].astype(jnp.bfloat16), bit, count)
                kept[at] = blocks[at].astype(jnp.float32) + arrived.astype(jnp.float32)
        blocks = kept
    return blocks[0]


def in_order(blocks, own, count):
    batch, rows, width = blocks[0].shape
    whole = jnp.zeros((batch, count * rows, width), blocks[0].dtype)
    for at in range(count):
        whole = lax.dynamic_update_slice(whole, blocks[at], (0, (own ^ at) * rows, 0))
    return whole


def from_order(whole, own, count):
    rows = whole.shape[1] // count
    return {
        at: lax.dynamic_slice_in_dim(whole, (own ^ at) * rows, rows, axis=1) for at in range(count)
    }


def dot(left, right):
    return jnp.dot(left, right, preferred_element_type=jnp.float32)


def dot_t(left, right):
    return lax.dot_general(
        left, right, (((1,), (1,)), ((), ())), preferred_element_type=jnp.float32
    )


def t_dot(left, right):
    return lax.dot_general(
        left, right, (((0,), (0,)), ((), ())), preferred_element_type=jnp.float32
    )


def per_device(
    fsdp,
    seq,
    tokens,
    w_query,
    w_key,
    w_value,
    w_out,
    w_gate,
    w_up,
    w_down,
    attn_gain,
    ffn_gain,
    qk_gain,
    cotangent,
):
    bf16 = jnp.bfloat16
    f32 = jnp.float32
    own = lax.axis_index("seq")
    batch, rows, width = tokens.shape
    length = rows * seq
    count = batch * length
    part = w_query.shape[0]
    q_width = w_query.shape[1] // seq
    kv_width = w_key.shape[1] // seq
    o_width = w_out.shape[1] // seq
    units = w_down.shape[0] // seq
    local = units * fsdp

    def columns(weight, size):
        return lax.dynamic_slice_in_dim(weight, own * size, size, axis=1)

    gains = jnp.stack([attn_gain, ffn_gain], axis=1)
    first = jnp.concatenate(
        [
            columns(w_query, q_width),
            columns(w_key, kv_width),
            columns(w_value, kv_width),
            columns(w_out, o_width),
            jnp.pad(gains, ((0, 0), (0, 126))),
        ],
        axis=1,
    )
    first_all = lax.all_gather(first, "fsdp", axis=0, tiled=True)
    qkv_width = q_width + 2 * kv_width
    w_qkv = first_all[:, :qkv_width]
    out_cols = first_all[:, qkv_width : qkv_width + o_width]
    attn_full = first_all[:, qkv_width + o_width].astype(f32)
    ffn_full = first_all[:, qkv_width + o_width + 1].astype(f32)

    def pick(weight):
        split = weight.reshape(part, fsdp, seq, units)
        return lax.dynamic_index_in_dim(split, own, axis=2, keepdims=False).reshape(part, local)

    down_own = lax.dynamic_slice_in_dim(w_down, own * units, units, axis=0)
    second = jnp.concatenate(
        [pick(w_gate), pick(w_up), down_own.reshape(part, local)], axis=1
    )
    second, _ = lax.optimization_barrier((second, first_all))
    second_all = lax.all_gather(second, "fsdp", axis=0, tiled=True)
    gate_w = second_all[:, :local]
    up_w = second_all[:, local : 2 * local]
    down_w = second_all[:, 2 * local :].reshape(fsdp, part, local).reshape(local, width)

    token_blocks = gather_blocks(tokens, seq)
    inputs_all = in_order(token_blocks, own, seq)
    cotangent_in, _ = lax.optimization_barrier((cotangent, inputs_all))
    cot_blocks = gather_blocks(cotangent_in, seq)
    cot_all = jnp.concatenate(
        [cot_blocks[at].reshape(batch * rows, width) for at in range(seq)], axis=0
    )
    out_w = lax.all_to_all(out_cols, "seq", split_axis=0, concat_axis=1, tiled=True)

    inputs_all32 = inputs_all.astype(f32)
    scale_all = rms_scale(inputs_all32)
    hat_all = inputs_all32 * scale_all
    normed = (hat_all * attn_full).astype(bf16)
    flat_normed = normed.reshape(count, width)
    qkv_raw = dot(flat_normed, w_qkv).reshape(batch, length, qkv_width)
    query_raw = qkv_raw[..., :q_width]
    key_raw = qkv_raw[..., q_width : q_width + kv_width]
    value_raw = qkv_raw[..., q_width + kv_width :]
    cosine, sine = rope_tables(jnp.arange(length, dtype=jnp.int32), HD)
    query_gain = qk_gain[0].astype(f32)
    key_gain = qk_gain[1].astype(f32)
    query_turned, query_scale = head_rope(query_raw, query_gain, cosine, sine)
    key_turned, key_scale = head_rope(key_raw, key_gain, cosine, sine)
    mixed, log_sums, query_low, key_low, value_low = attend(
        (query_turned.astype(bf16), key_turned.astype(bf16), value_raw.astype(bf16))
    )
    flat_mixed = mixed.reshape(count, q_width)
    branch = dot(flat_mixed, out_w).astype(bf16).reshape(batch, length, width)
    inputs = tokens.astype(f32)
    middle = inputs + scatter_blocks(from_order(branch, own, seq), seq)

    scale_two = rms_scale(middle)
    normed_two = (middle * scale_two * ffn_full).astype(bf16)
    two_blocks = gather_blocks(normed_two, seq)
    two_all = jnp.concatenate(
        [two_blocks[at].reshape(batch * rows, width) for at in range(seq)], axis=0
    )
    gate = dot(two_all, gate_w)
    upward = dot(two_all, up_w)
    grad_hidden = dot_t(cot_all, down_w)
    sigma = jax.nn.sigmoid(gate)
    activated = gate * sigma
    hidden = (activated * upward).astype(bf16)
    grad_gate_act = (grad_hidden * upward * sigma * (1.0 + gate * (1.0 - sigma))).astype(bf16)
    grad_upward = (grad_hidden * activated).astype(bf16)
    two_back = (dot_t(grad_gate_act, gate_w) + dot_t(grad_upward, up_w)).astype(bf16)

    def xor_blocks(flat):
        shaped = flat.reshape(seq, batch, rows, width)
        return {at: shaped[at] for at in range(seq)}

    grad_two = scatter_blocks(xor_blocks(two_back), seq)
    grad_middle_norm, grad_ffn_gain = norm_back(grad_two, middle, scale_two, ffn_full)
    grad_middle = cotangent.astype(f32) + grad_middle_norm
    grad_branch = grad_middle.astype(bf16)
    branch_blocks = gather_blocks(grad_branch, seq)
    grad_down = t_dot(hidden, cot_all).astype(bf16)
    grad_gate = t_dot(two_all, grad_gate_act).astype(bf16)
    grad_up = t_dot(two_all, grad_upward).astype(bf16)
    ffn_sums = jnp.concatenate(
        [grad_gate, grad_up, grad_down.reshape(fsdp, units, width).reshape(width, local)], axis=1
    )
    ffn_share = lax.psum_scatter(ffn_sums, "fsdp", scatter_dimension=0, tiled=True)
    result_part = dot(hidden, down_w).astype(bf16)
    result_part, _ = lax.optimization_barrier((result_part, tuple(branch_blocks.values())))
    result = (middle + scatter_blocks(xor_blocks(result_part), seq)).astype(bf16)

    branch_all = in_order(branch_blocks, own, seq).reshape(count, width)
    grad_out = t_dot(flat_mixed, branch_all).astype(bf16)
    grad_out_cols = lax.all_to_all(grad_out, "seq", split_axis=1, concat_axis=0, tiled=True)
    grad_mixed = dot_t(branch_all, out_w).astype(bf16).reshape(batch, length, q_width)
    grad_query_low, grad_key_low, grad_value_low = attend_back(
        query_low, key_low, value_low, log_sums, grad_mixed
    )
    grad_query_raw, grad_query_gain = head_rope_back(
        grad_query_low.astype(f32), query_raw, query_scale, query_gain, cosine, sine
    )
    grad_key_raw, grad_key_gain = head_rope_back(
        grad_key_low.astype(f32), key_raw, key_scale, key_gain, cosine, sine
    )
    grad_qkv = jnp.concatenate(
        [grad_query_raw.astype(bf16), grad_key_raw.astype(bf16), grad_value_low], axis=2
    ).reshape(count, qkv_width)
    normed_back = dot_t(grad_qkv, w_qkv)
    normed_back_low = normed_back.astype(bf16).reshape(batch, length, width)
    grad_attn_gain = jnp.sum(normed_back * hat_all.reshape(count, width), axis=0)
    grad_normed = scatter_blocks(from_order(normed_back_low, own, seq), seq)
    inputs_norm, _ = norm_back(grad_normed, inputs, rms_scale(inputs), attn_full)
    grad_tokens = grad_middle + inputs_norm

    gain_cols = jnp.stack([grad_attn_gain, jnp.sum(grad_ffn_gain.reshape(1, width), axis=0)], axis=1)
    last = jnp.concatenate(
        [
            t_dot(flat_normed, grad_qkv).astype(bf16),
            grad_out_cols,
            jnp.pad(gain_cols.astype(bf16), ((0, 0), (0, 126))),
        ],
        axis=1,
    )
    last_width = last.shape[1]
    qk_row = jnp.concatenate([grad_query_gain, grad_key_gain]).astype(bf16)
    qk_rows = jnp.zeros((fsdp, 16, last_width), bf16)
    qk_rows = qk_rows.at[:, 0, : 2 * HD].set(qk_row)
    last = jnp.concatenate([last.reshape(fsdp, part, last_width), qk_rows], axis=1)
    last_share = lax.psum_scatter(
        last.reshape(fsdp * (part + 16), last_width), "fsdp", scatter_dimension=0, tiled=True
    )
    ffn_shares = lax.all_gather(ffn_share, "seq", axis=0, tiled=False).astype(f32)
    last_shares = lax.all_gather(last_share, "seq", axis=0, tiled=False).astype(f32)

    def unpick(piece):
        split = piece.reshape(seq, part, fsdp, units)
        return jnp.transpose(split, (1, 2, 0, 3)).reshape(part, fsdp * seq * units)

    def side_by_side(piece):
        return jnp.transpose(piece, (1, 0, 2)).reshape(part, -1)

    shard_gate = unpick(ffn_shares[:, :, :local])
    shard_up = unpick(ffn_shares[:, :, local : 2 * local])
    shard_down = ffn_shares[:, :, 2 * local :].reshape(seq * units, width)
    top = last_shares[:, :part]
    shard_query = side_by_side(top[:, :, :q_width])
    shard_key = side_by_side(top[:, :, q_width : q_width + kv_width])
    shard_value = side_by_side(top[:, :, q_width + kv_width : qkv_width])
    shard_out = side_by_side(top[:, :, qkv_width : qkv_width + o_width])
    shard_gains = jnp.sum(top[:, :, qkv_width + o_width : qkv_width + o_width + 2], axis=0)
    gain_total = jnp.sum(last_shares[:, part, : 2 * HD], axis=0).reshape(2, HD)
    return (
        result,
        grad_tokens,
        shard_query,
        shard_key,
        shard_value,
        shard_out,
        shard_gate,
        shard_up,
        shard_down,
        shard_gains[:, 0],
        shard_gains[:, 1],
        gain_total,
    )


def solution(mesh):
    placed = (
        P("fsdp", "seq", None),
        P("fsdp", None),
        P("fsdp", None),
        P("fsdp", None),
        P("fsdp", None),
        P("fsdp", None),
        P("fsdp", None),
        P("fsdp", None),
        P("fsdp"),
        P("fsdp"),
        P(),
        P("fsdp", "seq", None),
    )
    return jax.shard_map(
        functools.partial(per_device, mesh.shape["fsdp"], mesh.shape["seq"]),
        mesh=mesh,
        in_specs=placed,
        out_specs=(
            P("fsdp", "seq", None),
            P("fsdp", "seq", None),
            P("fsdp", None),
            P("fsdp", None),
            P("fsdp", None),
            P("fsdp", None),
            P("fsdp", None),
            P("fsdp", None),
            P("fsdp", None),
            P("fsdp"),
            P("fsdp"),
            P(),
        ),
        check_vma=False,
    )
```

time: 1680 us -> 677 us (0.40)
  waiting for transfers between devices: 1130 us -> 182 us
  blocking collectives: 116 us -> 10.4 us
  local copies, waits for them, and re-layouts: 92.3 us -> 127 us
  other arithmetic: 81.1 us -> 105 us
    reduce_scatter x7 -> x2, waiting for transfers between devices: 662 us -> 0.01 us  [the longest x1 0.01 us: per_device(): lax.psum_scatter(ffn_sums, 'fsdp', scatter_dimension=0, tiled=True)]
    all_gather x7 -> x3, waiting for transfers between devices: 410 us -> 15.9 us  [the longest x1 12.4 us: per_device(): lax.all_gather(ffn_share, 'seq', axis=0, tiled=False).astype(f32)]
    ppermute x0 -> x24, waiting for transfers between devices: none -> 165 us  [swap(): return lax.ppermute(values, 'seq', [(i, i ^ bit) for i in range(count)])]
    all_to_all x7 -> x2, waiting for transfers between devices: 45 us -> 0.01 us  [the longest x1 0.01 us: per_device(): lax.all_to_all(out_cols, 'seq', split_axis=0, concat_axis=1, tiled=True)]
    psum x2 -> x0, blocking collectives: 44.1 us -> none  [the longest x1 37.7 us: per_device(): lax.psum(jnp.stack([grad_query_gain, grad_key_gain]), ('fsdp', 'seq'))]
    all_gather x2 -> x1, blocking collectives: 41.1 us -> 10.4 us  [per_device(): lax.all_gather(last_share, 'seq', axis=0, tiled=False).astype(f32)]
    unnamed x1 -> x0, blocking collectives: 19.4 us -> none
    all_to_all x7 -> x2, starting transfers between devices: 26.3 us -> 8.27 us  [the longest x1 4.14 us: per_device(): lax.all_to_all(grad_out, 'seq', split_axis=1, concat_axis=0, tiled=True)]
  transfers between devices with their start and end apart: 22 -> 31, of which waited for: 18 -> 11; matrix products, arithmetic and copies ran while one was open for 12% -> 52% of each run, Pallas kernels for 0% -> 0%
where the time goes in v1:
time: 677 us; the launch traced here: 669 us
  matrix products  204 us (30%)
  waiting for transfers between devices  182 us (27%)
  local copies, waits for them, and re-layouts  127 us (19%)
  other arithmetic  105 us (16%)
  starting transfers between devices  23.5 us (3%)
  between operations  15.3 us (2%)
  blocking collectives  10.4 us (2%)
    ppermute x24, waiting for transfers between devices, swap(): return lax.ppermute(values, 'seq', [(i, i ^ bit) for i in range(count)])  165 us
    dot_general x5, matrix products, dot_t(): lax.dot_general(left, right, (((1,), (1,)), ((), ())), preferred_element_...  46.5 us
    dot_general x5, matrix products, dot(): return jnp.dot(left, right, preferred_element_type=jnp.float32)  42.3 us
    dot_general x5, matrix products, t_dot(): lax.dot_general(left, right, (((0,), (0,)), ((), ())), preferred_element_...  35.4 us
    unnamed x152, local copies, waits for them, and re-layouts  24.7 us
    convert_element_type x2, other arithmetic, one_block(): grad_scores = (probs * (grad_probs - inner)).astype(jnp.bfloat16)  22.7 us
    dot_general x2, matrix products, one_block(): jnp.einsum('bqkgd,bskd->bkgqs', grad_block, value_heads, preferred_elemen...  22.5 us
    dynamic_update_slice x7, local copies, waits for them, and re-layouts, in_order(): lax.dynamic_update_slice(whole, blocks[at], (0, (own ^ at) * rows, 0))  15 us
  transfers between devices with their start and end apart: 31, of which 11 were waited for; matrix products, arithmetic and copies ran while one was open for 52% of the time, Pallas kernels for 0%

profile of v1, /device:TPU:0, one launch (start us, length us, event | category | flops | bytes accessed | tf_op | source)
XLA Modules:
  0.0 668.5 jit_solution(14584761970422402301)
XLA Ops:
  11.0 3.1 collective-permute-start.1
  16.0 21.5 %collective-permute-done.1 = bf16[2,256,1024]{2,1,0:T(8,128)(2,1)} collective-permute-done((bf16[2,256,1024]{2,1,0:T(8,128)(2,1)}, bf16[2,256,1024]{2,1,0:T(8,128)(2,1)}, u32[]{:S(2)}, u32[]{:S(2)}) %collective-permute-start.1) | collective-permute-done | bytes 1048608 | tf_op jit(solution)/shard_map/ppermute | solution.py:178
  54.9 3.1 fusion.55
  58.1 3.5 all-gather.6.cloned.1.call-done
  63.0 6.9 %fusion.96 = f32[2,1024,512]{1,2,0:T(8,128)} fusion(f32[1024]{0:T(1024)S(1)} %bitcast.435, bf16[2,1024,1024]{2,1,0:T(8,128)(2,1)} %constant_dynamic-update-slice_fusion.8, f32[2,1024]{1,0:T(2,128)S(1)} %add_rsqrt_fusion.2, bf16[1024,896]{0,1:T(8,128)(2,1)} %all-gather.6.cloned.1.call-done), kind=kOutput, calls=%fused_computation.153 | convolution fusion | flops 2155872256 | bytes 9449472 | tf_op jit(solution)/shard_map/dot_general | solution.py:217
  75.4 4.1 all-to-all-start
  95.7 29.2 %while.28 = (s32[]{:T(128)}, bf16[2,2,512,2,2,64]{2,5,4,3,1,0:T(8,128)(2,1)S(1)}, f32[2,2,2,2,512]{4,3,2,1,0:T(2,128)}, s32[2]{0:T(128)S(1)}, bf16[2,2,512,2,2,6...) while((s32[]{:T(128)}, ...), condition=%wide.region_6.7_spmd, body=%wide.region_3.6_spmd.sunk | while | flops 1124856320 | bytes 54661240 | solution.py:115
  100.2 4.3 fusion.163
  104.6 5.1 fusion.164
  114.8 4.3 fusion.163
  119.1 5.1 fusion.164
  137.1 23.5 %collective-permute-done.5 = bf16[2,256,1024]{2,1,0:T(8,128)(2,1)S(1)} collective-permute-done((bf16[2,256,1024]{2,1,0:T(8,128)(2,1)S(1)}, bf16[2,256,1024]{2,1,0:T(8,128)(2,1)S(1)}, u32[]{:S(2)}, u32[]{:S(2)}) %collective-permute-start.5) | collective-permute-done | bytes 1048608 | tf_op jit(solution)/shard_map/ppermute | solution.py:178
  163.7 24.0 %collective-permute-done.7 = bf16[2,256,1024]{2,1,0:T(8,128)(2,1)S(1)} collective-permute-done((bf16[2,256,1024]{2,1,0:T(8,128)(2,1)S(1)}, bf16[2,256,1024]{2,1,0:T(8,128)(2,1)S(1)}, u32[]{:S(2)}, u32[]{:S(2)}) %collective-permute-start.7) | collective-permute-done | bytes 1048608 | tf_op jit(solution)/shard_map/ppermute | solution.py:178
  188.3 20.7 %collective-permute-done.10 = bf16[2,256,1024]{2,1,0:T(8,128)(2,1)} collective-permute-done((bf16[2,256,1024]{2,1,0:T(8,128)(2,1)}, bf16[2,256,1024]{2,1,0:T(8,128)(2,1)}, u32[]{:S(2)}, u32[]{:S(2)}) %collective-permute-start.10) | collective-permute-done | bytes 1048608 | tf_op jit(solution)/shard_map/ppermute | solution.py:178
  210.0 12.2 %fusion.88 = f32[2048,1152]{1,0:T(8,128)} fusion(bf16[1024,3456]{0,1:T(8,128)(2,1)} %all-gather.8.cloned.1.call-done, bf16[512,1024]{1,0:T(8,128)(2,1)} %bitcast.39, bf16[512,1024]{1,0:T(8,128)(2,1)} %bitcast.443, bf16[512,1024]{1,0:T(8,128)(2,1)} %bitcast.447, bf16[512,1024]{1,0:T(8,128)(2,1)} %bitcast.420), kind=kOutput, calls=%fused_computation.146 | convolution fusion | flops 4848615424 | bytes 15990784 | tf_op jit(solution)/shard_map/dot_general | solution.py:217
  222.2 3.3 slice.207
  225.4 4.3 copy.197
  229.7 5.6 reshape_reshape.13
  235.3 12.3 %fusion.92 = f32[2048,1152]{1,0:T(8,128)} fusion(bf16[1024,3456]{0,1:T(8,128)(2,1)} %all-gather.8.cloned.1.call-done, bf16[512,1024]{1,0:T(8,128)(2,1)} %bitcast.39, bf16[512,1024]{1,0:T(8,128)(2,1)} %bitcast.444, bf16[512,1024]{1,0:T(8,128)(2,1)} %bitcast.448, bf16[512,1024]{1,0:T(8,128)(2,1)} %bitcast.421), kind=kOutput, calls=%fused_computation.150 | convolution fusion | flops 4848615424 | bytes 15990784 | tf_op jit(solution)/shard_map/dot_general | solution.py:217
  247.6 18.6 %multiply_convert_fusion = (bf16[2048,1152]{1,0:T(8,128)(2,1)}, bf16[2048,1152]{1,0:T(8,128)(2,1)}, bf16[2048,1152]{1,0:T(8,128)(2,1)}) fusion(f32[2048,1152]{1,0:T(8,128)} %fusion.92, f32[2048,1152]{1,0:T(8,128)} %fusion.88, bf16[1152,1024]{1,0:T(8,128)(2,1)} %reshape_reshape.13, bf16[512,1024]{1,0:T(8,128)(2,1)} %bitcast.47, ...), kind=kOutput, calls=%fused_computation.66 | convolution fusion | flops 4884004864 | bytes 39583744 | tf_op jit(solution)/shard_map/dot_general | solution.py:221
  266.2 8.3 %fusion.90 = f32[2048,1024]{1,0:T(8,128)S(1)} fusion(bf16[2048,1152]{1,0:T(8,128)(2,1)} %get-tuple-element.323, bf16[1024,3456]{0,1:T(8,128)(2,1)} %all-gather.8.cloned.1.call-done), kind=kOutput, calls=%fused_computation.148 | convolution fusion | flops 4831838208 | bytes 15466496 | tf_op jit(solution)/shard_map/dot_general | solution.py:221
  274.5 7.7 %add_convert_fusion = bf16[2048,1024]{1,0:T(8,128)(2,1)S(1)} fusion(f32[2048,1024]{1,0:T(8,128)S(1)} %fusion.90, bf16[2048,1152]{1,0:T(8,128)(2,1)S(1)} %copy-done.68, bf16[1024,3456]{0,1:T(8,128)(2,1)} %all-gather.8.cloned.1.call-done), kind=kOutput, calls=%fused_computation.74 | convolution fusion | flops 4836032512 | bytes 19660800 | tf_op jit(solution)/shard_map/dot_general | solution.py:221
  286.0 6.3 convert_multiply_fusion
  295.4 9.5 %convolution_convert_fusion = bf16[1152,1024]{1,0:T(8,128)(2,1)} fusion(bf16[2048,1152]{1,0:T(8,128)(2,1)} %get-tuple-element.324, bf16[512,1024]{1,0:T(8,128)(2,1)} %bitcast.47, bf16[512,1024]{1,0:T(8,128)(2,1)} %bitcast.46, bf16[512,1024]{1,0:T(8,128)(2,1)} %bitcast.45, bf16[512,1024]{1,0:T(8,128)(2,1)} %bitcast.44), kind=kOutput, calls=%fused_computation.82 | convolution fusion | flops 4849795072 | bytes 11272192 | tf_op jit(solution)/shard_map/dot_general | solution.py:227
  304.9 14.7 %collective-permute-done.14 = bf16[2,256,1024]{2,1,0:T(8,128)(2,1)S(1)} collective-permute-done((bf16[2,256,1024]{2,1,0:T(8,128)(2,1)S(1)}, bf16[2,256,1024]{2,1,0:T(8,128)(2,1)S(1)}, u32[]{:S(2)}, u32[]{:S(2)}) %collective-permute-start.14) | collective-permute-done | bytes 1048608 | tf_op jit(solution)/shard_map/ppermute | solution.py:178
  321.5 4.0 constant_dynamic-update-slice_fusion.7
  326.9 9.4 %convolution_convert_fusion.1 = bf16[1024,1152]{1,0:T(8,128)(2,1)} fusion(bf16[2048,1152]{1,0:T(8,128)(2,1)S(1)} %bitcast.452, bf16[512,1024]{1,0:T(8,128)(2,1)} %bitcast.39, bf16[512,1024]{1,0:T(8,128)(2,1)S(1)} %bitcast.445, bf16[512,1024]{1,0:T(8,128)(2,1)S(1)} %bitcast.449, bf16[512,1024]{1,0:T(8,128)(2,1)S(1)} %bitcast.422), kind=kOutput, calls=%fused_computation.83 | convolution fusion | flops 4849795072 | bytes 11272192 | tf_op jit(solution)/shard_map/dot_general | solution.py:227
  336.3 14.2 %collective-permute-done.15 = bf16[2,256,1024]{2,1,0:T(8,128)(2,1)} collective-permute-done((bf16[2,256,1024]{2,1,0:T(8,128)(2,1)}, bf16[2,256,1024]{2,1,0:T(8,128)(2,1)}, u32[]{:S(2)}, u32[]{:S(2)}) %collective-permute-start.15) | collective-permute-done | bytes 1048608 | tf_op jit(solution)/shard_map/ppermute | solution.py:178
  350.5 8.1 %convolution_convert_fusion.2 = bf16[1024,1152]{1,0:T(8,128)(2,1)} fusion(bf16[2048,1152]{1,0:T(8,128)(2,1)S(1)} %bitcast.454, bf16[512,1024]{1,0:T(8,128)(2,1)} %bitcast.39, bf16[512,1024]{1,0:T(8,128)(2,1)S(1)} %bitcast.446, bf16[512,1024]{1,0:T(8,128)(2,1)S(1)} %bitcast.450, bf16[512,1024]{1,0:T(8,128)(2,1)S(1)} %bitcast.423), kind=kOutput, calls=%fused_computation.84 | convolution fusion | flops 4849795072 | bytes 11272192 | tf_op jit(solution)/shard_map/dot_general | solution.py:227
  358.7 4.2 reshape_reshape.15
  362.8 5.7 pad_maximum_fusion
  376.2 3.6 convolution_convert_fusion.5
  383.4 93.9 %while.29 = (s32[]{:T(128)}, f32[2,1024,2,64]{1,3,2,0:T(8,128)}, f32[2,1024,2,64]{1,3,2,0:T(8,128)}, bf16[2,2,512,2,2,64]{2,5,4,3,1,0:T(8,128)(2,1)}, bf16[2,2,5...) while((s32[]{:T(128)}, f32[2,1024,2,64]{1,3,2,0:T(8,128)}, ...), condition=%wide.region_12.13_spmd.clone, body=%wide.region_10.12_spmd.clone.sunk | while | flops 2749624832 | bytes 161665392 | solution.py:164
  386.2 3.5 fusion.173
  389.7 4.9 fusion.177
  394.7 11.2 %fusion.174 = (f32[2,2,2,512]{3,2,1,0:T(2,128)}, f32[2,2,512,2,1024]{4,2,3,1,0:T(8,128)}) fusion(f32[2,2,512,2,1024]{4,2,3,1,0:T(8,128)S(1)} %fusion.173, f32[2,2,2,512]{3,2,1,0:T(2,128)} %copy-done.33, pred[512,1024]{1,0:T(8,128)(4,1)S(1)} %iota_compare_fusion.8, bf16[2,1024,2,64]{1,3,2,0:T(8,128)(2,1)} %get-tuple-element.550, ...), kind=kOutput, calls=%fused_computation.23.clone.1 | convolution fusion | flops 557838336 | bytes 35160068 | tf_op jit(solution)/shard_map/while/body/eval_jaxpr/bqkgd,bskd->bkgqs/dot_general | solution.py:143
  405.9 11.4 %fusion.175 = bf16[2,2,2,512,1024]{4,3,2,1,0:T(8,128)(2,1)} fusion(f32[2,2,512,2,1024]{4,2,3,1,0:T(8,128)} %get-tuple-element.491, f32[2,2,512,2,1024]{4,2,3,1,0:T(8,128)S(1)} %fusion.173, f32[2,2,2,512]{3,2,1,0:T(2,128)} %get-tuple-element.492, f32[2,2,2,512]{3,2,1,0:T(2,128)} %copy-done.33, pred[512,1024]{1,0:T(8,128)(4,1)S(1)} %iota_compare_fusion.8), kind=kLoop, calls=%fused_computation.25.clone.1 | loop fusion | flops 25165824 | bytes 42500096 | tf_op jit(solution)/shard_map/while/body/eval_jaxpr/convert_element_type | solution.py:147
  417.3 5.3 fusion.176
  422.6 6.5 fusion.178
  432.5 3.5 fusion.173
  436.0 5.9 fusion.177
  442.0 11.2 %fusion.174 = (f32[2,2,2,512]{3,2,1,0:T(2,128)}, f32[2,2,512,2,1024]{4,2,3,1,0:T(8,128)}) fusion(f32[2,2,512,2,1024]{4,2,3,1,0:T(8,128)S(1)} %fusion.173, f32[2,2,2,512]{3,2,1,0:T(2,128)} %copy-done.33, pred[512,1024]{1,0:T(8,128)(4,1)S(1)} %iota_compare_fusion.8, bf16[2,1024,2,64]{1,3,2,0:T(8,128)(2,1)} %get-tuple-element.550, ...), kind=kOutput, calls=%fused_computation.23.clone.1 | convolution fusion | flops 557838336 | bytes 35160068 | tf_op jit(solution)/shard_map/while/body/eval_jaxpr/bqkgd,bskd->bkgqs/dot_general | solution.py:143
  453.2 11.3 %fusion.175 = bf16[2,2,2,512,1024]{4,3,2,1,0:T(8,128)(2,1)} fusion(f32[2,2,512,2,1024]{4,2,3,1,0:T(8,128)} %get-tuple-element.491, f32[2,2,512,2,1024]{4,2,3,1,0:T(8,128)S(1)} %fusion.173, f32[2,2,2,512]{3,2,1,0:T(2,128)} %get-tuple-element.492, f32[2,2,2,512]{3,2,1,0:T(2,128)} %copy-done.33, pred[512,1024]{1,0:T(8,128)(4,1)S(1)} %iota_compare_fusion.8), kind=kLoop, calls=%fused_computation.25.clone.1 | loop fusion | flops 25165824 | bytes 42500096 | tf_op jit(solution)/shard_map/while/body/eval_jaxpr/convert_element_type | solution.py:147
  464.5 5.2 fusion.176
  469.7 6.5 fusion.178
  481.8 3.2 reshape.528
  485.0 4.0 reshape.527
  489.0 3.4 convolution_convert_fusion.6
  493.3 4.1 all-to-all-start.1
  499.6 3.6 copy.234
  503.2 3.1 reshape.542
  513.1 3.1 reshape.541
  519.8 3.1 fusion.68
  524.4 8.4 %fusion.56 = (bf16[1024]{0:T(1024)(128)(2,1)S(1)}, bf16[2048,1024]{1,0:T(8,128)(2,1)}) fusion(f32[2,1024,1024]{2,1,0:T(8,128)} %convert_multiply_fusion, bf16[1024,896]{0,1:T(8,128)(2,1)S(1)} %copy-done.38, bf16[2048,128]{1,0:T(8,128)(2,1)S(1)} %copy-done.44, bf16[2048,128]{1,0:T(8,128)(2,1)} %reshape.541, bf16[2048,256]{1,0:T(8,128)(2,1)} %bitcast.424), kind=kOutput, calls=%fused_computation.73 | convolution fusion | flops 2160065536 | bytes 15730688 | tf_op jit(solution)/shard_map/dot_general | solution.py:221
  532.9 5.0 bitcast_convert_fusion
  544.4 8.2 %convolution_convert_fusion.3 = bf16[2048,1024]{1,0:T(8,128)(2,1)S(1)} fusion(bf16[2048,1152]{1,0:T(8,128)(2,1)} %get-tuple-element.324, bf16[1152,1024]{1,0:T(8,128)(2,1)S(1)} %copy-done.34), kind=kOutput, calls=%fused_computation.85 | convolution fusion | flops 4833935360 | bytes 11272192 | tf_op jit(solution)/shard_map/dot_general | solution.py:217
  559.1 23.5 %collective-permute-done.23 = bf16[2,256,1024]{2,1,0:T(8,128)(2,1)S(1)} collective-permute-done((bf16[2,256,1024]{2,1,0:T(8,128)(2,1)S(1)}, bf16[2,256,1024]{2,1,0:T(8,128)(2,1)S(1)}, u32[]{:S(2)}, u32[]{:S(2)}) %collective-permute-start.23) | collective-permute-done | bytes 1048608 | tf_op jit(solution)/shard_map/ppermute | solution.py:178
  583.4 20.9 %collective-permute-done.20 = bf16[2,256,1024]{2,1,0:T(8,128)(2,1)S(1)} collective-permute-done((bf16[2,256,1024]{2,1,0:T(8,128)(2,1)S(1)}, bf16[2,256,1024]{2,1,0:T(8,128)(2,1)S(1)}, u32[]{:S(2)}, u32[]{:S(2)}) %collective-permute-start.20) | collective-permute-done | bytes 1048608 | tf_op jit(solution)/shard_map/ppermute | solution.py:178
  608.2 10.4 %all-gather = bf16[576,896]{1,0:T(8,128)(2,1)S(1)} all-gather(bf16[144,896]{1,0:T(8,128)(2,1)} %reduce-scatter.3.cloned.1.call-done), channel_id=2, replica_groups=mesh['fsdp'=8,'seq'=4] {'seq'}, dimensions={0}, use_global_device_ids=true | all-gather | bytes 1290240 | tf_op jit(solution)/shard_map/all_gather | solution.py:404
  626.5 12.4 %all-gather.10.cloned.1.call-done = bf16[512,3456]{1,0:T(8,128)(2,1)} async-done(((bf16[128,3456]{1,0:T(8,128)(2,1)}), bf16[512,3456]{1,0:T(8,128)(2,1)}) %all-gather.10.cloned.1.call-update) | async-done | bytes 3538960 | tf_op jit(solution)/shard_map/all_gather | solution.py:403
  638.9 4.8 fusion.126
  646.6 3.0 copy.243
  649.6 3.3 copy.218
  652.9 3.0 copy.224
  (368 shorter events, 154.3 us)
Async XLA Ops:
  7.2 54.4 %all-gather.6.cloned.1.call-start = ((), (), s32[]{:S(2)}) async-start(), calls=%async_computation.4 | async-start | bytes 2064384 | tf_op jit(solution)/shard_map/all_gather | solution.py:275
  11.0 26.5 %collective-permute-start.1 = (bf16[2,256,1024]{2,1,0:T(8,128)(2,1)}, bf16[2,256,1024]{2,1,0:T(8,128)(2,1)}, u32[]{:S(2)}, u32[]{:S(2)}) collective-permute-start(bf16[2,256,1024]{2,1,0:T(8,128)(2,1)} %param.18), channel_id=1, source_target_pairs={{0,2},{1,3},{2,0},{3,1},{4,6},{5,7},{6,4},{7,5},{8,10},{9,11},{10,... | collective-permute-start | bytes 3145736 | tf_op jit(solution)/shard_map/ppermute | solution.py:178
  14.0 34.0 %collective-permute-start = (bf16[2,256,1024]{2,1,0:T(8,128)(2,1)}, bf16[2,256,1024]{2,1,0:T(8,128)(2,1)}, u32[]{:S(2)}, u32[]{:S(2)}) collective-permute-start(bf16[2,256,1024]{2,1,0:T(8,128)(2,1)} %param.18), channel_id=1, source_target_pairs={{0,1},{1,0},{2,3},{3,2},{4,5},{5,4},{6,7},{7,6},{8,9},{9,8},{10,11... | collective-permute-start | bytes 3145736 | tf_op jit(solution)/shard_map/ppermute | solution.py:178
  15.2 77.8 %copy-start.22 = (f32[1024,64]{0,1:T(8,128)}, f32[1024,64]{0,1:T(8,128)S(1)}, u32[]{:S(2)}) copy-start(f32[1024,64]{0,1:T(8,128)S(1)} %get-tuple-element.362) | copy-start | bytes 786436
  15.2 77.8 %copy-start.24 = (f32[1024,64]{0,1:T(8,128)}, f32[1024,64]{0,1:T(8,128)S(1)}, u32[]{:S(2)}) copy-start(f32[1024,64]{0,1:T(8,128)S(1)} %get-tuple-element.363) | copy-start | bytes 786436
  15.9 65.8 %copy-start.60 = (f32[64]{0:T(128)}, f32[64]{0:T(128)S(1)}, u32[]{:S(2)}) copy-start(f32[64]{0:T(128)S(1)} %get-tuple-element.372) | copy-start | bytes 772
  15.9 68.3 %copy-start.62 = (f32[64]{0:T(128)}, f32[64]{0:T(128)S(1)}, u32[]{:S(2)}) copy-start(f32[64]{0:T(128)S(1)} %get-tuple-element.373) | copy-start | bytes 772
  37.5 15.1 %collective-permute-start.2 = (bf16[2,256,1024]{2,1,0:T(8,128)(2,1)}, bf16[2,256,1024]{2,1,0:T(8,128)(2,1)}, u32[]{:S(2)}, u32[]{:S(2)}) collective-permute-start(bf16[2,256,1024]{2,1,0:T(8,128)(2,1)} %collective-permute-done.1), channel_id=1, source_target_pairs={{0,1},{1,0},{2,3},{3,2},{4,5},{5,4},{6,7},{7,6},{8,9},{9,8},{10,11... | collective-permute-start | bytes 3145736 | tf_op jit(solution)/shard_map/ppermute | solution.py:178
  37.7 49.4 %copy-start.58 = (f32[256]{0:T(256)}, f32[256]{0:T(256)S(1)}, u32[]{:S(2)}) copy-start(f32[256]{0:T(256)S(1)} %mul.503) | copy-start | bytes 3076
  58.1 11.9 %copy-start.54 = (f32[2,1024]{1,0:T(2,128)}, f32[2,1024]{1,0:T(2,128)S(1)}, u32[]{:S(2)}) copy-start(f32[2,1024]{1,0:T(2,128)S(1)} %add_rsqrt_fusion.2) | copy-start | bytes 24580
  75.4 53.6 %all-to-all-start = ((bf16[4,256,256]{1,2,0:T(8,128)(2,1)}), bf16[4,256,256]{1,2,0:T(8,128)(2,1)}, u32[]{:S(2)}, u32[]{:S(2)}) async-start(bf16[4,256,256]{1,2,0:T(8,128)(2,1)} %bitcast.319), calls=%async_computation | async-start | bytes 1048576 | tf_op jit(solution)/shard_map/all_to_all | solution.py:303
  79.5 130.4 %all-gather.8.cloned.1.call-start = ((), (), s32[]{:S(2)}) async-start(), calls=%async_computation.5 | async-start | bytes 7962624 | tf_op jit(solution)/shard_map/all_gather | solution.py:291
  80.3 464.1 %reduce-scatter.5.cloned.1.call-start = ((), (), s32[]{:S(2)}) async-start(), calls=%async_computation.7 | async-start | bytes 7962624 | tf_op jit(solution)/shard_map/reduce_scatter | solution.py:358
  131.7 28.9 %copy-start.11 = (bf16[2,256,1024]{2,1,0:T(8,128)(2,1)S(1)}, bf16[2,256,1024]{2,1,0:T(8,128)(2,1)}, u32[]{:S(2)}) copy-start(bf16[2,256,1024]{2,1,0:T(8,128)(2,1)} %param.18) | copy-start | bytes 3145732
  131.9 2.8 collective-permute-start.4
  132.5 28.9 %copy-start.50 = (f32[1024,1]{0,1:T(1,128)S(1)}, f32[1024,1]{0,1:T(1,128)}, u32[]{:S(2)}) copy-start(f32[1024,1]{0,1:T(1,128)} %get-tuple-element.356) | copy-start | bytes 12292
  132.5 4.7 collective-permute-start.3
  135.2 25.5 %collective-permute-start.5 = (bf16[2,256,1024]{2,1,0:T(8,128)(2,1)S(1)}, bf16[2,256,1024]{2,1,0:T(8,128)(2,1)S(1)}, u32[]{:S(2)}, u32[]{:S(2)}) collective-permute-start(bf16[2,256,1024]{2,1,0:T(8,128)(2,1)S(1)} %add_convert_fusion.2), channel_id=1, source_target_pairs={{0,2},{1,3},{2,0},{3,1},{4,6},{5,7},{6,4},{7,5},{8,10},{9,11},{10,... | collective-permute-start | bytes 3145736 | tf_op jit(solution)/shard_map/ppermute | solution.py:178
  161.4 160.1 %copy-start.2 = (f32[2,256,1024]{2,1,0:T(8,128)}, f32[2,256,1024]{2,1,0:T(8,128)S(1)}, u32[]{:S(2)}) copy-start(f32[2,256,1024]{2,1,0:T(8,128)S(1)} %get-tuple-element.317) | copy-start | bytes 6291460
  161.6 26.1 %collective-permute-start.7 = (bf16[2,256,1024]{2,1,0:T(8,128)(2,1)S(1)}, bf16[2,256,1024]{2,1,0:T(8,128)(2,1)S(1)}, u32[]{:S(2)}, u32[]{:S(2)}) collective-permute-start(bf16[2,256,1024]{2,1,0:T(8,128)(2,1)S(1)} %multiply_convert_fusion.4), channel_id=1, source_target_pairs={{0,2},{1,3},{2,0},{3,1},{4,6},{5,7},{6,4},{7,5},{8,10},{9,11},{10,... | collective-permute-start | bytes 3145736 | tf_op jit(solution)/shard_map/ppermute | solution.py:178
  163.4 45.6 %collective-permute-start.10 = (bf16[2,256,1024]{2,1,0:T(8,128)(2,1)}, bf16[2,256,1024]{2,1,0:T(8,128)(2,1)}, u32[]{:S(2)}, u32[]{:S(2)}) collective-permute-start(bf16[2,256,1024]{2,1,0:T(8,128)(2,1)} %param.29), channel_id=1, source_target_pairs={{0,2},{1,3},{2,0},{3,1},{4,6},{5,7},{6,4},{7,5},{8,10},{9,11},{10,... | collective-permute-start | bytes 3145736 | tf_op jit(solution)/shard_map/ppermute | solution.py:178
  163.7 45.2 %collective-permute-start.6 = (bf16[2,256,1024]{2,1,0:T(8,128)(2,1)S(1)}, bf16[2,256,1024]{2,1,0:T(8,128)(2,1)S(1)}, u32[]{:S(2)}, u32[]{:S(2)}) collective-permute-start(bf16[2,256,1024]{2,1,0:T(8,128)(2,1)S(1)} %multiply_convert_fusion.4), channel_id=1, source_target_pairs={{0,1},{1,0},{2,3},{3,2},{4,5},{5,4},{6,7},{7,6},{8,9},{9,8},{10,11... | collective-permute-start | bytes 3145736 | tf_op jit(solution)/shard_map/ppermute | solution.py:178
  187.7 21.2 %copy-start.64 = (bf16[2,256,1024]{2,1,0:T(8,128)(2,1)}, bf16[2,256,1024]{2,1,0:T(8,128)(2,1)S(1)}, u32[]{:S(2)}) copy-start(bf16[2,256,1024]{2,1,0:T(8,128)(2,1)S(1)} %collective-permute-done.7) | copy-start | bytes 3145732
  187.7 22.2 %collective-permute-start.8 = (bf16[2,256,1024]{2,1,0:T(8,128)(2,1)S(1)}, bf16[2,256,1024]{2,1,0:T(8,128)(2,1)}, u32[]{:S(2)}, u32[]{:S(2)}) collective-permute-start(bf16[2,256,1024]{2,1,0:T(8,128)(2,1)S(1)} %collective-permute-done.7), channel_id=1, source_target_pairs={{0,1},{1,0},{2,3},{3,2},{4,5},{5,4},{6,7},{7,6},{8,9},{9,8},{10,11... | collective-permute-start | bytes 3145736 | tf_op jit(solution)/shard_map/ppermute | solution.py:178
  187.7 59.9 %collective-permute-start.9 = (bf16[2,256,1024]{2,1,0:T(8,128)(2,1)}, bf16[2,256,1024]{2,1,0:T(8,128)(2,1)}, u32[]{:S(2)}, u32[]{:S(2)}) collective-permute-start(bf16[2,256,1024]{2,1,0:T(8,128)(2,1)} %param.29), channel_id=1, source_target_pairs={{0,1},{1,0},{2,3},{3,2},{4,5},{5,4},{6,7},{7,6},{8,9},{9,8},{10,11... | collective-permute-start | bytes 3145736 | tf_op jit(solution)/shard_map/ppermute | solution.py:178
  209.0 38.6 %collective-permute-start.11 = (bf16[2,256,1024]{2,1,0:T(8,128)(2,1)}, bf16[2,256,1024]{2,1,0:T(8,128)(2,1)}, u32[]{:S(2)}, u32[]{:S(2)}) collective-permute-start(bf16[2,256,1024]{2,1,0:T(8,128)(2,1)} %collective-permute-done.10), channel_id=1, source_target_pairs={{0,1},{1,0},{2,3},{3,2},{4,5},{5,4},{6,7},{7,6},{8,9},{9,8},{10,11... | collective-permute-start | bytes 3145736 | tf_op jit(solution)/shard_map/ppermute | solution.py:178
  266.2 8.3 %copy-start.68 = (bf16[2048,1152]{1,0:T(8,128)(2,1)S(1)}, bf16[2048,1152]{1,0:T(8,128)(2,1)}, u32[]{:S(2)}) copy-start(bf16[2048,1152]{1,0:T(8,128)(2,1)} %get-tuple-element.322) | copy-start | bytes 14155780
  285.5 6.8 %collective-permute-start.13 = (bf16[2,256,1024]{2,1,0:T(8,128)(2,1)}, bf16[2,256,1024]{2,1,0:T(8,128)(2,1)}, u32[]{:S(2)}, u32[]{:S(2)}) collective-permute-start(bf16[2,256,1024]{2,1,0:T(8,128)(2,1)} %bitcast.51), channel_id=1, source_target_pairs={{0,1},{1,0},{2,3},{3,2},{4,5},{5,4},{6,7},{7,6},{8,9},{9,8},{10,11... | collective-permute-start | bytes 3145736 | tf_op jit(solution)/shard_map/ppermute | solution.py:178
  292.3 12.6 %collective-permute-start.12 = (bf16[2,256,1024]{2,1,0:T(8,128)(2,1)S(1)}, bf16[2,256,1024]{2,1,0:T(8,128)(2,1)S(1)}, u32[]{:S(2)}, u32[]{:S(2)}) collective-permute-start(bf16[2,256,1024]{2,1,0:T(8,128)(2,1)S(1)} %bitcast.429), channel_id=1, source_target_pairs={{0,1},{1,0},{2,3},{3,2},{4,5},{5,4},{6,7},{7,6},{8,9},{9,8},{10,11... | collective-permute-start | bytes 3145736 | tf_op jit(solution)/shard_map/ppermute | solution.py:178
  293.9 25.6 %collective-permute-start.14 = (bf16[2,256,1024]{2,1,0:T(8,128)(2,1)S(1)}, bf16[2,256,1024]{2,1,0:T(8,128)(2,1)S(1)}, u32[]{:S(2)}, u32[]{:S(2)}) collective-permute-start(bf16[2,256,1024]{2,1,0:T(8,128)(2,1)S(1)} %fusion.85), channel_id=1, source_target_pairs={{0,2},{1,3},{2,0},{3,1},{4,6},{5,7},{6,4},{7,5},{8,10},{9,11},{10,... | collective-permute-start | bytes 3145736 | tf_op jit(solution)/shard_map/ppermute | solution.py:178
  295.4 24.2 %copy-start.17 = (bf16[2048,1024]{1,0:T(8,128)(2,1)S(1)}, bf16[2048,1024]{1,0:T(8,128)(2,1)}, u32[]{:S(2)}) copy-start(bf16[2048,1024]{1,0:T(8,128)(2,1)} %copy-done.16) | copy-start | bytes 12582916
  295.4 24.2 %copy-start.32 = (bf16[512,1024]{1,0:T(8,128)(2,1)S(1)}, bf16[512,1024]{1,0:T(8,128)(2,1)}, u32[]{:S(2)}) copy-start(bf16[512,1024]{1,0:T(8,128)(2,1)} %get-tuple-element.337) | copy-start | bytes 3145732
  319.6 7.3 %slice-start.1 = ((s8[4718592]{0:T(1024)(128)(4,1)}), s8[4194304]{0:T(1024)(128)(4,1)S(1)}, s32[]{:S(2)}) async-start(s8[4718592]{0:T(1024)(128)(4,1)} %bitcast.451), calls=%async_computation.10 | async-start | bytes 8388608
  325.5 10.8 %copy-start.29 = (bf16[2,1024,1024]{2,1,0:T(8,128)(2,1)}, bf16[2,1024,1024]{2,1,0:T(8,128)(2,1)S(1)}, u32[]{:S(2)}) copy-start(bf16[2,1024,1024]{2,1,0:T(8,128)(2,1)S(1)} %get-tuple-element.313) | copy-start | bytes 12582916
  325.5 25.0 %slice-start.3 = ((s8[4718592]{0:T(1024)(128)(4,1)}), s8[4194304]{0:T(1024)(128)(4,1)S(1)}, s32[]{:S(2)}) async-start(s8[4718592]{0:T(1024)(128)(4,1)} %bitcast.453), calls=%async_computation.12 | async-start | bytes 8388608
  325.5 25.0 %slice-start.4 = ((s8[4718592]{0:T(1024)(128)(4,1)}), s8[524288]{0:T(1024)(128)(4,1)S(1)}, s32[]{:S(2)}) async-start(s8[4718592]{0:T(1024)(128)(4,1)} %bitcast.453), calls=%async_computation.13 | async-start | bytes 1048576
  325.5 25.0 %collective-permute-start.15 = (bf16[2,256,1024]{2,1,0:T(8,128)(2,1)}, bf16[2,256,1024]{2,1,0:T(8,128)(2,1)}, u32[]{:S(2)}, u32[]{:S(2)}) collective-permute-start(bf16[2,256,1024]{2,1,0:T(8,128)(2,1)} %get-tuple-element.314), channel_id=1, source_target_pairs={{0,2},{1,3},{2,0},{3,1},{4,6},{5,7},{6,4},{7,5},{8,10},{9,11},{10,... | collective-permute-start | bytes 3145736 | tf_op jit(solution)/shard_map/ppermute | solution.py:178
  336.3 32.8 %collective-permute-start.16 = (bf16[2,256,1024]{2,1,0:T(8,128)(2,1)}, bf16[2,256,1024]{2,1,0:T(8,128)(2,1)}, u32[]{:S(2)}, u32[]{:S(2)}) collective-permute-start(bf16[2,256,1024]{2,1,0:T(8,128)(2,1)} %get-tuple-element.314), channel_id=1, source_target_pairs={{0,1},{1,0},{2,3},{3,2},{4,5},{5,4},{6,7},{7,6},{8,9},{9,8},{10,11... | collective-permute-start | bytes 3145736 | tf_op jit(solution)/shard_map/ppermute | solution.py:178
  350.5 23.2 %collective-permute-start.17 = (bf16[2,256,1024]{2,1,0:T(8,128)(2,1)}, bf16[2,256,1024]{2,1,0:T(8,128)(2,1)}, u32[]{:S(2)}, u32[]{:S(2)}) collective-permute-start(bf16[2,256,1024]{2,1,0:T(8,128)(2,1)} %collective-permute-done.15), channel_id=1, source_target_pairs={{0,1},{1,0},{2,3},{3,2},{4,5},{5,4},{6,7},{7,6},{8,9},{9,8},{10,11... | collective-permute-start | bytes 3145736 | tf_op jit(solution)/shard_map/ppermute | solution.py:178
  405.9 11.4 %copy-start.4 = (f32[2,1024,2,64]{1,3,2,0:T(8,128)S(1)}, f32[2,1024,2,64]{1,3,2,0:T(8,128)}, u32[]{:S(2)}) copy-start(f32[2,1024,2,64]{1,3,2,0:T(8,128)} %get-tuple-element.530) | copy-start | bytes 3145732 | tf_op jit(solution)/shard_map/while
  405.9 11.4 %copy-start.8 = (bf16[2,2,512,2,2,64]{2,5,4,3,1,0:T(8,128)(2,1)S(1)}, bf16[2,2,512,2,2,64]{2,5,4,3,1,0:T(8,128)(2,1)}, u32[]{:S(2)}) copy-start(bf16[2,2,512,2,2,64]{2,5,4,3,1,0:T(8,128)(2,1)} %get-tuple-element.545) | copy-start | bytes 3145732 | tf_op jit(solution)/shard_map/while
  453.2 11.3 %copy-start.4 = (f32[2,1024,2,64]{1,3,2,0:T(8,128)S(1)}, f32[2,1024,2,64]{1,3,2,0:T(8,128)}, u32[]{:S(2)}) copy-start(f32[2,1024,2,64]{1,3,2,0:T(8,128)} %get-tuple-element.530) | copy-start | bytes 3145732 | tf_op jit(solution)/shard_map/while
  453.2 11.3 %copy-start.8 = (bf16[2,2,512,2,2,64]{2,5,4,3,1,0:T(8,128)(2,1)S(1)}, bf16[2,2,512,2,2,64]{2,5,4,3,1,0:T(8,128)(2,1)}, u32[]{:S(2)}) copy-start(bf16[2,2,512,2,2,64]{2,5,4,3,1,0:T(8,128)(2,1)} %get-tuple-element.545) | copy-start | bytes 3145732 | tf_op jit(solution)/shard_map/while
  481.8 7.2 %copy-start.21 = (bf16[2048,256]{0,1:T(8,128)(2,1)S(1)}, bf16[2048,256]{0,1:T(8,128)(2,1)}, u32[]{:S(2)}) copy-start(bf16[2048,256]{0,1:T(8,128)(2,1)} %copy-done.20) | copy-start | bytes 3145732
  492.5 13.9 %copy-start.6 = (f32[2,1024,2,64]{1,3,2,0:T(8,128)S(1)}, f32[2,1024,2,64]{1,3,2,0:T(8,128)}, u32[]{:S(2)}) copy-start(f32[2,1024,2,64]{1,3,2,0:T(8,128)} %get-tuple-element.125) | copy-start | bytes 3145732
  493.3 45.1 %all-to-all-start.1 = ((bf16[256,4,256]{2,0,1:T(8,128)(2,1)}), bf16[256,4,256]{2,0,1:T(8,128)(2,1)}, u32[]{:S(2)}, u32[]{:S(2)}) async-start(bf16[256,4,256]{2,0,1:T(8,128)(2,1)} %bitcast.410), calls=%async_computation.1 | async-start | bytes 1048576 | tf_op jit(solution)/shard_map/all_to_all | solution.py:365
  497.5 110.8 %reduce-scatter.3.cloned.1.call-start = ((), (), s32[]{:S(2)}) async-start(), calls=%async_computation.6 | async-start | bytes 2322432 | tf_op jit(solution)/shard_map/reduce_scatter | solution.py:400
  499.6 8.0 %copy-start.23 = (f32[1024,64]{0,1:T(8,128)S(1)}, f32[1024,64]{0,1:T(8,128)}, u32[]{:S(2)}) copy-start(f32[1024,64]{0,1:T(8,128)} %copy-done.22) | copy-start | bytes 786436
  499.6 8.0 %copy-start.47 = (f32[2,1024,2]{1,2,0:T(2,128)S(1)}, f32[2,1024,2]{1,2,0:T(2,128)}, u32[]{:S(2)}) copy-start(f32[2,1024,2]{1,2,0:T(2,128)} %copy-done.45) | copy-start | bytes 49156
  499.6 8.0 %copy-start.61 = (f32[64]{0:T(128)S(1)}, f32[64]{0:T(128)}, u32[]{:S(2)}) copy-start(f32[64]{0:T(128)} %copy-done.60) | copy-start | bytes 772
  524.4 8.4 %copy-start.35 = (bf16[2,1024,2,64]{1,3,2,0:T(8,128)(2,1)S(1)}, bf16[2,1024,2,64]{1,3,2,0:T(8,128)(2,1)}, u32[]{:S(2)}) copy-start(bf16[2,1024,2,64]{1,3,2,0:T(8,128)(2,1)} %convert_element_type.344) | copy-start | bytes 1572868
  524.4 8.4 %copy-start.37 = (bf16[2,1024,2,64]{1,3,2,0:T(8,128)(2,1)S(1)}, bf16[2,1024,2,64]{1,3,2,0:T(8,128)(2,1)}, u32[]{:S(2)}) copy-start(bf16[2,1024,2,64]{1,3,2,0:T(8,128)(2,1)} %copy-done.36) | copy-start | bytes 1572868
  524.4 8.4 %copy-start.53 = (f32[1024,1]{0,1:T(1,128)S(1)}, f32[1024,1]{0,1:T(1,128)}, u32[]{:S(2)}) copy-start(f32[1024,1]{0,1:T(1,128)} %copy-done.52) | copy-start | bytes 12292
  524.4 8.4 %copy-start.56 = (f32[2,1024]{1,0:T(2,128)S(1)}, f32[2,1024]{1,0:T(2,128)}, u32[]{:S(2)}) copy-start(f32[2,1024]{1,0:T(2,128)} %copy-done.54) | copy-start | bytes 24580
  540.9 97.9 %all-gather.10.cloned.1.call-start = ((), (), s32[]{:S(2)}) async-start(), calls=%async_computation.8 | async-start | bytes 4423680 | tf_op jit(solution)/shard_map/all_gather | solution.py:403
  543.9 9.7 %collective-permute-start.22 = (bf16[2,256,1024]{2,1,0:T(8,128)(2,1)}, bf16[2,256,1024]{2,1,0:T(8,128)(2,1)}, u32[]{:S(2)}, u32[]{:S(2)}) collective-permute-start(bf16[2,256,1024]{2,1,0:T(8,128)(2,1)} %get-tuple-element.330), channel_id=1, source_target_pairs={{0,1},{1,0},{2,3},{3,2},{4,5},{5,4},{6,7},{7,6},{8,9},{9,8},{10,11... | collective-permute-start | bytes 3145736 | tf_op jit(solution)/shard_map/ppermute | solution.py:178
  553.0 29.5 %copy-start.12 = (bf16[2,256,1024]{2,1,0:T(8,128)(2,1)S(1)}, bf16[2,256,1024]{2,1,0:T(8,128)(2,1)}, u32[]{:S(2)}) copy-start(bf16[2,256,1024]{2,1,0:T(8,128)(2,1)} %param.18) | copy-start | bytes 3145732
  553.0 5.2 collective-permute-start.19
  553.2 5.9 collective-permute-start.21
  556.4 47.9 %copy-start.3 = (f32[2,256,1024]{2,1,0:T(8,128)S(1)}, f32[2,256,1024]{2,1,0:T(8,128)}, u32[]{:S(2)}) copy-start(f32[2,256,1024]{2,1,0:T(8,128)} %copy-done.2) | copy-start | bytes 6291460
  556.4 26.1 %collective-permute-start.23 = (bf16[2,256,1024]{2,1,0:T(8,128)(2,1)S(1)}, bf16[2,256,1024]{2,1,0:T(8,128)(2,1)S(1)}, u32[]{:S(2)}, u32[]{:S(2)}) collective-permute-start(bf16[2,256,1024]{2,1,0:T(8,128)(2,1)S(1)} %add_convert_fusion.1), channel_id=1, source_target_pairs={{0,2},{1,3},{2,0},{3,1},{4,6},{5,7},{6,4},{7,5},{8,10},{9,11},{10,... | collective-permute-start | bytes 3145736 | tf_op jit(solution)/shard_map/ppermute | solution.py:178
  558.1 25.3 %collective-permute-start.18 = (bf16[2,256,1024]{2,1,0:T(8,128)(2,1)S(1)}, bf16[2,256,1024]{2,1,0:T(8,128)(2,1)S(1)}, u32[]{:S(2)}, u32[]{:S(2)}) collective-permute-start(bf16[2,256,1024]{2,1,0:T(8,128)(2,1)S(1)} %bitcast.428), channel_id=1, source_target_pairs={{0,1},{1,0},{2,3},{3,2},{4,5},{5,4},{6,7},{7,6},{8,9},{9,8},{10,11... | collective-permute-start | bytes 3145736 | tf_op jit(solution)/shard_map/ppermute | solution.py:178
  558.6 45.7 %collective-permute-start.20 = (bf16[2,256,1024]{2,1,0:T(8,128)(2,1)S(1)}, bf16[2,256,1024]{2,1,0:T(8,128)(2,1)S(1)}, u32[]{:S(2)}, u32[]{:S(2)}) collective-permute-start(bf16[2,256,1024]{2,1,0:T(8,128)(2,1)S(1)} %fusion.81), channel_id=1, source_target_pairs={{0,2},{1,3},{2,0},{3,1},{4,6},{5,7},{6,4},{7,5},{8,10},{9,11},{10,... | collective-permute-start | bytes 3145736 | tf_op jit(solution)/shard_map/ppermute | solution.py:178
  583.4 22.7 %copy-start.19 = (f32[2,256,1024]{2,1,0:T(8,128)S(1)}, f32[2,256,1024]{2,1,0:T(8,128)}, u32[]{:S(2)}) copy-start(f32[2,256,1024]{2,1,0:T(8,128)} %get-tuple-element.315) | copy-start | bytes 6291460
  (48 other events, 192.4 us)
Sparse Core Ops, SparseCore 0:
  11.1 50.4 all-gather.5
  83.0 107.7 all-gather.7
  368.6 127.3 reduce-scatter.4
  541.1 66.7 reduce-scatter.2
  609.2 29.5 all-gather.9

commit v2 on v1

v2 whole, which is shorter than its diff:
```python
import functools

import jax
import jax.numpy as jnp
from jax import lax
from jax.experimental import pallas as pl
from jax.experimental.pallas import tpu as pltpu
from jax.sharding import PartitionSpec as P

HD = 64


RMS_EPSILON = 1e-05
ROPE_THETA = 1000000.0


def rms_scale(values):
    return lax.rsqrt(jnp.mean(values * values, axis=-1, keepdims=True) + RMS_EPSILON)


def rope_tables(positions, head_size):
    half_size = head_size // 2
    freqs = ROPE_THETA ** (-(jnp.arange(half_size, dtype=jnp.float32) * 2.0) / head_size)
    angles = positions.astype(jnp.float32)[:, None] * freqs[None, :]
    angles = jnp.concatenate([angles, angles], axis=-1)
    return (jnp.cos(angles), jnp.sin(angles))


def norm_back(grad, values, scale, gain):
    weighted = grad * gain
    grad_values = scale * weighted - values * scale**3 * jnp.mean(
        weighted * values, axis=-1, keepdims=True
    )
    grad_gain = jnp.sum(grad * values * scale, axis=(0, 1))
    return (grad_values, grad_gain)


LANES = 128
BLOCK_ROWS = 256


def low_half(shape):
    return lax.broadcasted_iota(jnp.int32, shape, len(shape) - 1) % LANES < HD


def first_part(shape):
    return lax.broadcasted_iota(jnp.int32, shape, len(shape) - 1) % HD < HD // 2


def pair_scale(raw):
    squares = raw * raw
    low = low_half(raw.shape)
    one = jnp.sum(jnp.where(low, squares, 0.0), axis=1, keepdims=True)
    two = jnp.sum(jnp.where(low, 0.0, squares), axis=1, keepdims=True)
    one = lax.rsqrt(one * (1.0 / HD) + RMS_EPSILON)
    two = lax.rsqrt(two * (1.0 / HD) + RMS_EPSILON)
    return jnp.where(low, one, two)


def pair_turn(raw, gain, cosine, sine):
    normed = raw * pair_scale(raw) * gain
    half = HD // 2
    turned = jnp.where(
        first_part(raw.shape),
        -pltpu.roll(normed, LANES - half, 1),
        pltpu.roll(normed, half, 1),
    )
    return normed * cosine + turned * sine


def pair_turn_back(grad, raw, gain, cosine, sine):
    half = HD // 2
    crossed = grad * sine
    turned = jnp.where(
        first_part(raw.shape),
        pltpu.roll(crossed, LANES - half, 1),
        -pltpu.roll(crossed, half, 1),
    )
    grad_normed = grad * cosine + turned
    scale = pair_scale(raw)
    grad_gain = jnp.sum(grad_normed * raw * scale, axis=0, keepdims=True)
    weighted = grad_normed * gain
    product = weighted * raw
    low = low_half(raw.shape)
    one = jnp.sum(jnp.where(low, product, 0.0), axis=1, keepdims=True) * (1.0 / HD)
    two = jnp.sum(jnp.where(low, 0.0, product), axis=1, keepdims=True) * (1.0 / HD)
    mean = jnp.where(low, one, two)
    return scale * weighted - raw * (scale * scale * scale) * mean, grad_gain


def both_halves(values, group):
    mine = low_half(values.shape) == (group == 0)
    return jnp.where(mine, values, pltpu.roll(values, HD, 1))


def stack_pair(block):
    low = low_half(block.shape)
    return jnp.concatenate([jnp.where(low, block, 0.0), jnp.where(low, 0.0, block)], axis=0)


def mul(left, right, left_dim, right_dim):
    return lax.dot_general(
        left, right, (((left_dim,), (right_dim,)), ((), ())), preferred_element_type=jnp.float32
    )


def unstack_pair(turned):
    rows = turned.shape[1] // 2
    top = lax.broadcasted_iota(jnp.int32, (LANES, rows), 0) < HD
    return jnp.where(top, turned[:, :rows], turned[:, rows:]).T


def causal_block(rows):
    keys = lax.broadcasted_iota(jnp.int32, (rows, 2 * rows), 0)
    queries = lax.broadcasted_iota(jnp.int32, (rows, 2 * rows), 1) % rows
    return keys <= queries


def attend_kernel(
    q_ref, k_ref, v_ref, cos_ref, sin_ref, gain_ref, q_out, k_out, mixed_out, both_k, both_v
):
    group = pl.program_id(1)
    length = q_ref.shape[1]
    rows = min(BLOCK_ROWS, length)
    cosine = cos_ref[...]
    sine = sin_ref[...]
    queries = pair_turn(q_ref[0], gain_ref[0:1, :], cosine, sine).astype(jnp.bfloat16)
    keys = pair_turn(k_ref[0], gain_ref[1:2, :], cosine, sine).astype(jnp.bfloat16)
    q_out[0] = queries
    k_out[0] = keys
    both_k[...] = both_halves(keys.astype(jnp.float32), group).astype(jnp.bfloat16)
    both_v[...] = both_halves(v_ref[0], group).T.astype(jnp.bfloat16)
    diagonal = causal_block(rows)
    for at in range(length // rows):
        start = at * rows
        block = q_out[0, start : start + rows, :].astype(jnp.float32) * HD ** (-0.5)
        pair = stack_pair(block).astype(jnp.bfloat16)
        last = jnp.exp(mul(both_k[start : start + rows, :], pair, 1, 1))
        last = jnp.where(diagonal, last, 0.0)
        total = jnp.sum(last, axis=0, keepdims=True)
        mixed = mul(both_v[:, start : start + rows], last.astype(jnp.bfloat16), 1, 0)
        if at > 0:
            before = jnp.exp(mul(both_k[:start, :], pair, 1, 1))
            total = total + jnp.sum(before, axis=0, keepdims=True)
            mixed = mixed + mul(both_v[:, :start], before.astype(jnp.bfloat16), 1, 0)
        mixed = mixed / total
        mixed_out[0, start : start + rows, :] = unstack_pair(mixed).astype(jnp.bfloat16)


def attend_back_kernel(
    low_q_ref,
    low_k_ref,
    q_ref,
    k_ref,
    v_ref,
    grad_ref,
    cos_ref,
    sin_ref,
    gain_ref,
    grad_out,
    gain_out,
    both_k,
    both_k_turned,
    both_v,
    sum_k,
    sum_v,
    grad_q,
    kept_k,
    kept_v,
):
    group = pl.program_id(1)
    length = q_ref.shape[1]
    rows = min(BLOCK_ROWS, length)
    q_width = grad_out.shape[2] - 2 * LANES
    groups = q_width // LANES
    keys = both_halves(low_k_ref[0].astype(jnp.float32), group)
    both_k[...] = keys.astype(jnp.bfloat16)
    both_k_turned[...] = keys.T.astype(jnp.bfloat16)
    both_v[...] = both_halves(v_ref[0], group).astype(jnp.bfloat16)
    diagonal = causal_block(rows)
    head_scale = HD ** (-0.5)

    for at in range(length // rows):
        start = at * rows
        here = slice(start, start + rows)
        block = low_q_ref[0, here, :].astype(jnp.float32) * head_scale
        pair = stack_pair(block).astype(jnp.bfloat16)
        grad_pair = stack_pair(grad_ref[0, here, :].astype(jnp.float32)).astype(jnp.bfloat16)
        spans = [(here, True)] + ([(slice(0, start), False)] if at > 0 else [])
        parts = []
        total = 0.0
        for span, masked in spans:
            exps = jnp.exp(mul(both_k[span, :], pair, 1, 1))
            if masked:
                exps = jnp.where(diagonal, exps, 0.0)
            total = total + jnp.sum(exps, axis=0, keepdims=True)
            parts.append(exps)
        inverse = 1.0 / total
        inner = 0.0
        both = []
        for (span, masked), exps in zip(spans, parts):
            probs = exps * inverse
            grad_probs = mul(both_v[span, :], grad_pair, 1, 1)
            inner = inner + jnp.sum(probs * grad_probs, axis=0, keepdims=True)
            both.append((probs, grad_probs))
        turned = 0.0
        for (span, masked), (probs, grad_probs) in zip(spans, both):
            grad_scores = (probs * (grad_probs - inner)).astype(jnp.bfloat16)
            add_v = mul(probs.astype(jnp.bfloat16), grad_pair, 1, 0)
            add_k = mul(grad_scores, pair, 1, 0)
            if masked:
                sum_v[span, :] = add_v
                sum_k[span, :] = add_k
            else:
                sum_v[span, :] = sum_v[span, :] + add_v
                sum_k[span, :] = sum_k[span, :] + add_k
            turned = turned + mul(both_k_turned[:, span], grad_scores, 1, 0)
        grad_q[here, :] = unstack_pair(turned) * head_scale

    def low(values):
        return values.astype(jnp.bfloat16).astype(jnp.float32)

    cosine = cos_ref[...]
    sine = sin_ref[...]
    raw_grad, gain_grad = pair_turn_back(
        low(grad_q[...]), q_ref[0], gain_ref[0:1, :], cosine, sine
    )
    grad_out[0, :, pl.ds(pl.multiple_of(group * LANES, LANES), LANES)] = raw_grad.astype(
        jnp.bfloat16
    )

    @pl.when((group == 0) & (pl.program_id(0) == 0))
    def _():
        gain_out[...] = jnp.zeros_like(gain_out)

    gain_out[0:1, :] = gain_out[0:1, :] + gain_grad
    mine = low_half((length, LANES)) == (group == 0)
    whole_k = sum_k[...] + pltpu.roll(sum_k[...], HD, 1)
    whole_v = sum_v[...] + pltpu.roll(sum_v[...], HD, 1)

    @pl.when(group == 0)
    def _():
        kept_k[...] = whole_k
        kept_v[...] = whole_v

    @pl.when(group == groups - 1)
    def _():
        all_k = low(jnp.where(mine, whole_k, kept_k[...]))
        all_v = jnp.where(mine, whole_v, kept_v[...])
        raw_k, gain_k = pair_turn_back(all_k, k_ref[0], gain_ref[1:2, :], cosine, sine)
        grad_out[0, :, q_width : q_width + LANES] = raw_k.astype(jnp.bfloat16)
        grad_out[0, :, q_width + LANES :] = all_v.astype(jnp.bfloat16)
        gain_out[1:2, :] = gain_out[1:2, :] + gain_k


def head_tables(length, qk_gain):
    cosine, sine = rope_tables(jnp.arange(length, dtype=jnp.int32), HD)
    twice = lambda table: jnp.concatenate([table, table], axis=1)
    return twice(cosine), twice(sine), twice(qk_gain.astype(jnp.float32))


def attend(qkv_raw, tables):
    batch, length, width = qkv_raw.shape
    groups = width // LANES - 2
    assert groups == 2
    column = lambda at: pl.BlockSpec((1, length, LANES), lambda b, g: (b, 0, at))
    own_column = pl.BlockSpec((1, length, LANES), lambda b, g: (b, 0, g))
    table = pl.BlockSpec((length, LANES), lambda b, g: (0, 0))
    pairs = batch * groups * length * length
    return pl.pallas_call(
        attend_kernel,
        grid=(batch, groups),
        in_specs=[
            own_column,
            column(groups),
            column(groups + 1),
            table,
            table,
            pl.BlockSpec((2, LANES), lambda b, g: (0, 0)),
        ],
        out_specs=[own_column, column(0), own_column],
        out_shape=[
            jax.ShapeDtypeStruct((batch, length, groups * LANES), jnp.bfloat16),
            jax.ShapeDtypeStruct((batch, length, LANES), jnp.bfloat16),
            jax.ShapeDtypeStruct((batch, length, groups * LANES), jnp.bfloat16),
        ],
        scratch_shapes=[
            pltpu.VMEM((length, LANES), jnp.bfloat16),
            pltpu.VMEM((LANES, length), jnp.bfloat16),
        ],
        cost_estimate=pl.CostEstimate(
            flops=pairs * 512, transcendentals=pairs, bytes_accessed=8 * qkv_raw.size
        ),
        name="attend",
    )(qkv_raw, qkv_raw, qkv_raw, *tables)


def attend_back(query_low, key_low, qkv_raw, grad_mixed, tables):
    batch, length, width = qkv_raw.shape
    groups = width // LANES - 2
    column = lambda at: pl.BlockSpec((1, length, LANES), lambda b, g: (b, 0, at))
    own_column = pl.BlockSpec((1, length, LANES), lambda b, g: (b, 0, g))
    table = pl.BlockSpec((length, LANES), lambda b, g: (0, 0))
    pairs = batch * groups * length * length
    return pl.pallas_call(
        attend_back_kernel,
        grid=(batch, groups),
        in_specs=[
            own_column,
            column(0),
            own_column,
            column(groups),
            column(groups + 1),
            own_column,
            table,
            table,
            pl.BlockSpec((2, LANES), lambda b, g: (0, 0)),
        ],
        out_specs=[
            pl.BlockSpec((1, length, width), lambda b, g: (b, 0, 0)),
            pl.BlockSpec((8, LANES), lambda b, g: (0, 0)),
        ],
        out_shape=[
            jax.ShapeDtypeStruct((batch, length, width), jnp.bfloat16),
            jax.ShapeDtypeStruct((8, LANES), jnp.float32),
        ],
        scratch_shapes=[
            pltpu.VMEM((length, LANES), jnp.bfloat16),
            pltpu.VMEM((LANES, length), jnp.bfloat16),
            pltpu.VMEM((length, LANES), jnp.bfloat16),
        ]
        + [pltpu.VMEM((length, LANES), jnp.float32)] * 5,
        cost_estimate=pl.CostEstimate(
            flops=pairs * 1280, transcendentals=pairs, bytes_accessed=12 * qkv_raw.size
        ),
        name="attend_back",
    )(query_low, key_low, qkv_raw, qkv_raw, qkv_raw, grad_mixed, *tables)


FFN_ROWS = 256


def ffn_kernel(two_ref, cot_ref, gate_w, up_w, down_w, *refs):
    hidden_out, gate_out, up_out, result_out, back_out = refs[-5:]
    two = two_ref[...]
    gate = mul(two, gate_w[...], 1, 0)
    upward = mul(two, up_w[...], 1, 0)
    grad_hidden = mul(cot_ref[...], down_w[...], 1, 1)
    sigma = 1.0 / (1.0 + jnp.exp(-gate))
    activated = gate * sigma
    hidden = (activated * upward).astype(jnp.bfloat16)
    grad_gate = grad_hidden * upward * sigma * (1.0 + gate * (1.0 - sigma))
    grad_gate = grad_gate.astype(jnp.bfloat16)
    grad_up = (grad_hidden * activated).astype(jnp.bfloat16)
    hidden_out[...] = hidden
    gate_out[...] = grad_gate
    up_out[...] = grad_up
    result_out[...] = mul(hidden, down_w[...], 1, 0).astype(jnp.bfloat16)
    back = mul(grad_gate, gate_w[...], 1, 1) + mul(grad_up, up_w[...], 1, 1)
    back_out[...] = back.astype(jnp.bfloat16)


def ffn(two, cot_all, second_all, down_w, first_row, kept):
    rows, width = two.shape
    local = down_w.shape[0]
    step = min(FFN_ROWS, rows)
    offset = first_row // step
    here = lambda size: pl.BlockSpec((step, size), lambda i: (i, 0))
    there = lambda size: pl.BlockSpec((step, size), lambda i: (i + offset, 0))
    whole = lambda shape, at: pl.BlockSpec(shape, lambda i: (0, at))
    total = cot_all.shape[0]
    kept = () if kept is None else kept
    return pl.pallas_call(
        ffn_kernel,
        grid=(rows // step,),
        in_specs=[
            here(width),
            there(width),
            whole((width, local), 0),
            whole((width, local), 1),
            whole((local, width), 0),
        ]
        + [pl.BlockSpec(memory_space=pl.ANY)] * len(kept),
        out_specs=[there(local)] * 3 + [here(width)] * 2,
        out_shape=[jax.ShapeDtypeStruct((total, local), jnp.bfloat16)] * 3
        + [jax.ShapeDtypeStruct((rows, width), jnp.bfloat16)] * 2,
        input_output_aliases={5 + at: at for at in range(len(kept))},
        cost_estimate=pl.CostEstimate(
            flops=12 * rows * width * local,
            transcendentals=rows * local,
            bytes_accessed=2 * (3 * width * local + rows * (4 * width + 3 * local)),
        ),
        name="ffn",
    )(two, cot_all, second_all, second_all, down_w, *kept)


def fold_rows(piece, part):
    units, width = piece.shape
    extra = piece[part:].reshape(units - part, width // LANES, LANES)
    extra = jnp.transpose(extra, (1, 0, 2)).reshape(part, LANES)
    return jnp.concatenate([piece[:part], extra], axis=1)


def unfold_rows(folded, units):
    lead = folded.shape[:-2]
    part = folded.shape[-2]
    width = folded.shape[-1] - LANES
    extra = folded[..., width:].reshape(lead + (width // LANES, units - part, LANES))
    extra = jnp.swapaxes(extra, -3, -2).reshape(lead + (units - part, width))
    return jnp.concatenate([folded[..., :width], extra], axis=-2)


def bits_of(count):
    return [1 << i for i in range(count.bit_length() - 1)]


def swap(values, bit, count):
    return lax.ppermute(values, "seq", [(i, i ^ bit) for i in range(count)])


def gather_blocks(block, count):
    blocks = {0: block}
    for bit in reversed(bits_of(count)):
        for at in list(blocks):
            blocks[at | bit] = swap(blocks[at], bit, count)
    return blocks


def scatter_blocks(blocks, count):
    blocks = dict(blocks)
    for bit in bits_of(count):
        kept = {}
        for at in blocks:
            if not at & bit:
                arrived = swap(blocks[at | bit].astype(jnp.bfloat16), bit, count)
                kept[at] = blocks[at].astype(jnp.float32) + arrived.astype(jnp.float32)
        blocks = kept
    return blocks[0]


def in_order(blocks, own, count):
    batch, rows, width = blocks[0].shape
    whole = jnp.zeros((batch, count * rows, width), blocks[0].dtype)
    for at in range(count):
        whole = lax.dynamic_update_slice(whole, blocks[at], (0, (own ^ at) * rows, 0))
    return whole


def from_order(whole, own, count):
    rows = whole.shape[1] // count
    return {
        at: lax.dynamic_slice_in_dim(whole, (own ^ at) * rows, rows, axis=1) for at in range(count)
    }


def dot(left, right):
    return jnp.dot(left, right, preferred_element_type=jnp.float32)


def dot_t(left, right):
    return lax.dot_general(
        left, right, (((1,), (1,)), ((), ())), preferred_element_type=jnp.float32
    )


def t_dot(left, right):
    return lax.dot_general(
        left, right, (((0,), (0,)), ((), ())), preferred_element_type=jnp.float32
    )


def per_device(
    fsdp,
    seq,
    tokens,
    w_query,
    w_key,
    w_value,
    w_out,
    w_gate,
    w_up,
    w_down,
    attn_gain,
    ffn_gain,
    qk_gain,
    cotangent,
):
    bf16 = jnp.bfloat16
    f32 = jnp.float32
    own = lax.axis_index("seq")
    batch, rows, width = tokens.shape
    length = rows * seq
    count = batch * length
    part = w_query.shape[0]
    q_width = w_query.shape[1] // seq
    kv_width = w_key.shape[1] // seq
    o_width = w_out.shape[1] // seq
    units = w_down.shape[0] // seq
    local = units * fsdp

    def columns(weight, size):
        return lax.dynamic_slice_in_dim(weight, own * size, size, axis=1)

    gains = jnp.stack([attn_gain, ffn_gain], axis=1)
    first = jnp.concatenate(
        [
            columns(w_query, q_width),
            columns(w_key, kv_width),
            columns(w_value, kv_width),
            columns(w_out, o_width),
            jnp.pad(gains, ((0, 0), (0, 126))),
        ],
        axis=1,
    )
    first_all = lax.all_gather(first, "fsdp", axis=0, tiled=True)
    qkv_width = q_width + 2 * kv_width
    w_qkv = first_all[:, :qkv_width]
    out_cols = first_all[:, qkv_width : qkv_width + o_width]
    attn_full = first_all[:, qkv_width + o_width].astype(f32)
    ffn_full = first_all[:, qkv_width + o_width + 1].astype(f32)

    def pick(weight):
        split = weight.reshape(part, fsdp, seq, units)
        return lax.dynamic_index_in_dim(split, own, axis=2, keepdims=False).reshape(part, local)

    down_own = lax.dynamic_slice_in_dim(w_down, own * units, units, axis=0)
    second = jnp.concatenate(
        [pick(w_gate), pick(w_up), fold_rows(down_own, part)], axis=1
    )
    second, _ = lax.optimization_barrier((second, first_all))
    second_all = lax.all_gather(second, "fsdp", axis=0, tiled=True)
    down_w = unfold_rows(second_all[:, 2 * local :].reshape(fsdp, part, local), units)
    down_w = down_w.reshape(local, width)

    token_blocks = gather_blocks(tokens, seq)
    inputs_all = in_order(token_blocks, own, seq)
    cotangent_in, _ = lax.optimization_barrier((cotangent, inputs_all))
    cot_blocks = gather_blocks(cotangent_in, seq)
    cot_all = jnp.concatenate(
        [cot_blocks[at].reshape(batch * rows, width) for at in range(seq)], axis=0
    )
    out_w = lax.all_to_all(out_cols, "seq", split_axis=0, concat_axis=1, tiled=True)

    inputs_all32 = inputs_all.astype(f32)
    scale_all = rms_scale(inputs_all32)
    hat_all = inputs_all32 * scale_all
    normed = (hat_all * attn_full).astype(bf16)
    flat_normed = normed.reshape(count, width)
    qkv_raw = dot(flat_normed, w_qkv).reshape(batch, length, qkv_width)
    tables = head_tables(length, qk_gain)
    query_low, key_low, mixed = attend(qkv_raw, tables)
    flat_mixed = mixed.reshape(count, q_width)
    branch = dot(flat_mixed, out_w).astype(bf16).reshape(batch, length, width)
    branch, cot_all = lax.optimization_barrier((branch, cot_all))
    inputs = tokens.astype(f32)
    middle = inputs + scatter_blocks(from_order(branch, own, seq), seq)

    scale_two = rms_scale(middle)
    normed_two = (middle * scale_two * ffn_full).astype(bf16)
    two_blocks = gather_blocks(normed_two, seq)
    flat = lambda values: values.reshape(batch * rows, width)
    half = seq // 2
    near = jnp.concatenate([flat(two_blocks[at]) for at in range(half)], axis=0)
    *kept, result_near, back_near = ffn(near, cot_all, second_all, down_w, 0, None)
    far = jnp.concatenate([flat(two_blocks[at]) for at in range(half, seq)], axis=0)
    hidden, grad_gate_act, grad_upward, result_far, back_far = ffn(
        far, cot_all, second_all, down_w, half * batch * rows, kept
    )
    two_all = jnp.concatenate([near, far], axis=0)

    def xor_blocks(one, two):
        pieces = [values.reshape(half, batch, rows, width) for values in (one, two)]
        return {at: pieces[at // half][at % half] for at in range(seq)}

    grad_two = scatter_blocks(xor_blocks(back_near, back_far), seq)
    grad_middle_norm, grad_ffn_gain = norm_back(grad_two, middle, scale_two, ffn_full)
    grad_middle = cotangent.astype(f32) + grad_middle_norm
    grad_branch = grad_middle.astype(bf16)
    branch_blocks = gather_blocks(grad_branch, seq)
    grad_down = t_dot(hidden, cot_all).astype(bf16)
    grad_gate = t_dot(two_all, grad_gate_act).astype(bf16)
    grad_up = t_dot(two_all, grad_upward).astype(bf16)
    grad_down = jax.vmap(lambda piece: fold_rows(piece, part))(grad_down.reshape(fsdp, units, width))
    grad_down = grad_down.reshape(width, local)
    ffn_sums = jnp.concatenate(
        [grad_gate, grad_up, grad_down], axis=1
    )
    ffn_share = lax.psum_scatter(ffn_sums, "fsdp", scatter_dimension=0, tiled=True)
    result_parts, _ = lax.optimization_barrier(
        ((result_near, result_far), tuple(branch_blocks.values()))
    )
    result = (middle + scatter_blocks(xor_blocks(*result_parts), seq)).astype(bf16)

    branch_all = in_order(branch_blocks, own, seq).reshape(count, width)
    grad_out = t_dot(flat_mixed, branch_all).astype(bf16)
    grad_out_cols = lax.all_to_all(grad_out, "seq", split_axis=1, concat_axis=0, tiled=True)
    grad_mixed = dot_t(branch_all, out_w).astype(bf16).reshape(batch, length, q_width)
    grad_qkv, gain_sums = attend_back(query_low, key_low, qkv_raw, grad_mixed, tables)
    grad_qkv, result = lax.optimization_barrier((grad_qkv, result))
    grad_qkv = grad_qkv.reshape(count, qkv_width)
    normed_back = dot_t(grad_qkv, w_qkv)
    normed_back_low = normed_back.astype(bf16).reshape(batch, length, width)
    grad_attn_gain = jnp.sum(normed_back * hat_all.reshape(count, width), axis=0)
    grad_normed = scatter_blocks(from_order(normed_back_low, own, seq), seq)
    inputs_norm, _ = norm_back(grad_normed, inputs, rms_scale(inputs), attn_full)
    grad_tokens = grad_middle + inputs_norm

    gain_cols = jnp.stack([grad_attn_gain, jnp.sum(grad_ffn_gain.reshape(1, width), axis=0)], axis=1)
    last = jnp.concatenate(
        [
            t_dot(flat_normed, grad_qkv).astype(bf16),
            grad_out_cols,
            jnp.pad(gain_cols.astype(bf16), ((0, 0), (0, 126))),
        ],
        axis=1,
    )
    last_width = last.shape[1]
    gain_sums = gain_sums[:2, :HD] + gain_sums[:2, HD:]
    qk_row = gain_sums.reshape(2 * HD).astype(bf16)
    qk_rows = jnp.zeros((fsdp, 16, last_width), bf16)
    qk_rows = qk_rows.at[:, 0, : 2 * HD].set(qk_row)
    last = jnp.concatenate([last.reshape(fsdp, part, last_width), qk_rows], axis=1)
    last_share = lax.psum_scatter(
        last.reshape(fsdp * (part + 16), last_width), "fsdp", scatter_dimension=0, tiled=True
    )
    share_blocks = gather_blocks(ffn_share, seq)
    ffn_shares = jnp.stack([share_blocks[at] for at in range(seq)]).astype(f32)
    for bit in bits_of(seq):
        turned = ffn_shares.reshape(-1, 2, bit, part, ffn_share.shape[1])[:, ::-1]
        ffn_shares = jnp.where((own & bit) > 0, turned.reshape(ffn_shares.shape), ffn_shares)
    last_shares = lax.all_gather(last_share, "seq", axis=0, tiled=False).astype(f32)

    def unpick(piece):
        split = piece.reshape(seq, part, fsdp, units)
        return jnp.transpose(split, (1, 2, 0, 3)).reshape(part, fsdp * seq * units)

    def side_by_side(piece):
        return jnp.transpose(piece, (1, 0, 2)).reshape(part, -1)

    shard_gate = unpick(ffn_shares[:, :, :local])
    shard_up = unpick(ffn_shares[:, :, local : 2 * local])
    shard_down = unfold_rows(ffn_shares[:, :, 2 * local :], units).reshape(seq * units, width)
    top = last_shares[:, :part]
    shard_query = side_by_side(top[:, :, :q_width])
    shard_key = side_by_side(top[:, :, q_width : q_width + kv_width])
    shard_value = side_by_side(top[:, :, q_width + kv_width : qkv_width])
    shard_out = side_by_side(top[:, :, qkv_width : qkv_width + o_width])
    shard_gains = jnp.sum(top[:, :, qkv_width + o_width : qkv_width + o_width + 2], axis=0)
    gain_total = jnp.sum(last_shares[:, part, : 2 * HD], axis=0).reshape(2, HD)
    return (
        result,
        grad_tokens,
        shard_query,
        shard_key,
        shard_value,
        shard_out,
        shard_gate,
        shard_up,
        shard_down,
        shard_gains[:, 0],
        shard_gains[:, 1],
        gain_total,
    )


def solution(mesh):
    placed = (
        P("fsdp", "seq", None),
        P("fsdp", None),
        P("fsdp", None),
        P("fsdp", None),
        P("fsdp", None),
        P("fsdp", None),
        P("fsdp", None),
        P("fsdp", None),
        P("fsdp"),
        P("fsdp"),
        P(),
        P("fsdp", "seq", None),
    )
    return jax.shard_map(
        functools.partial(per_device, mesh.shape["fsdp"], mesh.shape["seq"]),
        mesh=mesh,
        in_specs=placed,
        out_specs=(
            P("fsdp", "seq", None),
            P("fsdp", "seq", None),
            P("fsdp", None),
            P("fsdp", None),
            P("fsdp", None),
            P("fsdp", None),
            P("fsdp", None),
            P("fsdp", None),
            P("fsdp", None),
            P("fsdp"),
            P("fsdp"),
            P(),
        ),
        check_vma=False,
    )
```

time: 677 us -> 577 us (0.85)
  matrix products: 204 us -> 49.6 us
  Pallas kernels: 0 us -> 88.3 us
  waiting for transfers between devices: 182 us -> 232 us
  local copies, waits for them, and re-layouts: 127 us -> 78.8 us
  other arithmetic: 105 us -> 71.7 us
    pallas_call x0 -> x4, Pallas kernels: none -> 88.3 us  [the longest x2 44.8 us: ffn(): pl.pallas_call(ffn_kernel, grid=(rows // step,), in_specs=[here(width), t...]
    dot_general x14 -> x0, matrix products: 79.8 us -> none  [the longest x2 22.5 us: one_block(): jnp.einsum('bqkgd,bskd->bkgqs', grad_block, value_heads, preferred_elemen...]
    all_gather x1, waiting for transfers between devices: 3.54 us -> 39.8 us  [per_device(): first_all = lax.all_gather(first, 'fsdp', axis=0, tiled=True)]
    dot_general x5 -> x2, matrix products: 46.5 us -> 12.7 us  [dot_t(): lax.dot_general(left, right, (((1,), (1,)), ((), ())), preferred_element_...]
    dot_general x5 -> x2, matrix products: 42.3 us -> 9.4 us  [dot(): return jnp.dot(left, right, preferred_element_type=jnp.float32)]
    convert_element_type x9 -> x1, local copies, waits for them, and re-layouts: 24 us -> 0.09 us  [per_device(): qk_row = gain_sums.reshape(2 * HD).astype(bf16)]
    convert_element_type x8 -> x3, other arithmetic: 33.1 us -> 9.43 us  [the longest x1 4.85 us: per_device(): ffn_shares = jnp.stack([share_blocks[at] for at in range(seq)]).astype(f32)]
    another operation x8 -> x3, local copies, waits for them, and re-layouts: 16.8 us -> 1.18 us  [the longest x1 5.6 us: per_device(): second_all[:, 2 * local:].reshape(fsdp, part, local).reshape(local, width)]
  transfers between devices with their start and end apart: 31 -> 33, of which waited for: 11 -> 14; matrix products, arithmetic and copies ran while one was open for 52% -> 18% of each run, Pallas kernels for 0% -> 8%
where the time goes in v2:
time: 577 us; the launch traced here: 570 us
  waiting for transfers between devices  232 us (40%)
  Pallas kernels  88.3 us (15%)
  local copies, waits for them, and re-layouts  78.8 us (14%)
  other arithmetic  71.7 us (12%)
  matrix products  49.6 us (9%)
  starting transfers between devices  24 us (4%)
  between operations  15 us (3%)
  blocking collectives  10.1 us (2%)
    ppermute x27, waiting for transfers between devices, swap(): return lax.ppermute(values, 'seq', [(i, i ^ bit) for i in range(count)])  178 us
    pallas_call x2, Pallas kernels, ffn(): pl.pallas_call(ffn_kernel, grid=(rows // step,), in_specs=[here(width), t...  44.8 us
    all_gather x1, waiting for transfers between devices, per_device(): first_all = lax.all_gather(first, 'fsdp', axis=0, tiled=True)  39.8 us
    dot_general x5, matrix products, t_dot(): lax.dot_general(left, right, (((0,), (0,)), ((), ())), preferred_element_...  27.5 us
    unnamed x82, local copies, waits for them, and re-layouts  26.5 us
    pallas_call x1, Pallas kernels, attend_back(): pl.pallas_call(attend_back_kernel, grid=(batch, groups), in_specs=[own_co...  26.3 us
    pallas_call x1, Pallas kernels, attend(): pl.pallas_call(attend_kernel, grid=(batch, groups), in_specs=[own_column,...  17.2 us
    ppermute x27, starting transfers between devices, swap(): return lax.ppermute(values, 'seq', [(i, i ^ bit) for i in range(count)])  16.2 us
  transfers between devices with their start and end apart: 33, of which 14 were waited for; matrix products, arithmetic and copies ran while one was open for 18% of the time, Pallas kernels for 8%

profile of v2, /device:TPU:0, one launch (start us, length us, event | category | flops | bytes accessed | tf_op | source)
XLA Modules:
  0.0 569.6 jit_solution(16680486963504816468)
XLA Ops:
  12.2 1.7 copy.119
  13.9 2.5 copy.120
  16.4 1.8 constant_dynamic-slice_fusion.3
  21.5 39.8 %all-gather.4.cloned.1.call-done = bf16[1024,896]{1,0:T(8,128)(2,1)} async-done(((bf16[128,896]{1,0:T(8,128)(2,1)}), bf16[1024,896]{1,0:T(8,128)(2,1)}) %all-gather.4.cloned.1.call-update) | async-done | bytes 1835024 | tf_op jit(solution)/shard_map/all_gather | solution.py:515
  63.0 21.8 %collective-permute-done.1 = bf16[2,256,1024]{2,1,0:T(8,128)(2,1)S(1)} collective-permute-done((bf16[2,256,1024]{2,1,0:T(8,128)(2,1)S(1)}, bf16[2,256,1024]{2,1,0:T(8,128)(2,1)S(1)}, u32[]{:S(2)}, u32[]{:S(2)}) %collective-permute-start.1) | collective-permute-done | bytes 1048608 | tf_op jit(solution)/shard_map/ppermute | solution.py:418
  90.7 2.2 fusion.20
  95.4 19.3 %collective-permute-done.4 = bf16[2,256,1024]{2,1,0:T(8,128)(2,1)} collective-permute-done((bf16[2,256,1024]{2,1,0:T(8,128)(2,1)S(1)}, bf16[2,256,1024]{2,1,0:T(8,128)(2,1)}, u32[]{:S(2)}, u32[]{:S(2)}) %collective-permute-start.4) | collective-permute-done | bytes 1048608 | tf_op jit(solution)/shard_map/ppermute | solution.py:418
  115.7 3.5 all-to-all-start
  119.5 6.7 %fusion.14.q_ref.k_ref.v_ref = f32[2,1024,512]{2,1,0:T(8,128)} fusion(f32[1024]{0:T(1024)S(1)} %get-tuple-element.121, bf16[2,1024,1024]{2,1,0:T(8,128)(2,1)} %copy-done.2, f32[2,1024]{1,0:T(2,128)S(1)} %add_rsqrt_fusion, bf16[1024,896]{1,0:T(8,128)(2,1)S(1)} %copy-done.17), kind=kOutput, calls=%fused_computation.51 | convolution fusion | flops 2155872256 | bytes 9449472 | tf_op jit(solution)/shard_map/dot_general | solution.py:457
  126.2 17.2 %attend.1 = (bf16[2,1024,256]{2,1,0:T(8,128)(2,1)}, bf16[2,1024,128]{2,1,0:T(8,128)(2,1)}, bf16[2,1024,256]{2,1,0:T(8,128)(2,1)}) custom-call(f32[2,1024,512]{2,1,0:T(8,128)} %fusion.14.q_ref.k_ref.v_ref, f32[2,1024,512]{2,1,0:T(8,128)} %fusion.14.q_ref.k_ref.v_ref, f32[2,1024,512]{2,1,0:T(8,128)} %fusion.14.q_ref.k_ref.v_ref, ...), custom_call_target="tpu_custom_call" | custom-call | flops 2147483648 | bytes 8388608 | tf_op jit(solution)/shard_map/attend/pallas_call | solution.py:270
  143.4 2.7 convolution_convert_fusion.3
  146.2 3.7 pad_maximum_fusion.1.cot_ref
  150.7 2.2 collective-permute-done.7
  153.4 1.9 collective-permute-start.8
  155.2 23.6 %collective-permute-done.8 = bf16[2,256,1024]{2,1,0:T(8,128)(2,1)S(1)} collective-permute-done((bf16[2,256,1024]{2,1,0:T(8,128)(2,1)S(1)}, bf16[2,256,1024]{2,1,0:T(8,128)(2,1)S(1)}, u32[]{:S(2)}, u32[]{:S(2)}) %collective-permute-start.8) | collective-permute-done | bytes 1048608 | tf_op jit(solution)/shard_map/ppermute | solution.py:418
  179.9 1.6 collective-permute-start.11
  181.5 23.0 %collective-permute-done.11 = bf16[2,256,1024]{2,1,0:T(8,128)(2,1)S(1)} collective-permute-done((bf16[2,256,1024]{2,1,0:T(8,128)(2,1)S(1)}, bf16[2,256,1024]{2,1,0:T(8,128)(2,1)S(1)}, u32[]{:S(2)}, u32[]{:S(2)}) %collective-permute-start.11) | collective-permute-done | bytes 1048608 | tf_op jit(solution)/shard_map/ppermute | solution.py:418
  204.5 1.6 pad_maximum_fusion.5.two_ref
  209.7 1.8 slice.176
  215.0 3.2 pad_maximum_fusion.3
  218.3 22.1 %ffn.2 = (bf16[2048,1152]{1,0:T(8,128)(2,1)}, bf16[2048,1152]{1,0:T(8,128)(2,1)}, bf16[2048,1152]{1,0:T(8,128)(2,1)}, bf16[1024,1024]{1,0:T(8,128)(2,1)}, bf16[1024,1024]{1,0:T(8,128)(2,1)}) custom-call(bf16[1024,1024]{1,0:T(8,128)(2,1)} %pad_maximum_fusion.5.two_ref, bf16[2048,1024]{1,0:T(8,128)(2,1)} %pad_maximum_fusion.1.cot_ref, ...), custom_call_target="tpu_custom_call" | custom-call | flops 14495514624 | bytes 22544384 | tf_op jit(solution)/shard_map/ffn/pallas_call | solution.py:373
  240.4 22.7 %ffn.3 = (bf16[2048,1152]{1,0:T(8,128)(2,1)}, bf16[2048,1152]{1,0:T(8,128)(2,1)}, bf16[2048,1152]{1,0:T(8,128)(2,1)}, bf16[1024,1024]{1,0:T(8,128)(2,1)}, bf16[1024,1024]{1,0:T(8,128)(2,1)}) custom-call(bf16[1024,1024]{1,0:T(8,128)(2,1)} %pad_maximum_fusion.6.two_ref, ...), custom_call_target="tpu_custom_call", output_to_operand_aliasing={{0}: (5, {}), {1}: (6, {}), {2}: (7, {})} | custom-call | flops 14495514624 | bytes 22544384 | tf_op jit(solution)/shard_map/ffn/pallas_call | solution.py:373
  263.1 8.5 %convolution_convert_fusion = bf16[1152,1024]{1,0:T(8,128)(2,1)S(1)} fusion(bf16[2048,1152]{1,0:T(8,128)(2,1)} %get-tuple-element.69, bf16[2048,1024]{1,0:T(8,128)(2,1)} %pad_maximum_fusion.1.cot_ref), kind=kOutput, calls=%fused_computation.12 | convolution fusion | flops 4833017856 | bytes 11272192 | tf_op jit(solution)/shard_map/dot_general | solution.py:467
  273.7 6.1 %convolution_convert_fusion.2 = bf16[1024,1152]{1,0:T(8,128)(2,1)S(1)} fusion(bf16[2048,1152]{1,0:T(8,128)(2,1)S(1)} %copy-done.31, bf16[512,1024]{1,0:T(8,128)(2,1)S(1)} %bitcast.208, bf16[512,1024]{1,0:T(8,128)(2,1)S(1)} %bitcast.202, bf16[512,1024]{1,0:T(8,128)(2,1)S(1)} %bitcast.205, bf16[512,1024]{1,0:T(8,128)(2,1)S(1)} %bitcast.169), kind=kOutput, calls=%fused_computation.14 | convolution fusion | flops 4849795072 | bytes 11272192 | tf_op jit(solution)/shard_map/dot_general | solution.py:467
  279.8 6.1 %convolution_convert_fusion.1 = bf16[1024,1152]{1,0:T(8,128)(2,1)S(1)} fusion(bf16[2048,1152]{1,0:T(8,128)(2,1)S(1)} %bitcast.218, bf16[512,1024]{1,0:T(8,128)(2,1)S(1)} %bitcast.209, bf16[512,1024]{1,0:T(8,128)(2,1)S(1)} %bitcast.203, bf16[512,1024]{1,0:T(8,128)(2,1)S(1)} %bitcast.206, bf16[512,1024]{1,0:T(8,128)(2,1)S(1)} %bitcast.170), kind=kOutput, calls=%fused_computation.13 | convolution fusion | flops 4849795072 | bytes 11272192 | tf_op jit(solution)/shard_map/dot_general | solution.py:467
  286.0 3.4 pad_maximum_fusion
  289.5 1.9 fusion.28
  292.1 1.9 collective-permute-done.13
  295.9 23.9 %collective-permute-done.14 = bf16[2,256,1024]{2,1,0:T(8,128)(2,1)S(1)} collective-permute-done((bf16[2,256,1024]{2,1,0:T(8,128)(2,1)S(1)}, bf16[2,256,1024]{2,1,0:T(8,128)(2,1)S(1)}, u32[]{:S(2)}, u32[]{:S(2)}) %collective-permute-start.14) | collective-permute-done | bytes 1048608 | tf_op jit(solution)/shard_map/ppermute | solution.py:418
  322.3 2.2 constant_dynamic-update-slice_fusion.3
  325.9 23.1 %collective-permute-done.16 = bf16[2,256,1024]{2,1,0:T(8,128)(2,1)S(1)} collective-permute-done((bf16[2,256,1024]{2,1,0:T(8,128)(2,1)S(1)}, bf16[2,256,1024]{2,1,0:T(8,128)(2,1)S(1)}, u32[]{:S(2)}, u32[]{:S(2)}) %collective-permute-start.16) | collective-permute-done | bytes 1048608 | tf_op jit(solution)/shard_map/ppermute | solution.py:418
  349.1 3.9 convert_multiply_fusion
  357.5 2.0 copy-done.5
  361.6 4.1 all-to-all-start.1
  365.8 3.0 fusion.8
  368.8 1.9 collective-permute-start.20
  370.7 4.5 convolution_convert_fusion.4
  375.2 26.3 %attend_back.1 = (bf16[2,1024,512]{2,1,0:T(8,128)(2,1)}, f32[8,128]{1,0:T(8,128)}) custom-call(bf16[2,1024,256]{2,1,0:T(8,128)(2,1)} %get-tuple-element.47.low_q_ref, bf16[2,1024,128]{2,1,0:T(8,128)(2,1)} %get-tuple-element.48.low_k_ref, f32[2,1024,512]{2,1,0:T(8,128)} %fusion.14.q_ref.k_ref.v_ref, f32[2,1024,512]{2,1,0:T(8,128)} %fusion.14.q_ref.k_ref.v_ref, ...), custom_call_target="tpu_custom_call" | custom-call | flops 5368709120 | bytes 12582912 | tf_op jit(solution)/shard_map/attend_back/pallas_call | solution.py:305
  402.5 3.7 fusion.11
  406.2 8.1 %fusion.1 = (bf16[1024]{0:T(1024)(128)(2,1)S(1)}, bf16[2048,1024]{1,0:T(8,128)(2,1)}) fusion(f32[2,1024,1024]{2,1,0:T(8,128)} %convert_multiply_fusion, bf16[2048,512]{1,0:T(8,128)(2,1)S(1)} %bitcast.164, bf16[1024,896]{1,0:T(8,128)(2,1)S(1)} %copy-done.18), kind=kOutput, calls=%fused_computation.4 | convolution fusion | flops 2153774080 | bytes 15730688 | tf_op jit(solution)/shard_map/dot_general | solution.py:461
  416.3 5.7 %bitcast_convert_fusion = bf16[1024,512]{1,0:T(8,128)(2,1)} fusion(bf16[2,1024,512]{2,1,0:T(8,128)(2,1)S(1)} %copy-done.11, f32[1024]{0:T(1024)S(1)} %get-tuple-element.121, bf16[2,1024,1024]{2,1,0:T(8,128)(2,1)} %copy-done.2, f32[2,1024]{1,0:T(2,128)S(1)} %add_rsqrt_fusion), kind=kOutput, calls=%fused_computation.41 | convolution fusion | flops 2156396544 | bytes 7352320 | tf_op jit(solution)/shard_map/dot_general | solution.py:467
  422.0 2.9 pad_maximum_fusion.7
  424.9 2.7 constant_dynamic-slice_fusion.2
  428.1 2.1 collective-permute-done.22
  430.3 2.6 add_convert_fusion
  433.0 1.9 collective-permute-start.25
  434.9 24.3 %collective-permute-done.23 = bf16[2,256,1024]{2,1,0:T(8,128)(2,1)} collective-permute-done((bf16[2,256,1024]{2,1,0:T(8,128)(2,1)}, bf16[2,256,1024]{2,1,0:T(8,128)(2,1)}, u32[]{:S(2)}, u32[]{:S(2)}) %collective-permute-start.23) | collective-permute-done | bytes 1048608 | tf_op jit(solution)/shard_map/ppermute | solution.py:418
  459.2 2.7 fusion.3
  462.0 4.1 fusion.6
  466.0 11.3 %collective-permute-done.25 = bf16[128,3456]{1,0:T(8,128)(2,1)} collective-permute-done((bf16[128,3456]{1,0:T(8,128)(2,1)}, bf16[128,3456]{1,0:T(8,128)(2,1)}, u32[]{:S(2)}, u32[]{:S(2)}) %collective-permute-start.25) | collective-permute-done | bytes 884768 | tf_op jit(solution)/shard_map/ppermute | solution.py:418
  477.4 14.5 %reduce-scatter.3.cloned.1.call-done = bf16[144,896]{1,0:T(8,128)(2,1)} async-done(((bf16[1152,896]{1,0:T(8,128)(2,1)}), bf16[144,896]{1,0:T(8,128)(2,1)}) %reduce-scatter.3.cloned.1.call-update) | async-done | bytes 258064 | tf_op jit(solution)/shard_map/reduce_scatter | solution.py:623
  491.9 10.1 %all-gather = bf16[576,896]{1,0:T(8,128)(2,1)S(1)} all-gather(bf16[144,896]{1,0:T(8,128)(2,1)} %reduce-scatter.3.cloned.1.call-done), channel_id=2, replica_groups=mesh['fsdp'=8,'seq'=4] {'seq'}, dimensions={0}, use_global_device_ids=true | all-gather | bytes 1290240 | tf_op jit(solution)/shard_map/all_gather | solution.py:631
  509.8 4.8 maximum_convert_fusion
  514.6 6.3 %rev.6 = f32[2,2,1,128,3456]{4,3,1,0,2:T(8,128)} reverse(f32[2,2,1,128,3456]{4,3,1,0,2:T(8,128)} %bitcast.145), dimensions={1} | reverse | bytes 14155776 | tf_op jit(solution)/shard_map/rev | solution.py:629
  521.0 8.6 %bitcast_select_fusion.1 = f32[1,2,2,128,3456]{4,3,2,1,0:T(8,128)} fusion(f32[1,2,2,128,3456]{4,3,2,1,0:T(8,128)} %bitcast.147, pred[]{:T(512)S(6)} %gt.7, f32[2,2,1,128,3456]{4,3,1,0,2:T(8,128)} %bitcast.146), kind=kLoop, calls=%fused_computation.9 | loop fusion | flops 1769472 | bytes 21233664 | tf_op jit(solution)/shard_map/jit(_where)/select_n | solution.py:630
  529.6 6.4 %rev.7 = f32[1,2,2,128,3456]{4,3,2,1,0:T(8,128)} reverse(f32[1,2,2,128,3456]{4,3,2,1,0:T(8,128)} %bitcast_select_fusion.1), dimensions={1} | reverse | bytes 14155776 | tf_op jit(solution)/shard_map/rev | solution.py:629
  536.0 6.5 %fusion.2 = f32[4,128,3456]{2,1,0:T(8,128)S(1)} fusion(f32[2,2,1,128,3456]{4,3,1,0,2:T(8,128)} %rev.6, f32[1,2,2,128,3456]{4,3,2,1,0:T(8,128)} %rev.7, pred[]{:T(512)S(6)} %gt.7, pred[]{:T(512)S(6)} %gt.6, bf16[1,128,3456]{2,1,0:T(8,128)(2,1)} %bitcast.63, bf16[1,128,3456]{2,1,0:T(8,128)(2,1)} %bitcast.62, bf16[1,128,3456]{2,1,0:T(8,128)(2,1)} %bitcast.61, ...), kind=kLoop, calls=%fused_computation.8 | loop fusion | flops 10616832 | bytes 24772610 | tf_op jit(solution)/shard_map/jit(_where)/select_n | solution.py:630
  542.5 2.6 fusion.24
  547.5 2.0 copy.134
  549.6 1.6 copy.135
  551.2 3.0 copy.143
  554.2 2.0 copy.136
  556.2 1.6 copy.137
  557.9 3.2 copy.144
  (205 shorter events, 59.4 us)
Async XLA Ops:
  7.2 13.3 %copy-start = (bf16[576,1024]{1,0:T(8,128)(2,1)S(1)}, bf16[576,1024]{1,0:T(8,128)(2,1)}, u32[]{:S(2)}) copy-start(bf16[576,1024]{1,0:T(8,128)(2,1)} %param.21) | copy-start | bytes 3538948
  7.2 54.2 %all-gather.4.cloned.1.call-start = ((), (), s32[]{:S(2)}) async-start(), calls=%async_computation.4 | async-start | bytes 2064384 | tf_op jit(solution)/shard_map/all_gather | solution.py:515
  12.1 197.6 %all-gather.6.cloned.1.call-start = ((), (), s32[]{:S(2)}) async-start(), calls=%async_computation.5 | async-start | bytes 7962624 | tf_op jit(solution)/shard_map/all_gather | solution.py:531
  13.9 47.5 %copy-start.6 = (bf16[2,256,1024]{2,1,0:T(8,128)(2,1)S(1)}, bf16[2,256,1024]{2,1,0:T(8,128)(2,1)}, u32[]{:S(2)}) copy-start(bf16[2,256,1024]{2,1,0:T(8,128)(2,1)} %param.14) | copy-start | bytes 3145732
  13.9 70.9 %copy-start.30 = (bf16[2,64]{1,0:T(2,128)(2,1)S(1)}, bf16[2,64]{1,0:T(2,128)(2,1)}, u32[]{:S(2)}) copy-start(bf16[2,64]{1,0:T(2,128)(2,1)} %param.24) | copy-start | bytes 772
  61.4 23.3 %collective-permute-start.1 = (bf16[2,256,1024]{2,1,0:T(8,128)(2,1)S(1)}, bf16[2,256,1024]{2,1,0:T(8,128)(2,1)S(1)}, u32[]{:S(2)}, u32[]{:S(2)}) collective-permute-start(bf16[2,256,1024]{2,1,0:T(8,128)(2,1)S(1)} %copy-done.6), channel_id=1, source_target_pairs={{0,2},{1,3},{2,0},{3,1},{4,6},{5,7},{6,4},{7,5},{8,10},{9,11},{10,... | collective-permute-start | bytes 3145736 | tf_op jit(solution)/shard_map/ppermute | solution.py:418
  62.9 23.1 %collective-permute-start = (bf16[2,256,1024]{2,1,0:T(8,128)(2,1)S(1)}, bf16[2,256,1024]{2,1,0:T(8,128)(2,1)}, u32[]{:S(2)}, u32[]{:S(2)}) collective-permute-start(bf16[2,256,1024]{2,1,0:T(8,128)(2,1)S(1)} %copy-done.6), channel_id=1, source_target_pairs={{0,1},{1,0},{2,3},{3,2},{4,5},{5,4},{6,7},{7,6},{8,9},{9,8},{10,11... | collective-permute-start | bytes 3145736 | tf_op jit(solution)/shard_map/ppermute | solution.py:418
  84.7 2.9 collective-permute-start.2
  86.0 2.9 copy-start.15
  88.9 6.4 %copy-start.2 = (bf16[2,1024,1024]{2,1,0:T(8,128)(2,1)}, bf16[2,1024,1024]{2,1,0:T(8,128)(2,1)S(1)}, u32[]{:S(2)}) copy-start(bf16[2,1024,1024]{2,1,0:T(8,128)(2,1)S(1)} %constant_dynamic-update-slice_fusion.4) | copy-start | bytes 12582916
  88.9 25.7 %collective-permute-start.4 = (bf16[2,256,1024]{2,1,0:T(8,128)(2,1)S(1)}, bf16[2,256,1024]{2,1,0:T(8,128)(2,1)}, u32[]{:S(2)}, u32[]{:S(2)}) collective-permute-start(bf16[2,256,1024]{2,1,0:T(8,128)(2,1)S(1)} %copy-done.15), channel_id=1, source_target_pairs={{0,2},{1,3},{2,0},{3,1},{4,6},{5,7},{6,4},{7,5},{8,10},{9,11},{10,... | collective-permute-start | bytes 3145736 | tf_op jit(solution)/shard_map/ppermute | solution.py:418
  92.9 21.8 %slice-start.1 = ((bf16[1024,896]{1,0:T(8,128)(2,1)}), bf16[1024,256]{1,0:T(8,128)(2,1)S(1)}, s32[]{:S(2)}) async-start(bf16[1024,896]{1,0:T(8,128)(2,1)} %all-gather.4.cloned.1.call-done), calls=%async_computation.9 | async-start | bytes 1048576 | tf_op jit(solution)/shard_map/slice | solution.py:518
  94.2 25.0 %copy-start.17 = (bf16[1024,896]{1,0:T(8,128)(2,1)S(1)}, bf16[1024,896]{1,0:T(8,128)(2,1)}, u32[]{:S(2)}) copy-start(bf16[1024,896]{1,0:T(8,128)(2,1)} %all-gather.4.cloned.1.call-done) | copy-start | bytes 5505028
  94.2 51.9 %collective-permute-start.3 = (bf16[2,256,1024]{2,1,0:T(8,128)(2,1)S(1)}, bf16[2,256,1024]{2,1,0:T(8,128)(2,1)}, u32[]{:S(2)}, u32[]{:S(2)}) collective-permute-start(bf16[2,256,1024]{2,1,0:T(8,128)(2,1)S(1)} %copy-done.15), channel_id=1, source_target_pairs={{0,1},{1,0},{2,3},{3,2},{4,5},{5,4},{6,7},{7,6},{8,9},{9,8},{10,11... | collective-permute-start | bytes 3145736 | tf_op jit(solution)/shard_map/ppermute | solution.py:418
  114.7 31.5 %collective-permute-start.5 = (bf16[2,256,1024]{2,1,0:T(8,128)(2,1)}, bf16[2,256,1024]{2,1,0:T(8,128)(2,1)}, u32[]{:S(2)}, u32[]{:S(2)}) collective-permute-start(bf16[2,256,1024]{2,1,0:T(8,128)(2,1)} %collective-permute-done.4), channel_id=1, source_target_pairs={{0,1},{1,0},{2,3},{3,2},{4,5},{5,4},{6,7},{7,6},{8,9},{9,8},{10,11... | collective-permute-start | bytes 3145736 | tf_op jit(solution)/shard_map/ppermute | solution.py:418
  115.7 27.8 %all-to-all-start = ((bf16[4,256,256]{1,2,0:T(8,128)(2,1)}), bf16[4,256,256]{1,2,0:T(8,128)(2,1)S(1)}, u32[]{:S(2)}, u32[]{:S(2)}) async-start(bf16[4,256,256]{1,2,0:T(8,128)(2,1)} %copy.118), calls=%async_computation | async-start | bytes 1048576 | tf_op jit(solution)/shard_map/all_to_all | solution.py:542
  119.1 313.8 %reduce-scatter.5.cloned.1.call-start = ((), (), s32[]{:S(2)}) async-start(), calls=%async_computation.7 | async-start | bytes 7962624 | tf_op jit(solution)/shard_map/reduce_scatter | solution.py:588
  143.4 2.7 copy-start.19
  149.9 29.0 %copy-start.7 = (bf16[2,256,1024]{2,1,0:T(8,128)(2,1)S(1)}, bf16[2,256,1024]{2,1,0:T(8,128)(2,1)}, u32[]{:S(2)}) copy-start(bf16[2,256,1024]{2,1,0:T(8,128)(2,1)} %param.14) | copy-start | bytes 3145732
  150.0 2.9 collective-permute-start.7
  150.7 4.5 collective-permute-start.6
  153.4 25.5 %collective-permute-start.8 = (bf16[2,256,1024]{2,1,0:T(8,128)(2,1)S(1)}, bf16[2,256,1024]{2,1,0:T(8,128)(2,1)S(1)}, u32[]{:S(2)}, u32[]{:S(2)}) collective-permute-start(bf16[2,256,1024]{2,1,0:T(8,128)(2,1)S(1)} %add_convert_fusion.1), channel_id=1, source_target_pairs={{0,2},{1,3},{2,0},{3,1},{4,6},{5,7},{6,4},{7,5},{8,10},{9,11},{10,... | collective-permute-start | bytes 3145736 | tf_op jit(solution)/shard_map/ppermute | solution.py:418
  179.8 24.7 %copy-start.13 = (bf16[2,256,1024]{2,1,0:T(8,128)(2,1)}, bf16[2,256,1024]{2,1,0:T(8,128)(2,1)S(1)}, u32[]{:S(2)}) copy-start(bf16[2,256,1024]{2,1,0:T(8,128)(2,1)S(1)} %multiply_convert_fusion.1) | copy-start | bytes 3145732
  179.9 24.6 %collective-permute-start.11 = (bf16[2,256,1024]{2,1,0:T(8,128)(2,1)S(1)}, bf16[2,256,1024]{2,1,0:T(8,128)(2,1)S(1)}, u32[]{:S(2)}, u32[]{:S(2)}) collective-permute-start(bf16[2,256,1024]{2,1,0:T(8,128)(2,1)S(1)} %multiply_convert_fusion.1), channel_id=1, source_target_pairs={{0,2},{1,3},{2,0},{3,1},{4,6},{5,7},{6,4},{7,5},{8,10},{9,11},{10,... | collective-permute-start | bytes 3145736 | tf_op jit(solution)/shard_map/ppermute | solution.py:418
  181.5 23.0 %collective-permute-start.9 = (bf16[2,256,1024]{2,1,0:T(8,128)(2,1)S(1)}, bf16[2,256,1024]{2,1,0:T(8,128)(2,1)S(1)}, u32[]{:S(2)}, u32[]{:S(2)}) collective-permute-start(bf16[2,256,1024]{2,1,0:T(8,128)(2,1)S(1)} %multiply_convert_fusion.1), channel_id=1, source_target_pairs={{0,1},{1,0},{2,3},{3,2},{4,5},{5,4},{6,7},{7,6},{8,9},{9,8},{10,11... | collective-permute-start | bytes 3145736 | tf_op jit(solution)/shard_map/ppermute | solution.py:418
  204.5 2.7 copy-start.23
  204.5 2.7 collective-permute-start.12
  204.5 2.7 copy-start.25
  263.1 8.7 %copy-start.31 = (bf16[2048,1152]{1,0:T(8,128)(2,1)S(1)}, bf16[2048,1152]{1,0:T(8,128)(2,1)}, u32[]{:S(2)}) copy-start(bf16[2048,1152]{1,0:T(8,128)(2,1)} %get-tuple-element.67) | copy-start | bytes 14155780
  271.5 1.8 copy-start.26
  271.5 2.1 copy-start.28
  271.6 8.2 %slice-start.2 = ((s8[4718592]{0:T(1024)(128)(4,1)}), s8[4194304]{0:T(1024)(128)(4,1)S(1)}, s32[]{:S(2)}) async-start(s8[4718592]{0:T(1024)(128)(4,1)} %bitcast.217), calls=%async_computation.10 | async-start | bytes 8388608
  273.7 6.1 %slice-start.3 = ((s8[4718592]{0:T(1024)(128)(4,1)}), s8[524288]{0:T(1024)(128)(4,1)S(1)}, s32[]{:S(2)}) async-start(s8[4718592]{0:T(1024)(128)(4,1)} %bitcast.217), calls=%async_computation.11 | async-start | bytes 1048576
  289.4 2.2 copy-start.9
  291.3 2.7 collective-permute-start.13
  291.9 4.0 collective-permute-start.10
  294.5 25.3 %collective-permute-start.14 = (bf16[2,256,1024]{2,1,0:T(8,128)(2,1)S(1)}, bf16[2,256,1024]{2,1,0:T(8,128)(2,1)S(1)}, u32[]{:S(2)}, u32[]{:S(2)}) collective-permute-start(bf16[2,256,1024]{2,1,0:T(8,128)(2,1)S(1)} %fusion.12), channel_id=1, source_target_pairs={{0,2},{1,3},{2,0},{3,1},{4,6},{5,7},{6,4},{7,5},{8,10},{9,11},{10,... | collective-permute-start | bytes 3145736 | tf_op jit(solution)/shard_map/ppermute | solution.py:418
  322.3 26.7 %copy-start.3 = (bf16[2,1024,1024]{2,1,0:T(8,128)(2,1)S(1)}, bf16[2,1024,1024]{2,1,0:T(8,128)(2,1)}, u32[]{:S(2)}) copy-start(bf16[2,1024,1024]{2,1,0:T(8,128)(2,1)} %copy-done.2) | copy-start | bytes 12582916
  324.6 28.4 %copy-start.21 = (bf16[1024,1024]{1,0:T(8,128)(2,1)S(1)}, bf16[1024,1024]{1,0:T(8,128)(2,1)}, u32[]{:S(2)}) copy-start(bf16[1024,1024]{1,0:T(8,128)(2,1)} %get-tuple-element.63) | copy-start | bytes 6291460
  324.6 24.5 %collective-permute-start.16 = (bf16[2,256,1024]{2,1,0:T(8,128)(2,1)S(1)}, bf16[2,256,1024]{2,1,0:T(8,128)(2,1)S(1)}, u32[]{:S(2)}, u32[]{:S(2)}) collective-permute-start(bf16[2,256,1024]{2,1,0:T(8,128)(2,1)S(1)} %get-tuple-element.127), channel_id=1, source_target_pairs={{0,2},{1,3},{2,0},{3,1},{4,6},{5,7},{6,4},{7,5},{8,10},{9,11},{10,... | collective-permute-start | bytes 3145736 | tf_op jit(solution)/shard_map/ppermute | solution.py:418
  325.9 27.1 %collective-permute-start.15 = (bf16[2,256,1024]{2,1,0:T(8,128)(2,1)S(1)}, bf16[2,256,1024]{2,1,0:T(8,128)(2,1)S(1)}, u32[]{:S(2)}, u32[]{:S(2)}) collective-permute-start(bf16[2,256,1024]{2,1,0:T(8,128)(2,1)S(1)} %get-tuple-element.127), channel_id=1, source_target_pairs={{0,1},{1,0},{2,3},{3,2},{4,5},{5,4},{6,7},{7,6},{8,9},{9,8},{10,11... | collective-permute-start | bytes 3145736 | tf_op jit(solution)/shard_map/ppermute | solution.py:418
  349.0 3.9 collective-permute-start.17
  353.0 2.4 copy-start.20
  354.5 11.3 %collective-permute-start.19 = (bf16[2,256,1024]{2,1,0:T(8,128)(2,1)}, bf16[2,256,1024]{2,1,0:T(8,128)(2,1)}, u32[]{:S(2)}, u32[]{:S(2)}) collective-permute-start(bf16[2,256,1024]{2,1,0:T(8,128)(2,1)} %bitcast.35), channel_id=1, source_target_pairs={{0,1},{1,0},{2,3},{3,2},{4,5},{5,4},{6,7},{7,6},{8,9},{9,8},{10,11... | collective-permute-start | bytes 3145736 | tf_op jit(solution)/shard_map/ppermute | solution.py:418
  355.4 4.0 copy-start.12
  356.9 45.6 %collective-permute-start.18 = (bf16[2,256,1024]{2,1,0:T(8,128)(2,1)}, bf16[2,256,1024]{2,1,0:T(8,128)(2,1)}, u32[]{:S(2)}, u32[]{:S(2)}) collective-permute-start(bf16[2,256,1024]{2,1,0:T(8,128)(2,1)} %bitcast.33), channel_id=1, source_target_pairs={{0,1},{1,0},{2,3},{3,2},{4,5},{5,4},{6,7},{7,6},{8,9},{9,8},{10,11... | collective-permute-start | bytes 3145736 | tf_op jit(solution)/shard_map/ppermute | solution.py:418
  357.5 2.0 copy-start.5
  361.6 60.4 %all-to-all-start.1 = ((bf16[256,4,256]{2,0,1:T(8,128)(2,1)}), bf16[256,4,256]{2,0,1:T(8,128)(2,1)}, u32[]{:S(2)}, u32[]{:S(2)}) async-start(bf16[256,4,256]{2,0,1:T(8,128)(2,1)} %bitcast.183), calls=%async_computation.1 | async-start | bytes 1048576 | tf_op jit(solution)/shard_map/all_to_all | solution.py:596
  365.7 126.1 %reduce-scatter.3.cloned.1.call-start = ((), (), s32[]{:S(2)}) async-start(), calls=%async_computation.6 | async-start | bytes 2322432 | tf_op jit(solution)/shard_map/reduce_scatter | solution.py:623
  368.8 33.7 %collective-permute-start.20 = (bf16[2,256,1024]{2,1,0:T(8,128)(2,1)}, bf16[2,256,1024]{2,1,0:T(8,128)(2,1)}, u32[]{:S(2)}, u32[]{:S(2)}) collective-permute-start(bf16[2,256,1024]{2,1,0:T(8,128)(2,1)} %fusion.8), channel_id=1, source_target_pairs={{0,2},{1,3},{2,0},{3,1},{4,6},{5,7},{6,4},{7,5},{8,10},{9,11},{10,... | collective-permute-start | bytes 3145736 | tf_op jit(solution)/shard_map/ppermute | solution.py:418
  402.5 3.8 copy-start.10
  402.5 3.8 copy-start.18
  406.2 10.1 %copy-start.11 = (bf16[2,1024,512]{2,1,0:T(8,128)(2,1)S(1)}, bf16[2,1024,512]{2,1,0:T(8,128)(2,1)}, u32[]{:S(2)}) copy-start(bf16[2,1024,512]{2,1,0:T(8,128)(2,1)} %get-tuple-element.65) | copy-start | bytes 6291460
  427.6 2.7 collective-permute-start.22
  427.6 34.3 %copy-start.8 = (f32[2,256,1024]{2,1,0:T(8,128)S(1)}, f32[2,256,1024]{2,1,0:T(8,128)}, u32[]{:S(2)}) copy-start(f32[2,256,1024]{2,1,0:T(8,128)} %get-tuple-element.128) | copy-start | bytes 6291460
  427.6 7.3 %collective-permute-start.21 = (bf16[2,256,1024]{2,1,0:T(8,128)(2,1)}, bf16[2,256,1024]{2,1,0:T(8,128)(2,1)}, u32[]{:S(2)}, u32[]{:S(2)}) collective-permute-start(bf16[2,256,1024]{2,1,0:T(8,128)(2,1)} %get-tuple-element.135), channel_id=1, source_target_pairs={{0,1},{1,0},{2,3},{3,2},{4,5},{5,4},{6,7},{7,6},{8,9},{9,8},{10,11... | collective-permute-start | bytes 3145736 | tf_op jit(solution)/shard_map/ppermute | solution.py:418
  432.9 26.3 %collective-permute-start.23 = (bf16[2,256,1024]{2,1,0:T(8,128)(2,1)}, bf16[2,256,1024]{2,1,0:T(8,128)(2,1)}, u32[]{:S(2)}, u32[]{:S(2)}) collective-permute-start(bf16[2,256,1024]{2,1,0:T(8,128)(2,1)} %add_convert_fusion), channel_id=1, source_target_pairs={{0,2},{1,3},{2,0},{3,1},{4,6},{5,7},{6,4},{7,5},{8,10},{9,11},{10,... | collective-permute-start | bytes 3145736 | tf_op jit(solution)/shard_map/ppermute | solution.py:418
  433.0 44.4 %collective-permute-start.25 = (bf16[128,3456]{1,0:T(8,128)(2,1)}, bf16[128,3456]{1,0:T(8,128)(2,1)}, u32[]{:S(2)}, u32[]{:S(2)}) collective-permute-start(bf16[128,3456]{1,0:T(8,128)(2,1)} %reduce-scatter.5.cloned.1.call-done), channel_id=1, source_target_pairs={{0,2},{1,3},{2,0},{3,1},{4,6},{5,7},{6,4},{7,5},{8,10},{9,11},{10,... | collective-permute-start | bytes 2654216 | tf_op jit(solution)/shard_map/ppermute | solution.py:418
  466.0 43.8 %collective-permute-start.24 = (bf16[128,3456]{1,0:T(8,128)(2,1)}, bf16[128,3456]{1,0:T(8,128)(2,1)}, u32[]{:S(2)}, u32[]{:S(2)}) collective-permute-start(bf16[128,3456]{1,0:T(8,128)(2,1)} %reduce-scatter.5.cloned.1.call-done), channel_id=1, source_target_pairs={{0,1},{1,0},{2,3},{3,2},{4,5},{5,4},{6,7},{7,6},{8,9},{9,8},{10,11... | collective-permute-start | bytes 2654216 | tf_op jit(solution)/shard_map/ppermute | solution.py:418
  477.4 32.4 %collective-permute-start.26 = (bf16[128,3456]{1,0:T(8,128)(2,1)}, bf16[128,3456]{1,0:T(8,128)(2,1)}, u32[]{:S(2)}, u32[]{:S(2)}) collective-permute-start(bf16[128,3456]{1,0:T(8,128)(2,1)} %collective-permute-done.25), channel_id=1, source_target_pairs={{0,1},{1,0},{2,3},{3,2},{4,5},{5,4},{6,7},{7,6},{8,9},{9,8},{10,11... | collective-permute-start | bytes 2654216 | tf_op jit(solution)/shard_map/ppermute | solution.py:418
  542.5 4.3 copy-start.4
  557.9 3.2 slice-start
  557.9 3.2 copy-start.22
  557.9 4.8 copy-start.1
  (5 other events, 5.7 us)
Sparse Core Ops, SparseCore 0:
  12.2 49.0 all-gather.3
  64.1 106.9 all-gather.5
  289.6 129.3 reduce-scatter.4
  425.0 66.7 reduce-scatter.2

commit v3 on v2

--- a/solution.py
+++ b/solution.py
@@ -414,28 +414,71 @@
     return [1 << i for i in range(count.bit_length() - 1)]
 
 
-def swap(values, bit, count):
-    return lax.ppermute(values, "seq", [(i, i ^ bit) for i in range(count)])
-
-
-def gather_blocks(block, count):
+def swap(values, bit, count, axis="seq"):
+    total = lax.axis_size(axis)
+    return lax.ppermute(values, axis, [(i, i ^ bit) for i in range(total)])
+
+
+def after(value, *others):
+    return lax.optimization_barrier((value, others))[0]
+
+
+def gather_blocks(block, count, hold=None):
     blocks = {0: block}
     for bit in reversed(bits_of(count)):
         for at in list(blocks):
-            blocks[at | bit] = swap(blocks[at], bit, count)
+            sent = blocks[at] if at == 0 or hold is None else after(blocks[at], *hold)
+            blocks[at | bit] = swap(sent, bit, count)
     return blocks
 
 
-def scatter_blocks(blocks, count):
+def scatter_sums(blocks, count):
     blocks = dict(blocks)
-    for bit in bits_of(count):
+    bits = bits_of(count)
+    for bit in bits[:-1]:
         kept = {}
         for at in blocks:
             if not at & bit:
                 arrived = swap(blocks[at | bit].astype(jnp.bfloat16), bit, count)
                 kept[at] = blocks[at].astype(jnp.float32) + arrived.astype(jnp.float32)
         blocks = kept
-    return blocks[0]
+    return blocks[0], blocks[bits[-1]].astype(jnp.bfloat16)
+
+
+def last_swap(sent, count):
+    return swap(sent, bits_of(count)[-1], count).astype(jnp.float32)
+
+
+def scatter_blocks(blocks, count):
+    kept, sent = scatter_sums(blocks, count)
+    return kept + last_swap(sent, count)
+
+
+def gather_rows(block, count):
+    own = lax.axis_index("fsdp")
+    held = [(0, block)]
+    stacked = block[None]
+    for bit in reversed(bits_of(count)):
+        arrived = swap(stacked, bit, count, "fsdp")
+        held = held + [(at | bit, arrived[i]) for i, (at, _) in enumerate(held)]
+        stacked = jnp.concatenate([stacked, arrived], axis=0)
+    rows, width = block.shape
+    whole = jnp.zeros((count * rows, width), block.dtype)
+    for at, piece in held:
+        whole = lax.dynamic_update_slice(whole, piece, ((own ^ at) * rows, 0))
+    return whole
+
+
+def scatter_rows(sums, count):
+    own = lax.axis_index("fsdp")
+    _, rows, width = sums.shape
+    for bit in bits_of(count):
+        mine = (own & bit) // bit
+        split = sums.reshape(-1, 2, rows, width)
+        pick = lambda at: lax.dynamic_index_in_dim(split, at, axis=1, keepdims=False)
+        arrived = swap(pick(1 - mine).astype(jnp.bfloat16), bit, count, "fsdp")
+        sums = pick(mine).astype(jnp.float32) + arrived.astype(jnp.float32)
+    return sums.reshape(rows, width).astype(jnp.bfloat16)
 
 
 def in_order(blocks, own, count):
@@ -512,7 +555,7 @@
         ],
         axis=1,
     )
-    first_all = lax.all_gather(first, "fsdp", axis=0, tiled=True)
+    first_all = gather_rows(first, fsdp)
     qkv_width = q_width + 2 * kv_width
     w_qkv = first_all[:, :qkv_width]
     out_cols = first_all[:, qkv_width : qkv_width + o_width]
@@ -527,18 +570,12 @@
     second = jnp.concatenate(
         [pick(w_gate), pick(w_up), fold_rows(down_own, part)], axis=1
     )
-    second, _ = lax.optimization_barrier((second, first_all))
     second_all = lax.all_gather(second, "fsdp", axis=0, tiled=True)
     down_w = unfold_rows(second_all[:, 2 * local :].reshape(fsdp, part, local), units)
     down_w = down_w.reshape(local, width)
 
     token_blocks = gather_blocks(tokens, seq)
     inputs_all = in_order(token_blocks, own, seq)
-    cotangent_in, _ = lax.optimization_barrier((cotangent, inputs_all))
-    cot_blocks = gather_blocks(cotangent_in, seq)
-    cot_all = jnp.concatenate(
-        [cot_blocks[at].reshape(batch * rows, width) for at in range(seq)], axis=0
-    )
     out_w = lax.all_to_all(out_cols, "seq", split_axis=0, concat_axis=1, tiled=True)
 
     inputs_all32 = inputs_all.astype(f32)
@@ -551,18 +588,25 @@
     query_low, key_low, mixed = attend(qkv_raw, tables)
     flat_mixed = mixed.reshape(count, q_width)
     branch = dot(flat_mixed, out_w).astype(bf16).reshape(batch, length, width)
+    cot_blocks = gather_blocks(after(cotangent, *token_blocks.values()), seq, (mixed,))
+    cot_all = jnp.concatenate(
+        [cot_blocks[at].reshape(batch * rows, width) for at in range(seq)], axis=0
+    )
     branch, cot_all = lax.optimization_barrier((branch, cot_all))
     inputs = tokens.astype(f32)
     middle = inputs + scatter_blocks(from_order(branch, own, seq), seq)
 
     scale_two = rms_scale(middle)
     normed_two = (middle * scale_two * ffn_full).astype(bf16)
-    two_blocks = gather_blocks(normed_two, seq)
     flat = lambda values: values.reshape(batch * rows, width)
     half = seq // 2
-    near = jnp.concatenate([flat(two_blocks[at]) for at in range(half)], axis=0)
+    high = bits_of(seq)[-1]
+    opposite = swap(normed_two, high, seq)
+    near_blocks = gather_blocks(normed_two, half)
+    near = jnp.concatenate([flat(near_blocks[at]) for at in range(half)], axis=0)
     *kept, result_near, back_near = ffn(near, cot_all, second_all, down_w, 0, None)
-    far = jnp.concatenate([flat(two_blocks[at]) for at in range(half, seq)], axis=0)
+    far_blocks = gather_blocks(after(opposite, back_near), half)
+    far = jnp.concatenate([flat(far_blocks[at]) for at in range(half)], axis=0)
     hidden, grad_gate_act, grad_upward, result_far, back_far = ffn(
         far, cot_all, second_all, down_w, half * batch * rows, kept
     )
@@ -572,11 +616,11 @@
         pieces = [values.reshape(half, batch, rows, width) for values in (one, two)]
         return {at: pieces[at // half][at % half] for at in range(seq)}
 
-    grad_two = scatter_blocks(xor_blocks(back_near, back_far), seq)
-    grad_middle_norm, grad_ffn_gain = norm_back(grad_two, middle, scale_two, ffn_full)
-    grad_middle = cotangent.astype(f32) + grad_middle_norm
-    grad_branch = grad_middle.astype(bf16)
-    branch_blocks = gather_blocks(grad_branch, seq)
+    two_kept, two_sent = scatter_sums(xor_blocks(back_near, back_far), seq)
+    two_arrived = last_swap(two_sent, seq)
+    hidden, grad_gate_act, grad_upward, two_sent = lax.optimization_barrier(
+        (hidden, grad_gate_act, grad_upward, two_sent)
+    )
     grad_down = t_dot(hidden, cot_all).astype(bf16)
     grad_gate = t_dot(two_all, grad_gate_act).astype(bf16)
     grad_up = t_dot(two_all, grad_upward).astype(bf16)
@@ -585,6 +629,12 @@
     ffn_sums = jnp.concatenate(
         [grad_gate, grad_up, grad_down], axis=1
     )
+    two_arrived, ffn_sums = lax.optimization_barrier((two_arrived, ffn_sums))
+    grad_two = two_kept + two_arrived
+    grad_middle_norm, grad_ffn_gain = norm_back(grad_two, middle, scale_two, ffn_full)
+    grad_middle = cotangent.astype(f32) + grad_middle_norm
+    grad_branch = grad_middle.astype(bf16)
+    branch_blocks = gather_blocks(grad_branch, seq)
     ffn_share = lax.psum_scatter(ffn_sums, "fsdp", scatter_dimension=0, tiled=True)
     result_parts, _ = lax.optimization_barrier(
         ((result_near, result_far), tuple(branch_blocks.values()))
@@ -601,34 +651,34 @@
     normed_back = dot_t(grad_qkv, w_qkv)
     normed_back_low = normed_back.astype(bf16).reshape(batch, length, width)
     grad_attn_gain = jnp.sum(normed_back * hat_all.reshape(count, width), axis=0)
-    grad_normed = scatter_blocks(from_order(normed_back_low, own, seq), seq)
+    normed_kept, normed_sent = scatter_sums(from_order(normed_back_low, own, seq), seq)
+    normed_arrived = last_swap(normed_sent, seq)
+
+    last = jnp.concatenate([t_dot(flat_normed, grad_qkv).astype(bf16), grad_out_cols], axis=1)
+    last_width = last.shape[1]
+    gain_sums = gain_sums[:2, :HD] + gain_sums[:2, HD:]
+    gain_row = jnp.concatenate(
+        [
+            jnp.broadcast_to(gain_sums.reshape(1, 2 * HD), (fsdp, 2 * HD)),
+            grad_attn_gain.reshape(fsdp, part),
+            grad_ffn_gain.reshape(fsdp, part),
+        ],
+        axis=1,
+    ).astype(bf16)
+    gain_row = jnp.pad(gain_row[:, None, :], ((0, 0), (0, 15), (0, last_width - gain_row.shape[1])))
+    last = jnp.concatenate([last.reshape(fsdp, part, last_width), gain_row], axis=1)
+    last_share = scatter_rows(last, fsdp)
+    normed_arrived, last_share = lax.optimization_barrier((normed_arrived, last_share))
+    grad_normed = normed_kept + normed_arrived
     inputs_norm, _ = norm_back(grad_normed, inputs, rms_scale(inputs), attn_full)
     grad_tokens = grad_middle + inputs_norm
-
-    gain_cols = jnp.stack([grad_attn_gain, jnp.sum(grad_ffn_gain.reshape(1, width), axis=0)], axis=1)
-    last = jnp.concatenate(
-        [
-            t_dot(flat_normed, grad_qkv).astype(bf16),
-            grad_out_cols,
-            jnp.pad(gain_cols.astype(bf16), ((0, 0), (0, 126))),
-        ],
-        axis=1,
-    )
-    last_width = last.shape[1]
-    gain_sums = gain_sums[:2, :HD] + gain_sums[:2, HD:]
-    qk_row = gain_sums.reshape(2 * HD).astype(bf16)
-    qk_rows = jnp.zeros((fsdp, 16, last_width), bf16)
-    qk_rows = qk_rows.at[:, 0, : 2 * HD].set(qk_row)
-    last = jnp.concatenate([last.reshape(fsdp, part, last_width), qk_rows], axis=1)
-    last_share = lax.psum_scatter(
-        last.reshape(fsdp * (part + 16), last_width), "fsdp", scatter_dimension=0, tiled=True
-    )
-    share_blocks = gather_blocks(ffn_share, seq)
-    ffn_shares = jnp.stack([share_blocks[at] for at in range(seq)]).astype(f32)
-    for bit in bits_of(seq):
-        turned = ffn_shares.reshape(-1, 2, bit, part, ffn_share.shape[1])[:, ::-1]
-        ffn_shares = jnp.where((own & bit) > 0, turned.reshape(ffn_shares.shape), ffn_shares)
     last_shares = lax.all_gather(last_share, "seq", axis=0, tiled=False).astype(f32)
+    share_blocks = gather_blocks(after(ffn_share, last_shares), seq)
+    ffn_shares = jnp.zeros((seq,) + ffn_share.shape, bf16)
+    for at in range(seq):
+        ffn_shares = lax.dynamic_update_slice(
+            ffn_shares, share_blocks[at][None], (own ^ at, 0, 0)
+        )
 
     def unpick(piece):
         split = piece.reshape(seq, part, fsdp, units)
@@ -637,16 +687,17 @@
     def side_by_side(piece):
         return jnp.transpose(piece, (1, 0, 2)).reshape(part, -1)
 
-    shard_gate = unpick(ffn_shares[:, :, :local])
-    shard_up = unpick(ffn_shares[:, :, local : 2 * local])
+    shard_gate = unpick(ffn_shares[:, :, :local]).astype(f32)
+    shard_up = unpick(ffn_shares[:, :, local : 2 * local]).astype(f32)
     shard_down = unfold_rows(ffn_shares[:, :, 2 * local :], units).reshape(seq * units, width)
+    shard_down = shard_down.astype(f32)
     top = last_shares[:, :part]
     shard_query = side_by_side(top[:, :, :q_width])
     shard_key = side_by_side(top[:, :, q_width : q_width + kv_width])
     shard_value = side_by_side(top[:, :, q_width + kv_width : qkv_width])
-    shard_out = side_by_side(top[:, :, qkv_width : qkv_width + o_width])
-    shard_gains = jnp.sum(top[:, :, qkv_width + o_width : qkv_width + o_width + 2], axis=0)
-    gain_total = jnp.sum(last_shares[:, part, : 2 * HD], axis=0).reshape(2, HD)
+    shard_out = side_by_side(top[:, :, qkv_width:])
+    gains = jnp.sum(last_shares[:, part], axis=0)
+    gain_total = gains[: 2 * HD].reshape(2, HD)
     return (
         result,
         grad_tokens,
@@ -657,8 +708,8 @@
         shard_gate,
         shard_up,
         shard_down,
-        shard_gains[:, 0],
-        shard_gains[:, 1],
+        gains[2 * HD : 2 * HD + part],
+        gains[2 * HD + part : 2 * HD + 2 * part],
         gain_total,
     )
 

time: 577 us -> 554 us (0.960)
  waiting for transfers between devices: 232 us -> 190 us
  blocking collectives: 10.1 us -> 21.2 us
  local copies, waits for them, and re-layouts: 78.8 us -> 86.9 us
  matrix products: 49.6 us -> 43.8 us
    all_gather x1 -> x0, waiting for transfers between devices: 39.8 us -> none  [per_device(): first_all = lax.all_gather(first, 'fsdp', axis=0, tiled=True)]
    select_n x2 -> x0, other arithmetic: 15.1 us -> none  [per_device(): jnp.where(own & bit > 0, turned.reshape(ffn_shares.shape), ffn_shares)]
    reduce_scatter x1 -> x0, waiting for transfers between devices: 14.5 us -> none  [per_device(): lax.psum_scatter(last.reshape(fsdp * (part + 16), last_width), 'fsdp', sc...]
    convert_element_type x1 -> x6, local copies, waits for them, and re-layouts: 0.09 us -> 14.2 us  [the longest x2 6.34 us: per_device(): shard_up = unpick(ffn_shares[:, :, local:2 * local]).astype(f32)]
    rev x2 -> x0, local copies, waits for them, and re-layouts: 12.7 us -> none  [per_device(): turned = ffn_shares.reshape(-1, 2, bit, part, ffn_share.shape[1])[:, ::-1]]
    all_to_all x0 -> x1, blocking collectives: none -> 12.5 us  [per_device(): lax.all_to_all(out_cols, 'seq', split_axis=0, concat_axis=1, tiled=True)]
    ppermute x27 -> x33, waiting for transfers between devices: 178 us -> 190 us  [swap(): return lax.ppermute(values, axis, [(i, i ^ bit) for i in range(total)])]
    ppermute x27 -> x33, starting transfers between devices: 16.2 us -> 23.4 us  [swap(): return lax.ppermute(values, axis, [(i, i ^ bit) for i in range(total)])]
  transfers between devices with their start and end apart: 33 -> 36, of which waited for: 14 -> 16; matrix products, arithmetic and copies ran while one was open for 18% -> 28% of each run, Pallas kernels for 8% -> 12%
where the time goes in v3:
time: 554 us; the launch traced here: 545 us
  waiting for transfers between devices  190 us (34%)
  Pallas kernels  88 us (16%)
  local copies, waits for them, and re-layouts  86.9 us (16%)
  other arithmetic  71.7 us (13%)
  matrix products  43.8 us (8%)
  starting transfers between devices  27.6 us (5%)
  blocking collectives  21.2 us (4%)
  between operations  15.4 us (3%)
    ppermute x33, waiting for transfers between devices, swap(): return lax.ppermute(values, axis, [(i, i ^ bit) for i in range(total)])  190 us
    pallas_call x2, Pallas kernels, ffn(): pl.pallas_call(ffn_kernel, grid=(rows // step,), in_specs=[here(width), t...  44.7 us
    unnamed x102, local copies, waits for them, and re-layouts  32.1 us
    pallas_call x1, Pallas kernels, attend_back(): pl.pallas_call(attend_back_kernel, grid=(batch, groups), in_specs=[own_co...  26.3 us
    dot_general x5, matrix products, t_dot(): lax.dot_general(left, right, (((0,), (0,)), ((), ())), preferred_element_...  25 us
    ppermute x33, starting transfers between devices, swap(): return lax.ppermute(values, axis, [(i, i ^ bit) for i in range(total)])  23.4 us
    pallas_call x1, Pallas kernels, attend(): pl.pallas_call(attend_kernel, grid=(batch, groups), in_specs=[own_column,...  17.1 us
    dot_general x2, matrix products, dot_t(): lax.dot_general(left, right, (((1,), (1,)), ((), ())), preferred_element_...  13.1 us
  transfers between devices with their start and end apart: 36, of which 16 were waited for; matrix products, arithmetic and copies ran while one was open for 28% of the time, Pallas kernels for 12%

profile of v3, /device:TPU:0, one launch (start us, length us, event | category | flops | bytes accessed | tf_op | source)
XLA Modules:
  0.0 544.6 jit_solution(15505589317850864118)
XLA Ops:
  14.8 2.6 collective-permute-start.1
  20.8 2.7 collective-permute-start.3
  24.3 23.0 %collective-permute-done.3 = bf16[1,128,896]{2,1,0:T(8,128)(2,1)S(1)} collective-permute-done((bf16[1,128,896]{2,1,0:T(8,128)(2,1)S(1)}, bf16[1,128,896]{2,1,0:T(8,128)(2,1)S(1)}, u32[]{:S(2)}, u32[]{:S(2)}) %collective-permute-start.3) | collective-permute-done | bytes 229408 | tf_op jit(solution)/shard_map/ppermute | solution.py:419
  47.4 2.1 collective-permute-start.4
  49.7 2.2 fusion.22
  53.9 16.6 %collective-permute-done.4 = bf16[2,128,896]{2,1,0:T(8,128)(2,1)S(1)} collective-permute-done((bf16[2,128,896]{2,1,0:T(8,128)(2,1)S(1)}, bf16[2,128,896]{2,1,0:T(8,128)(2,1)S(1)}, u32[]{:S(2)}, u32[]{:S(2)}) %collective-permute-start.4) | collective-permute-done | bytes 458784 | tf_op jit(solution)/shard_map/ppermute | solution.py:419
  75.1 32.8 %collective-permute-done.5 = bf16[4,128,896]{2,1,0:T(8,128)(2,1)S(1)} collective-permute-done((bf16[4,128,896]{2,1,0:T(8,128)(2,1)S(1)}, bf16[4,128,896]{2,1,0:T(8,128)(2,1)S(1)}, u32[]{:S(2)}, u32[]{:S(2)}) %collective-permute-start.5) | collective-permute-done | bytes 917536 | tf_op jit(solution)/shard_map/ppermute | solution.py:419
  110.7 4.5 fusion.15.q_ref.k_ref.v_ref
  115.2 17.1 %attend.1 = (bf16[2,1024,256]{2,1,0:T(8,128)(2,1)}, bf16[2,1024,128]{2,1,0:T(8,128)(2,1)}, bf16[2,1024,256]{2,1,0:T(8,128)(2,1)}) custom-call(f32[2,1024,512]{2,1,0:T(8,128)} %fusion.15.q_ref.k_ref.v_ref, f32[2,1024,512]{2,1,0:T(8,128)} %fusion.15.q_ref.k_ref.v_ref, f32[2,1024,512]{2,1,0:T(8,128)} %fusion.15.q_ref.k_ref.v_ref, ...), custom_call_target="tpu_custom_call" | custom-call | flops 2147483648 | bytes 8388608 | tf_op jit(solution)/shard_map/attend/pallas_call | solution.py:270
  132.8 1.9 slice.188
  134.7 2.0 copy.159
  136.7 12.5 %all_to_all.35 = bf16[4,256,256]{1,2,0:T(8,128)(2,1)S(1)} all-to-all(bf16[4,256,256]{1,2,0:T(8,128)(2,1)} %copy.159), channel_id=1, replica_groups=mesh['fsdp'=8,'seq'=4] {'seq'}, dimensions={0} | all-to-all | bytes 1048576 | tf_op jit(solution)/shard_map/all_to_all | solution.py:579
  150.5 3.6 pad_maximum_fusion.1.cot_ref
  154.8 2.1 collective-permute-done.10
  158.5 24.2 %collective-permute-done.11 = bf16[2,256,1024]{2,1,0:T(8,128)(2,1)S(1)} collective-permute-done((bf16[2,256,1024]{2,1,0:T(8,128)(2,1)S(1)}, bf16[2,256,1024]{2,1,0:T(8,128)(2,1)S(1)}, u32[]{:S(2)}, u32[]{:S(2)}) %collective-permute-start.11) | collective-permute-done | bytes 1048608 | tf_op jit(solution)/shard_map/ppermute | solution.py:419
  185.0 2.5 collective-permute-done.12
  188.4 2.8 pad_maximum_fusion.4.two_ref
  196.6 3.2 pad_maximum_fusion.3
  199.8 22.1 %ffn.2 = (bf16[2048,1152]{1,0:T(8,128)(2,1)}, bf16[2048,1152]{1,0:T(8,128)(2,1)}, bf16[2048,1152]{1,0:T(8,128)(2,1)}, bf16[1024,1024]{1,0:T(8,128)(2,1)}, bf16[1024,1024]{1,0:T(8,128)(2,1)}) custom-call(bf16[1024,1024]{1,0:T(8,128)(2,1)} %pad_maximum_fusion.4.two_ref, bf16[2048,1024]{1,0:T(8,128)(2,1)} %pad_maximum_fusion.1.cot_ref, ...), custom_call_target="tpu_custom_call" | custom-call | flops 14495514624 | bytes 22544384 | tf_op jit(solution)/shard_map/ffn/pallas_call | solution.py:373
  222.2 2.7 collective-permute-done.15
  225.9 2.8 pad_maximum_fusion.5.two_ref
  228.7 22.5 %ffn.3 = (bf16[2048,1152]{1,0:T(8,128)(2,1)}, bf16[2048,1152]{1,0:T(8,128)(2,1)}, bf16[2048,1152]{1,0:T(8,128)(2,1)}, bf16[1024,1024]{1,0:T(8,128)(2,1)}, bf16[1024,1024]{1,0:T(8,128)(2,1)}) custom-call(bf16[1024,1024]{1,0:T(8,128)(2,1)} %pad_maximum_fusion.5.two_ref, ...), custom_call_target="tpu_custom_call", output_to_operand_aliasing={{0}: (5, {}), {1}: (6, {}), {2}: (7, {})} | custom-call | flops 14495514624 | bytes 22544384 | tf_op jit(solution)/shard_map/ffn/pallas_call | solution.py:373
  257.6 7.4 %convolution_convert_fusion.2 = bf16[1024,1152]{1,0:T(8,128)(2,1)S(1)} fusion(bf16[2048,1152]{1,0:T(8,128)(2,1)S(1)} %copy-done.39, bf16[512,1024]{1,0:T(8,128)(2,1)S(1)} %bitcast.239, bf16[512,1024]{1,0:T(8,128)(2,1)} %bitcast.34, bf16[512,1024]{1,0:T(8,128)(2,1)S(1)} %bitcast.236, bf16[512,1024]{1,0:T(8,128)(2,1)} %bitcast.20), kind=kOutput, calls=%fused_computation.11 | convolution fusion | flops 4849795072 | bytes 11272192 | tf_op jit(solution)/shard_map/dot_general | solution.py:510
  265.1 7.4 %convolution_convert_fusion.1 = bf16[1024,1152]{1,0:T(8,128)(2,1)S(1)} fusion(bf16[2048,1152]{1,0:T(8,128)(2,1)S(1)} %bitcast.253, bf16[512,1024]{1,0:T(8,128)(2,1)S(1)} %bitcast.240, bf16[512,1024]{1,0:T(8,128)(2,1)} %bitcast.34, bf16[512,1024]{1,0:T(8,128)(2,1)S(1)} %bitcast.237, bf16[512,1024]{1,0:T(8,128)(2,1)} %bitcast.20), kind=kOutput, calls=%fused_computation.10 | convolution fusion | flops 4849795072 | bytes 11272192 | tf_op jit(solution)/shard_map/dot_general | solution.py:510
  272.5 5.4 convolution_convert_fusion
  278.2 3.5 pad_maximum_fusion
  282.7 2.8 convert_element_type.260
  285.6 3.0 multiply_reduce_fusion
  292.1 1.9 copy-done.8
  294.6 24.1 %collective-permute-done.19 = bf16[2,256,1024]{2,1,0:T(8,128)(2,1)} collective-permute-done((bf16[2,256,1024]{2,1,0:T(8,128)(2,1)}, bf16[2,256,1024]{2,1,0:T(8,128)(2,1)}, u32[]{:S(2)}, u32[]{:S(2)}) %collective-permute-start.19) | collective-permute-done | bytes 1048608 | tf_op jit(solution)/shard_map/ppermute | solution.py:419
  318.7 6.5 %convert_multiply_fusion = f32[2,1024,1024]{2,1,0:T(8,128)} fusion(bf16[2,1024,1024]{2,1,0:T(8,128)(2,1)} %copy-done.3, f32[2,1024]{1,0:T(2,128)S(1)} %add_rsqrt_fusion), kind=kLoop, calls=%fused_computation | loop fusion | flops 4194304 | bytes 12591104 | tf_op jit(solution)/shard_map/mul | solution.py:583
  334.1 1.9 copy-done.10
  338.1 4.1 all-to-all-start.1
  342.3 3.0 fusion.8
  345.3 2.0 collective-permute-start.23
  347.3 4.5 convolution_convert_fusion.4
  351.8 26.3 %attend_back.1 = (bf16[2,1024,512]{2,1,0:T(8,128)(2,1)}, f32[8,128]{1,0:T(8,128)}) custom-call(bf16[2,1024,256]{2,1,0:T(8,128)(2,1)} %get-tuple-element.44.low_q_ref, bf16[2,1024,128]{2,1,0:T(8,128)(2,1)} %get-tuple-element.45.low_k_ref, f32[2,1024,512]{2,1,0:T(8,128)} %fusion.15.q_ref.k_ref.v_ref, f32[2,1024,512]{2,1,0:T(8,128)} %fusion.15.q_ref.k_ref.v_ref, ...), custom_call_target="tpu_custom_call" | custom-call | flops 5368709120 | bytes 12582912 | tf_op jit(solution)/shard_map/attend_back/pallas_call | solution.py:305
  379.1 3.7 fusion.11
  382.9 8.5 %fusion.1 = (bf16[1024]{0:T(1024)(128)(2,1)S(1)}, bf16[2048,1024]{1,0:T(8,128)(2,1)}) fusion(f32[2,1024,1024]{2,1,0:T(8,128)} %convert_multiply_fusion, bf16[2048,512]{1,0:T(8,128)(2,1)S(1)} %bitcast.198, bf16[1024,896]{1,0:T(8,128)(2,1)S(1)} %copy-done.16), kind=kOutput, calls=%fused_computation.4 | convolution fusion | flops 2153774080 | bytes 15730688 | tf_op jit(solution)/shard_map/dot_general | solution.py:504
  391.4 3.6 bitcast_convert_fusion
  397.7 2.1 collective-permute-start.27
  401.3 18.7 %collective-permute-done.27 = bf16[4,144,768]{2,1,0:T(8,128)(2,1)} collective-permute-done((bf16[4,144,768]{2,1,0:T(8,128)(2,1)}, bf16[4,144,768]{2,1,0:T(8,128)(2,1)}, u32[]{:S(2)}, u32[]{:S(2)}) %collective-permute-start.27) | collective-permute-done | bytes 884768 | tf_op jit(solution)/shard_map/ppermute | solution.py:419
  423.6 2.9 add_convert_fusion
  427.2 8.3 %collective-permute-done.28 = bf16[2,144,768]{2,1,0:T(8,128)(2,1)} collective-permute-done((bf16[2,144,768]{2,1,0:T(8,128)(2,1)}, bf16[2,144,768]{2,1,0:T(8,128)(2,1)}, u32[]{:S(2)}, u32[]{:S(2)}) %collective-permute-start.28) | collective-permute-done | bytes 442400 | tf_op jit(solution)/shard_map/ppermute | solution.py:419
  438.5 2.3 collective-permute-start.29
  440.8 9.5 %collective-permute-done.29 = bf16[1,144,768]{2,1,0:T(8,128)(2,1)S(1)} collective-permute-done((bf16[1,144,768]{2,1,0:T(8,128)(2,1)}, bf16[1,144,768]{2,1,0:T(8,128)(2,1)S(1)}, u32[]{:S(2)}, u32[]{:S(2)}) %collective-permute-start.29) | collective-permute-done | bytes 221216 | tf_op jit(solution)/shard_map/ppermute | solution.py:419
  451.4 2.8 convert_element_type.281
  454.2 8.7 %all-gather = bf16[576,768]{1,0:T(8,128)(2,1)S(1)} all-gather(bf16[144,768]{1,0:T(8,128)(2,1)S(1)} %fusion.30), channel_id=2, replica_groups=mesh['fsdp'=8,'seq'=4] {'seq'}, dimensions={0}, use_global_device_ids=true | all-gather | bytes 1105920 | tf_op jit(solution)/shard_map/all_gather | solution.py:675
  465.3 2.1 copy.171
  467.4 2.0 copy.180
  469.4 2.1 copy.174
  471.5 2.0 copy.183
  473.5 1.9 slice_bitcast_fusion.2
  481.3 3.1 fusion.3
  485.1 4.0 fusion.6
  490.7 20.6 %collective-permute-done.31 = bf16[128,3456]{1,0:T(8,128)(2,1)S(1)} collective-permute-done((bf16[128,3456]{1,0:T(8,128)(2,1)}, bf16[128,3456]{1,0:T(8,128)(2,1)S(1)}, u32[]{:S(2)}, u32[]{:S(2)}) %collective-permute-start.31) | collective-permute-done | bytes 884768 | tf_op jit(solution)/shard_map/ppermute | solution.py:419
  511.5 2.2 collective-permute-done.32
  514.0 2.5 slice_convert_fusion
  518.4 3.0 copy.175
  521.5 3.3 copy.176
  524.8 3.0 copy.184
  527.8 3.0 copy.177
  530.9 3.3 copy.178
  534.2 3.1 copy.185
  (244 shorter events, 84.3 us)
Async XLA Ops:
  7.2 3.0 copy-start.30
  7.2 184.1 %all-gather.3.cloned.1.call-start = ((), (), s32[]{:S(2)}) async-start(), calls=%async_computation.3 | async-start | bytes 7962624 | tf_op jit(solution)/shard_map/all_gather | solution.py:573
  11.6 5.7 %copy-start.36 = (bf16[128]{0:T(256)(128)(2,1)S(1)}, bf16[128]{0:T(256)(128)(2,1)}, u32[]{:S(2)}) copy-start(bf16[128]{0:T(256)(128)(2,1)} %param.21) | copy-start | bytes 772
  11.6 5.7 %copy-start.37 = (bf16[128]{0:T(256)(128)(2,1)S(1)}, bf16[128]{0:T(256)(128)(2,1)}, u32[]{:S(2)}) copy-start(bf16[128]{0:T(256)(128)(2,1)} %param.20) | copy-start | bytes 772
  14.1 474.9 %reduce-scatter.2.cloned.1.call-start = ((), (), s32[]{:S(2)}) async-start(), calls=%async_computation.4 | async-start | bytes 7962624 | tf_op jit(solution)/shard_map/reduce_scatter | solution.py:638
  14.2 58.1 %collective-permute-start = (bf16[2,256,1024]{2,1,0:T(8,128)(2,1)S(1)}, bf16[2,256,1024]{2,1,0:T(8,128)(2,1)}, u32[]{:S(2)}, u32[]{:S(2)}) collective-permute-start(bf16[2,256,1024]{2,1,0:T(8,128)(2,1)S(1)} %copy-done.11), channel_id=1, source_target_pairs={{0,1},{1,0},{2,3},{3,2},{4,5},{5,4},{6,7},{7,6},{8,9},{9,8},{10,11... | collective-permute-start | bytes 3145736 | tf_op jit(solution)/shard_map/ppermute | solution.py:419
  14.8 57.5 %collective-permute-start.1 = (bf16[2,256,1024]{2,1,0:T(8,128)(2,1)S(1)}, bf16[2,256,1024]{2,1,0:T(8,128)(2,1)}, u32[]{:S(2)}, u32[]{:S(2)}) collective-permute-start(bf16[2,256,1024]{2,1,0:T(8,128)(2,1)S(1)} %copy-done.11), channel_id=1, source_target_pairs={{0,2},{1,3},{2,0},{3,1},{4,6},{5,7},{6,4},{7,5},{8,10},{9,11},{10,... | collective-permute-start | bytes 3145736 | tf_op jit(solution)/shard_map/ppermute | solution.py:419
  20.8 26.6 %collective-permute-start.3 = (bf16[1,128,896]{2,1,0:T(8,128)(2,1)S(1)}, bf16[1,128,896]{2,1,0:T(8,128)(2,1)S(1)}, u32[]{:S(2)}, u32[]{:S(2)}) collective-permute-start(bf16[1,128,896]{2,1,0:T(8,128)(2,1)S(1)} %bitcast.209), channel_id=1, source_target_pairs={{0,16},{4,20},{8,24},{12,28},{16,0},{20,4},{24,8},{28,12},{1,17},{... | collective-permute-start | bytes 688136 | tf_op jit(solution)/shard_map/ppermute | solution.py:419
  24.3 27.6 %copy-start.38 = (bf16[2,64]{1,0:T(2,128)(2,1)S(1)}, bf16[2,64]{1,0:T(2,128)(2,1)}, u32[]{:S(2)}) copy-start(bf16[2,64]{1,0:T(2,128)(2,1)} %param.22) | copy-start | bytes 772
  47.4 23.1 %collective-permute-start.4 = (bf16[2,128,896]{2,1,0:T(8,128)(2,1)S(1)}, bf16[2,128,896]{2,1,0:T(8,128)(2,1)S(1)}, u32[]{:S(2)}, u32[]{:S(2)}) collective-permute-start(bf16[2,128,896]{2,1,0:T(8,128)(2,1)S(1)} %pad_maximum_fusion.14), channel_id=1, source_target_pairs={{0,8},{4,12},{8,0},{12,4},{16,24},{20,28},{24,16},{28,20},{1,9},{5... | collective-permute-start | bytes 1376264 | tf_op jit(solution)/shard_map/ppermute | solution.py:419
  70.6 37.3 %collective-permute-start.5 = (bf16[4,128,896]{2,1,0:T(8,128)(2,1)S(1)}, bf16[4,128,896]{2,1,0:T(8,128)(2,1)S(1)}, u32[]{:S(2)}, u32[]{:S(2)}) collective-permute-start(bf16[4,128,896]{2,1,0:T(8,128)(2,1)S(1)} %pad_maximum_fusion.7), channel_id=1, source_target_pairs={{0,4},{4,0},{8,12},{12,8},{16,20},{20,16},{24,28},{28,24},{1,5},{5... | collective-permute-start | bytes 2752520 | tf_op jit(solution)/shard_map/ppermute | solution.py:419
  72.3 36.1 %collective-permute-start.2 = (bf16[2,256,1024]{2,1,0:T(8,128)(2,1)}, bf16[2,256,1024]{2,1,0:T(8,128)(2,1)S(1)}, u32[]{:S(2)}, u32[]{:S(2)}) collective-permute-start(bf16[2,256,1024]{2,1,0:T(8,128)(2,1)} %collective-permute-done.1), channel_id=1, source_target_pairs={{0,1},{1,0},{2,3},{3,2},{4,5},{5,4},{6,7},{7,6},{8,9},{9,8},{10,11... | collective-permute-start | bytes 3145736 | tf_op jit(solution)/shard_map/ppermute | solution.py:419
  73.7 34.7 %copy-start.12 = (bf16[2,256,1024]{2,1,0:T(8,128)(2,1)S(1)}, bf16[2,256,1024]{2,1,0:T(8,128)(2,1)}, u32[]{:S(2)}) copy-start(bf16[2,256,1024]{2,1,0:T(8,128)(2,1)} %param.23) | copy-start | bytes 3145732
  108.4 23.9 %collective-permute-start.7 = (bf16[2,256,1024]{2,1,0:T(8,128)(2,1)S(1)}, bf16[2,256,1024]{2,1,0:T(8,128)(2,1)}, u32[]{:S(2)}, u32[]{:S(2)}) collective-permute-start(bf16[2,256,1024]{2,1,0:T(8,128)(2,1)S(1)} %copy-done.12), channel_id=1, source_target_pairs={{0,2},{1,3},{2,0},{3,1},{4,6},{5,7},{6,4},{7,5},{8,10},{9,11},{10,... | collective-permute-start | bytes 3145736 | tf_op jit(solution)/shard_map/ppermute | solution.py:419
  109.7 40.8 %collective-permute-start.6 = (bf16[2,256,1024]{2,1,0:T(8,128)(2,1)S(1)}, bf16[2,256,1024]{2,1,0:T(8,128)(2,1)}, u32[]{:S(2)}, u32[]{:S(2)}) collective-permute-start(bf16[2,256,1024]{2,1,0:T(8,128)(2,1)S(1)} %copy-done.12), channel_id=1, source_target_pairs={{0,1},{1,0},{2,3},{3,2},{4,5},{5,4},{6,7},{7,6},{8,9},{9,8},{10,11... | collective-permute-start | bytes 3145736 | tf_op jit(solution)/shard_map/ppermute | solution.py:419
  109.8 5.4 copy-start.3
  132.2 16.9 %copy-start.18 = (bf16[2,1024,256]{2,1,0:T(8,128)(2,1)S(1)}, bf16[2,1024,256]{2,1,0:T(8,128)(2,1)}, u32[]{:S(2)}) copy-start(bf16[2,1024,256]{2,1,0:T(8,128)(2,1)} %get-tuple-element.46) | copy-start | bytes 3145732
  132.3 18.2 %collective-permute-start.8 = (bf16[2,256,1024]{2,1,0:T(8,128)(2,1)}, bf16[2,256,1024]{2,1,0:T(8,128)(2,1)}, u32[]{:S(2)}, u32[]{:S(2)}) collective-permute-start(bf16[2,256,1024]{2,1,0:T(8,128)(2,1)} %collective-permute-done.7), channel_id=1, source_target_pairs={{0,1},{1,0},{2,3},{3,2},{4,5},{5,4},{6,7},{7,6},{8,9},{9,8},{10,11... | collective-permute-start | bytes 3145736 | tf_op jit(solution)/shard_map/ppermute | solution.py:419
  154.3 2.7 collective-permute-start.10
  154.3 4.1 collective-permute-start.9
  157.4 25.3 %collective-permute-start.11 = (bf16[2,256,1024]{2,1,0:T(8,128)(2,1)S(1)}, bf16[2,256,1024]{2,1,0:T(8,128)(2,1)S(1)}, u32[]{:S(2)}, u32[]{:S(2)}) collective-permute-start(bf16[2,256,1024]{2,1,0:T(8,128)(2,1)S(1)} %add_convert_fusion.1), channel_id=1, source_target_pairs={{0,2},{1,3},{2,0},{3,1},{4,6},{5,7},{6,4},{7,5},{8,10},{9,11},{10,... | collective-permute-start | bytes 3145736 | tf_op jit(solution)/shard_map/ppermute | solution.py:419
  184.6 2.9 collective-permute-start.12
  184.6 37.4 %collective-permute-start.14 = (bf16[2,256,1024]{2,1,0:T(8,128)(2,1)}, bf16[2,256,1024]{2,1,0:T(8,128)(2,1)}, u32[]{:S(2)}, u32[]{:S(2)}) collective-permute-start(bf16[2,256,1024]{2,1,0:T(8,128)(2,1)} %multiply_convert_fusion.1), channel_id=1, source_target_pairs={{0,2},{1,3},{2,0},{3,1},{4,6},{5,7},{6,4},{7,5},{8,10},{9,11},{10,... | collective-permute-start | bytes 3145736 | tf_op jit(solution)/shard_map/ppermute | solution.py:419
  222.0 2.9 collective-permute-start.15
  253.1 2.7 collective-permute-start.16
  253.5 4.2 copy-start.39
  254.9 30.6 %collective-permute-start.13 = (bf16[2,256,1024]{2,1,0:T(8,128)(2,1)}, bf16[2,256,1024]{2,1,0:T(8,128)(2,1)}, u32[]{:S(2)}, u32[]{:S(2)}) collective-permute-start(bf16[2,256,1024]{2,1,0:T(8,128)(2,1)} %bitcast.33), channel_id=1, source_target_pairs={{0,1},{1,0},{2,3},{3,2},{4,5},{5,4},{6,7},{7,6},{8,9},{9,8},{10,11... | collective-permute-start | bytes 3145736 | tf_op jit(solution)/shard_map/ppermute | solution.py:419
  255.8 9.2 %slice-start.2 = ((s8[4718592]{0:T(1024)(128)(4,1)}), s8[4194304]{0:T(1024)(128)(4,1)S(1)}, s32[]{:S(2)}) async-start(s8[4718592]{0:T(1024)(128)(4,1)} %bitcast.252), calls=%async_computation.7 | async-start | bytes 8388608
  257.2 25.5 %collective-permute-start.17 = (bf16[2,256,1024]{2,1,0:T(8,128)(2,1)}, bf16[2,256,1024]{2,1,0:T(8,128)(2,1)}, u32[]{:S(2)}, u32[]{:S(2)}) collective-permute-start(bf16[2,256,1024]{2,1,0:T(8,128)(2,1)} %fusion.12), channel_id=1, source_target_pairs={{0,2},{1,3},{2,0},{3,1},{4,6},{5,7},{6,4},{7,5},{8,10},{9,11},{10,... | collective-permute-start | bytes 3145736 | tf_op jit(solution)/shard_map/ppermute | solution.py:419
  257.6 7.5 %slice-start.3 = ((s8[4718592]{0:T(1024)(128)(4,1)}), s8[524288]{0:T(1024)(128)(4,1)S(1)}, s32[]{:S(2)}) async-start(s8[4718592]{0:T(1024)(128)(4,1)} %bitcast.252), calls=%async_computation.8 | async-start | bytes 1048576
  257.6 14.9 %slice-start = ((s8[4718592]{0:T(1024)(128)(4,1)}), s8[4194304]{0:T(1024)(128)(4,1)S(1)}, s32[]{:S(2)}) async-start(s8[4718592]{0:T(1024)(128)(4,1)} %bitcast.250), calls=%async_computation.5 | async-start | bytes 8388608
  265.1 7.4 %copy-start.23 = (bf16[2048,1024]{1,0:T(8,128)(2,1)S(1)}, bf16[2048,1024]{1,0:T(8,128)(2,1)}, u32[]{:S(2)}) copy-start(bf16[2048,1024]{1,0:T(8,128)(2,1)} %pad_maximum_fusion.1.cot_ref) | copy-start | bytes 12582916
  265.1 7.4 %slice-start.1 = ((s8[4718592]{0:T(1024)(128)(4,1)}), s8[524288]{0:T(1024)(128)(4,1)S(1)}, s32[]{:S(2)}) async-start(s8[4718592]{0:T(1024)(128)(4,1)} %bitcast.250), calls=%async_computation.6 | async-start | bytes 1048576
  288.5 3.6 copy-start.5
  294.0 24.7 %collective-permute-start.19 = (bf16[2,256,1024]{2,1,0:T(8,128)(2,1)}, bf16[2,256,1024]{2,1,0:T(8,128)(2,1)}, u32[]{:S(2)}, u32[]{:S(2)}) collective-permute-start(bf16[2,256,1024]{2,1,0:T(8,128)(2,1)} %get-tuple-element.143), channel_id=1, source_target_pairs={{0,2},{1,3},{2,0},{3,1},{4,6},{5,7},{6,4},{7,5},{8,10},{9,11},{10,... | collective-permute-start | bytes 3145736 | tf_op jit(solution)/shard_map/ppermute | solution.py:419
  294.6 30.6 %collective-permute-start.18 = (bf16[2,256,1024]{2,1,0:T(8,128)(2,1)}, bf16[2,256,1024]{2,1,0:T(8,128)(2,1)}, u32[]{:S(2)}, u32[]{:S(2)}) collective-permute-start(bf16[2,256,1024]{2,1,0:T(8,128)(2,1)} %get-tuple-element.143), channel_id=1, source_target_pairs={{0,1},{1,0},{2,3},{3,2},{4,5},{5,4},{6,7},{7,6},{8,9},{9,8},{10,11... | collective-permute-start | bytes 3145736 | tf_op jit(solution)/shard_map/ppermute | solution.py:419
  318.7 6.5 %collective-permute-start.20 = (bf16[2,256,1024]{2,1,0:T(8,128)(2,1)}, bf16[2,256,1024]{2,1,0:T(8,128)(2,1)}, u32[]{:S(2)}, u32[]{:S(2)}) collective-permute-start(bf16[2,256,1024]{2,1,0:T(8,128)(2,1)} %collective-permute-done.19), channel_id=1, source_target_pairs={{0,1},{1,0},{2,3},{3,2},{4,5},{5,4},{6,7},{7,6},{8,9},{9,8},{10,11... | collective-permute-start | bytes 3145736 | tf_op jit(solution)/shard_map/ppermute | solution.py:419
  318.7 6.5 %copy-start.28 = (bf16[1024,1024]{1,0:T(8,128)(2,1)S(1)}, bf16[1024,1024]{1,0:T(8,128)(2,1)}, u32[]{:S(2)}) copy-start(bf16[1024,1024]{1,0:T(8,128)(2,1)} %get-tuple-element.68) | copy-start | bytes 6291460
  325.1 3.1 copy-start.9
  326.7 4.3 copy-start.27
  326.7 15.6 %collective-permute-start.22 = (bf16[2,256,1024]{2,1,0:T(8,128)(2,1)}, bf16[2,256,1024]{2,1,0:T(8,128)(2,1)}, u32[]{:S(2)}, u32[]{:S(2)}) collective-permute-start(bf16[2,256,1024]{2,1,0:T(8,128)(2,1)} %bitcast.47), channel_id=1, source_target_pairs={{0,1},{1,0},{2,3},{3,2},{4,5},{5,4},{6,7},{7,6},{8,9},{9,8},{10,11... | collective-permute-start | bytes 3145736 | tf_op jit(solution)/shard_map/ppermute | solution.py:419
  330.9 5.1 copy-start.19
  332.4 46.6 %collective-permute-start.21 = (bf16[2,256,1024]{2,1,0:T(8,128)(2,1)}, bf16[2,256,1024]{2,1,0:T(8,128)(2,1)}, u32[]{:S(2)}, u32[]{:S(2)}) collective-permute-start(bf16[2,256,1024]{2,1,0:T(8,128)(2,1)} %bitcast.45), channel_id=1, source_target_pairs={{0,1},{1,0},{2,3},{3,2},{4,5},{5,4},{6,7},{7,6},{8,9},{9,8},{10,11... | collective-permute-start | bytes 3145736 | tf_op jit(solution)/shard_map/ppermute | solution.py:419
  338.1 56.9 %all-to-all-start.1 = ((bf16[256,4,256]{2,0,1:T(8,128)(2,1)}), bf16[256,4,256]{2,0,1:T(8,128)(2,1)}, u32[]{:S(2)}, u32[]{:S(2)}) async-start(bf16[256,4,256]{2,0,1:T(8,128)(2,1)} %bitcast.218), calls=%async_computation.1 | async-start | bytes 1048576 | tf_op jit(solution)/shard_map/all_to_all | solution.py:646
  342.2 5.0 copy-start.26
  345.3 33.8 %collective-permute-start.23 = (bf16[2,256,1024]{2,1,0:T(8,128)(2,1)}, bf16[2,256,1024]{2,1,0:T(8,128)(2,1)}, u32[]{:S(2)}, u32[]{:S(2)}) collective-permute-start(bf16[2,256,1024]{2,1,0:T(8,128)(2,1)} %fusion.8), channel_id=1, source_target_pairs={{0,2},{1,3},{2,0},{3,1},{4,6},{5,7},{6,4},{7,5},{8,10},{9,11},{10,... | collective-permute-start | bytes 3145736 | tf_op jit(solution)/shard_map/ppermute | solution.py:419
  379.1 3.8 copy-start.16
  379.1 3.8 copy-start.17
  382.9 8.5 %copy-start.4 = (bf16[2,1024,1024]{2,1,0:T(8,128)(2,1)S(1)}, bf16[2,1024,1024]{2,1,0:T(8,128)(2,1)}, u32[]{:S(2)}) copy-start(bf16[2,1024,1024]{2,1,0:T(8,128)(2,1)} %copy-done.3) | copy-start | bytes 12582916
  395.0 4.8 copy-start.2
  396.7 4.6 copy-start.20
  397.7 22.3 %collective-permute-start.27 = (bf16[4,144,768]{2,1,0:T(8,128)(2,1)}, bf16[4,144,768]{2,1,0:T(8,128)(2,1)}, u32[]{:S(2)}, u32[]{:S(2)}) collective-permute-start(bf16[4,144,768]{2,1,0:T(8,128)(2,1)} %dynamic-slice_bitcast_fusion), channel_id=1, source_target_pairs={{0,4},{4,0},{8,12},{12,8},{16,20},{20,16},{24,28},{28,24},{1,5},{5... | collective-permute-start | bytes 2654216 | tf_op jit(solution)/shard_map/ppermute | solution.py:419
  401.3 22.3 %collective-permute-start.25 = (bf16[2,256,1024]{2,1,0:T(8,128)(2,1)}, bf16[2,256,1024]{2,1,0:T(8,128)(2,1)}, u32[]{:S(2)}, u32[]{:S(2)}) collective-permute-start(bf16[2,256,1024]{2,1,0:T(8,128)(2,1)} %get-tuple-element.150), channel_id=1, source_target_pairs={{0,1},{1,0},{2,3},{3,2},{4,5},{5,4},{6,7},{7,6},{8,9},{9,8},{10,11... | collective-permute-start | bytes 3145736 | tf_op jit(solution)/shard_map/ppermute | solution.py:419
  423.6 11.9 %collective-permute-start.28 = (bf16[2,144,768]{2,1,0:T(8,128)(2,1)}, bf16[2,144,768]{2,1,0:T(8,128)(2,1)}, u32[]{:S(2)}, u32[]{:S(2)}) collective-permute-start(bf16[2,144,768]{2,1,0:T(8,128)(2,1)} %fusion.21), channel_id=1, source_target_pairs={{0,8},{4,12},{8,0},{12,4},{16,24},{20,28},{24,16},{28,20},{1,9},{5... | collective-permute-start | bytes 1327112 | tf_op jit(solution)/shard_map/ppermute | solution.py:419
  426.5 24.9 %collective-permute-start.26 = (bf16[2,256,1024]{2,1,0:T(8,128)(2,1)}, bf16[2,256,1024]{2,1,0:T(8,128)(2,1)}, u32[]{:S(2)}, u32[]{:S(2)}) collective-permute-start(bf16[2,256,1024]{2,1,0:T(8,128)(2,1)} %add_convert_fusion), channel_id=1, source_target_pairs={{0,2},{1,3},{2,0},{3,1},{4,6},{5,7},{6,4},{7,5},{8,10},{9,11},{10,... | collective-permute-start | bytes 3145736 | tf_op jit(solution)/shard_map/ppermute | solution.py:419
  438.5 11.8 %collective-permute-start.29 = (bf16[1,144,768]{2,1,0:T(8,128)(2,1)}, bf16[1,144,768]{2,1,0:T(8,128)(2,1)S(1)}, u32[]{:S(2)}, u32[]{:S(2)}) collective-permute-start(bf16[1,144,768]{2,1,0:T(8,128)(2,1)} %dynamic-slice_convert_fusion.1), channel_id=1, source_target_pairs={{0,16},{4,20},{8,24},{12,28},{16,0},{20,4},{24,8},{28,12},{1,17},{... | collective-permute-start | bytes 663560 | tf_op jit(solution)/shard_map/ppermute | solution.py:419
  440.8 40.5 %collective-permute-start.24 = (bf16[2,256,1024]{2,1,0:T(8,128)(2,1)}, bf16[2,256,1024]{2,1,0:T(8,128)(2,1)}, u32[]{:S(2)}, u32[]{:S(2)}) collective-permute-start(bf16[2,256,1024]{2,1,0:T(8,128)(2,1)} %get-tuple-element.149), channel_id=1, source_target_pairs={{0,1},{1,0},{2,3},{3,2},{4,5},{5,4},{6,7},{7,6},{8,9},{9,8},{10,11... | collective-permute-start | bytes 3145736 | tf_op jit(solution)/shard_map/ppermute | solution.py:419
  481.3 3.1 copy-start.6
  481.3 3.5 copy-start.7
  481.3 3.7 copy-start.14
  489.0 22.3 %collective-permute-start.30 = (bf16[128,3456]{1,0:T(8,128)(2,1)}, bf16[128,3456]{1,0:T(8,128)(2,1)S(1)}, u32[]{:S(2)}, u32[]{:S(2)}) collective-permute-start(bf16[128,3456]{1,0:T(8,128)(2,1)} %reduce-scatter.2.cloned.1.call-done), channel_id=1, source_target_pairs={{0,1},{1,0},{2,3},{3,2},{4,5},{5,4},{6,7},{7,6},{8,9},{9,8},{10,11... | collective-permute-start | bytes 2654216 | tf_op jit(solution)/shard_map/ppermute | solution.py:419
  489.4 21.9 %collective-permute-start.31 = (bf16[128,3456]{1,0:T(8,128)(2,1)}, bf16[128,3456]{1,0:T(8,128)(2,1)S(1)}, u32[]{:S(2)}, u32[]{:S(2)}) collective-permute-start(bf16[128,3456]{1,0:T(8,128)(2,1)} %reduce-scatter.2.cloned.1.call-done), channel_id=1, source_target_pairs={{0,2},{1,3},{2,0},{3,1},{4,6},{5,7},{6,4},{7,5},{8,10},{9,11},{10,... | collective-permute-start | bytes 2654216 | tf_op jit(solution)/shard_map/ppermute | solution.py:419
  511.3 2.4 collective-permute-start.32
  534.1 3.1 copy-start.1
  (16 other events, 28.0 us)
Sparse Core Ops, SparseCore 0:
  14.3 139.8 all-gather.2
  285.7 130.5 reduce-scatter.1

commit v4 on v3

--- a/solution.py
+++ b/solution.py
@@ -6,6 +6,7 @@
 from jax.experimental import pallas as pl
 from jax.experimental.pallas import tpu as pltpu
 from jax.sharding import PartitionSpec as P
+
 
 HD = 64
 
@@ -414,7 +415,7 @@
     return [1 << i for i in range(count.bit_length() - 1)]
 
 
-def swap(values, bit, count, axis="seq"):
+def swap(values, bit, axis="seq"):
     total = lax.axis_size(axis)
     return lax.ppermute(values, axis, [(i, i ^ bit) for i in range(total)])
 
@@ -428,7 +429,7 @@
     for bit in reversed(bits_of(count)):
         for at in list(blocks):
             sent = blocks[at] if at == 0 or hold is None else after(blocks[at], *hold)
-            blocks[at | bit] = swap(sent, bit, count)
+            blocks[at | bit] = swap(sent, bit)
     return blocks
 
 
@@ -439,46 +440,44 @@
         kept = {}
         for at in blocks:
             if not at & bit:
-                arrived = swap(blocks[at | bit].astype(jnp.bfloat16), bit, count)
+                arrived = swap(blocks[at | bit].astype(jnp.bfloat16), bit)
                 kept[at] = blocks[at].astype(jnp.float32) + arrived.astype(jnp.float32)
         blocks = kept
     return blocks[0], blocks[bits[-1]].astype(jnp.bfloat16)
 
 
 def last_swap(sent, count):
-    return swap(sent, bits_of(count)[-1], count).astype(jnp.float32)
+    return swap(sent, bits_of(count)[-1])
 
 
 def scatter_blocks(blocks, count):
     kept, sent = scatter_sums(blocks, count)
-    return kept + last_swap(sent, count)
-
-
-def gather_rows(block, count):
-    own = lax.axis_index("fsdp")
-    held = [(0, block)]
-    stacked = block[None]
-    for bit in reversed(bits_of(count)):
-        arrived = swap(stacked, bit, count, "fsdp")
-        held = held + [(at | bit, arrived[i]) for i, (at, _) in enumerate(held)]
-        stacked = jnp.concatenate([stacked, arrived], axis=0)
-    rows, width = block.shape
-    whole = jnp.zeros((count * rows, width), block.dtype)
-    for at, piece in held:
-        whole = lax.dynamic_update_slice(whole, piece, ((own ^ at) * rows, 0))
+    return kept + last_swap(sent, count).astype(jnp.float32)
+
+
+def exchange(pieces, own, count, axis, whole):
+    rows, width = pieces.shape[1:]
+    for at in range(count):
+        piece = lax.dynamic_index_in_dim(pieces, own ^ at, axis=0, keepdims=False)
+        if at:
+            piece = swap(piece, at)
+        start = (own ^ at) * (rows, width)[axis]
+        whole = lax.dynamic_update_slice(whole, piece, (start, 0) if axis == 0 else (0, start))
     return whole
 
 
-def scatter_rows(sums, count):
+def scatter_rows(sums, count, waiting):
     own = lax.axis_index("fsdp")
     _, rows, width = sums.shape
     for bit in bits_of(count):
         mine = (own & bit) // bit
         split = sums.reshape(-1, 2, rows, width)
         pick = lambda at: lax.dynamic_index_in_dim(split, at, axis=1, keepdims=False)
-        arrived = swap(pick(1 - mine).astype(jnp.bfloat16), bit, count, "fsdp")
+        arrived = swap(pick(1 - mine).astype(jnp.bfloat16), bit, "fsdp")
+        if bit == 1:
+            arrived, waiting = lax.optimization_barrier((arrived, waiting))
         sums = pick(mine).astype(jnp.float32) + arrived.astype(jnp.float32)
-    return sums.reshape(rows, width).astype(jnp.bfloat16)
+    return sums.reshape(rows, width).astype(jnp.bfloat16), waiting
 
 
 def in_order(blocks, own, count):
@@ -512,7 +511,7 @@
     )
 
 
-def per_device(
+def step(
     fsdp,
     seq,
     tokens,
@@ -555,7 +554,7 @@
         ],
         axis=1,
     )
-    first_all = gather_rows(first, fsdp)
+    first_all = lax.all_gather(first, "fsdp", axis=0, tiled=True)
     qkv_width = q_width + 2 * kv_width
     w_qkv = first_all[:, :qkv_width]
     out_cols = first_all[:, qkv_width : qkv_width + o_width]
@@ -570,13 +569,18 @@
     second = jnp.concatenate(
         [pick(w_gate), pick(w_up), fold_rows(down_own, part)], axis=1
     )
-    second_all = lax.all_gather(second, "fsdp", axis=0, tiled=True)
+    second_all = lax.all_gather(after(second, first_all), "fsdp", axis=0, tiled=True)
     down_w = unfold_rows(second_all[:, 2 * local :].reshape(fsdp, part, local), units)
     down_w = down_w.reshape(local, width)
 
-    token_blocks = gather_blocks(tokens, seq)
+    high = bits_of(seq)[-1]
+    far_tokens = swap(tokens, high)
+    token_blocks = gather_blocks(tokens, seq // 2)
+    far_blocks = gather_blocks(far_tokens, seq // 2)
+    token_blocks |= {at | high: far_blocks[at] for at in far_blocks}
     inputs_all = in_order(token_blocks, own, seq)
-    out_w = lax.all_to_all(out_cols, "seq", split_axis=0, concat_axis=1, tiled=True)
+    out_pieces = out_cols.reshape(seq, q_width, o_width)
+    out_w = exchange(out_pieces, own, seq, 1, jnp.zeros((q_width, width), bf16))
 
     inputs_all32 = inputs_all.astype(f32)
     scale_all = rms_scale(inputs_all32)
@@ -586,6 +590,7 @@
     qkv_raw = dot(flat_normed, w_qkv).reshape(batch, length, qkv_width)
     tables = head_tables(length, qk_gain)
     query_low, key_low, mixed = attend(qkv_raw, tables)
+    mixed, out_w = lax.optimization_barrier((mixed, out_w))
     flat_mixed = mixed.reshape(count, q_width)
     branch = dot(flat_mixed, out_w).astype(bf16).reshape(batch, length, width)
     cot_blocks = gather_blocks(after(cotangent, *token_blocks.values()), seq, (mixed,))
@@ -600,8 +605,7 @@
     normed_two = (middle * scale_two * ffn_full).astype(bf16)
     flat = lambda values: values.reshape(batch * rows, width)
     half = seq // 2
-    high = bits_of(seq)[-1]
-    opposite = swap(normed_two, high, seq)
+    opposite = swap(normed_two, high)
     near_blocks = gather_blocks(normed_two, half)
     near = jnp.concatenate([flat(near_blocks[at]) for at in range(half)], axis=0)
     *kept, result_near, back_near = ffn(near, cot_all, second_all, down_w, 0, None)
@@ -630,27 +634,32 @@
         [grad_gate, grad_up, grad_down], axis=1
     )
     two_arrived, ffn_sums = lax.optimization_barrier((two_arrived, ffn_sums))
-    grad_two = two_kept + two_arrived
+    grad_two = two_kept + two_arrived.astype(f32)
     grad_middle_norm, grad_ffn_gain = norm_back(grad_two, middle, scale_two, ffn_full)
     grad_middle = cotangent.astype(f32) + grad_middle_norm
     grad_branch = grad_middle.astype(bf16)
-    branch_blocks = gather_blocks(grad_branch, seq)
+    hat_low = after(inputs_all, grad_branch).astype(f32) * scale_all
+    hat_low = hat_low.astype(bf16)
+    result_kept, result_sent = scatter_sums(
+        xor_blocks(*after((result_near, result_far), two_sent)), seq
+    )
+    result_kept = middle + result_kept
+    branch_blocks = gather_blocks(grad_branch, seq, (hat_low, result_kept, result_sent))
     ffn_share = lax.psum_scatter(ffn_sums, "fsdp", scatter_dimension=0, tiled=True)
-    result_parts, _ = lax.optimization_barrier(
-        ((result_near, result_far), tuple(branch_blocks.values()))
-    )
-    result = (middle + scatter_blocks(xor_blocks(*result_parts), seq)).astype(bf16)
+    result_sent = after(result_sent, *branch_blocks.values())
+    result = (result_kept + last_swap(result_sent, seq).astype(f32)).astype(bf16)
 
     branch_all = in_order(branch_blocks, own, seq).reshape(count, width)
     grad_out = t_dot(flat_mixed, branch_all).astype(bf16)
-    grad_out_cols = lax.all_to_all(grad_out, "seq", split_axis=1, concat_axis=0, tiled=True)
+    out_pieces = jnp.swapaxes(grad_out.reshape(q_width, seq, o_width), 0, 1)
+    grad_out_cols = exchange(out_pieces, own, seq, 0, jnp.zeros((width, o_width), bf16))
     grad_mixed = dot_t(branch_all, out_w).astype(bf16).reshape(batch, length, q_width)
     grad_qkv, gain_sums = attend_back(query_low, key_low, qkv_raw, grad_mixed, tables)
     grad_qkv, result = lax.optimization_barrier((grad_qkv, result))
     grad_qkv = grad_qkv.reshape(count, qkv_width)
     normed_back = dot_t(grad_qkv, w_qkv)
     normed_back_low = normed_back.astype(bf16).reshape(batch, length, width)
-    grad_attn_gain = jnp.sum(normed_back * hat_all.reshape(count, width), axis=0)
+    grad_attn_gain = jnp.sum(normed_back * hat_low.reshape(count, width).astype(f32), axis=0)
     normed_kept, normed_sent = scatter_sums(from_order(normed_back_low, own, seq), seq)
     normed_arrived = last_swap(normed_sent, seq)
 
@@ -667,13 +676,12 @@
     ).astype(bf16)
     gain_row = jnp.pad(gain_row[:, None, :], ((0, 0), (0, 15), (0, last_width - gain_row.shape[1])))
     last = jnp.concatenate([last.reshape(fsdp, part, last_width), gain_row], axis=1)
-    last_share = scatter_rows(last, fsdp)
-    normed_arrived, last_share = lax.optimization_barrier((normed_arrived, last_share))
-    grad_normed = normed_kept + normed_arrived
+    last_share, ffn_share = scatter_rows(last, fsdp, ffn_share)
+    last_shares = lax.all_gather(last_share, "seq", axis=0, tiled=False)
+    share_blocks = gather_blocks(ffn_share, seq)
+    grad_normed = normed_kept + after(normed_arrived, last_shares).astype(f32)
     inputs_norm, _ = norm_back(grad_normed, inputs, rms_scale(inputs), attn_full)
     grad_tokens = grad_middle + inputs_norm
-    last_shares = lax.all_gather(last_share, "seq", axis=0, tiled=False).astype(f32)
-    share_blocks = gather_blocks(after(ffn_share, last_shares), seq)
     ffn_shares = jnp.zeros((seq,) + ffn_share.shape, bf16)
     for at in range(seq):
         ffn_shares = lax.dynamic_update_slice(
@@ -685,10 +693,12 @@
         return jnp.transpose(split, (1, 2, 0, 3)).reshape(part, fsdp * seq * units)
 
     def side_by_side(piece):
-        return jnp.transpose(piece, (1, 0, 2)).reshape(part, -1)
-
-    shard_gate = unpick(ffn_shares[:, :, :local]).astype(f32)
-    shard_up = unpick(ffn_shares[:, :, local : 2 * local]).astype(f32)
+        return jnp.concatenate([piece[at] for at in range(seq)], axis=1).astype(f32)
+
+    shard_gate, shard_up = lax.optimization_barrier(
+        (unpick(ffn_shares[:, :, :local]), unpick(ffn_shares[:, :, local : 2 * local]))
+    )
+    shard_gate, shard_up = shard_gate.astype(f32), shard_up.astype(f32)
     shard_down = unfold_rows(ffn_shares[:, :, 2 * local :], units).reshape(seq * units, width)
     shard_down = shard_down.astype(f32)
     top = last_shares[:, :part]
@@ -696,7 +706,7 @@
     shard_key = side_by_side(top[:, :, q_width : q_width + kv_width])
     shard_value = side_by_side(top[:, :, q_width + kv_width : qkv_width])
     shard_out = side_by_side(top[:, :, qkv_width:])
-    gains = jnp.sum(last_shares[:, part], axis=0)
+    gains = jnp.sum(last_shares[:, part].astype(f32), axis=0)
     gain_total = gains[: 2 * HD].reshape(2, HD)
     return (
         result,
@@ -730,7 +740,7 @@
         P("fsdp", "seq", None),
     )
     return jax.shard_map(
-        functools.partial(per_device, mesh.shape["fsdp"], mesh.shape["seq"]),
+        functools.partial(step, mesh.shape["fsdp"], mesh.shape["seq"]),
         mesh=mesh,
         in_specs=placed,
         out_specs=(

time: 554 us -> 499 us (0.901)
  waiting for transfers between devices: 190 us -> 161 us
  local copies, waits for them, and re-layouts: 86.9 us -> 68.1 us
  other arithmetic: 71.7 us -> 60.2 us
  blocking collectives: 21.2 us -> 29.6 us
  starting transfers between devices: 27.6 us -> 21.1 us
    ppermute x33 -> x36, waiting for transfers between devices: 190 us -> 115 us  [swap(): return lax.ppermute(values, axis, [(i, i ^ bit) for i in range(total)])]
    all_gather x1 -> x2, waiting for transfers between devices: 0.01 us -> 45.4 us  [the longest x1 41.5 us: step(): first_all = lax.all_gather(first, 'fsdp', axis=0, tiled=True)]
    all_gather x1, blocking collectives: 8.73 us -> 29.6 us  [step(): last_shares = lax.all_gather(last_share, 'seq', axis=0, tiled=False)]
    convert_element_type x6 -> x2, local copies, waits for them, and re-layouts: 14.2 us -> 0.84 us  [scatter_rows(): arrived = swap(pick(1 - mine).astype(jnp.bfloat16), bit, 'fsdp')]
    all_to_all x1 -> x0, blocking collectives: 12.5 us -> none  [per_device(): lax.all_to_all(out_cols, 'seq', split_axis=0, concat_axis=1, tiled=True)]
    unnamed x102 -> x89, local copies, waits for them, and re-layouts: 32.1 us -> 20.7 us
    transpose x6 -> x2, local copies, waits for them, and re-layouts: 9.19 us -> 0.17 us  [unpick(): return jnp.transpose(split, (1, 2, 0, 3)).reshape(part, fsdp * seq * units)]
    concatenate x2 -> x6, local copies, waits for them, and re-layouts: 0.03 us -> 6.95 us  [the longest x4 6.27 us: step(): jnp.concatenate([last.reshape(fsdp, part, last_width), gain_row], axis=1)]
  transfers between devices with their start and end apart: 36 -> 39, of which waited for: 16 -> 17; matrix products, arithmetic and copies ran while one was open for 28% -> 30% of each run, Pallas kernels for 12% -> 13%
where the time goes in v4:
time: 499 us; the launch traced here: 489 us
  waiting for transfers between devices  161 us (32%)
  Pallas kernels  87.9 us (18%)
  local copies, waits for them, and re-layouts  68.1 us (14%)
  other arithmetic  60.2 us (12%)
  matrix products  46.2 us (9%)
  blocking collectives  29.6 us (6%)
  starting transfers between devices  21.1 us (4%)
  between operations  15.2 us (3%)
    ppermute x36, waiting for transfers between devices, swap(): return lax.ppermute(values, axis, [(i, i ^ bit) for i in range(total)])  115 us
    pallas_call x2, Pallas kernels, ffn(): pl.pallas_call(ffn_kernel, grid=(rows // step,), in_specs=[here(width), t...  44.3 us
    all_gather x1, waiting for transfers between devices, step(): first_all = lax.all_gather(first, 'fsdp', axis=0, tiled=True)  41.5 us
    dot_general x5, matrix products, t_dot(): lax.dot_general(left, right, (((0,), (0,)), ((), ())), preferred_element_...  29.6 us
    all_gather x1, blocking collectives, step(): last_shares = lax.all_gather(last_share, 'seq', axis=0, tiled=False)  29.6 us
    pallas_call x1, Pallas kernels, attend_back(): pl.pallas_call(attend_back_kernel, grid=(batch, groups), in_specs=[own_co...  26.5 us
    ppermute x36, starting transfers between devices, swap(): return lax.ppermute(values, axis, [(i, i ^ bit) for i in range(total)])  21 us
    unnamed x89, local copies, waits for them, and re-layouts  20.7 us
  transfers between devices with their start and end apart: 39, of which 17 were waited for; matrix products, arithmetic and copies ran while one was open for 30% of the time, Pallas kernels for 13%

profile of v4, /device:TPU:0, one launch (start us, length us, event | category | flops | bytes accessed | tf_op | source)
XLA Modules:
  0.0 488.8 jit_solution(4715769684645739605)
XLA Ops:
  12.2 1.7 copy.122
  13.9 1.7 copy.123
  19.9 41.5 %all-gather.3.cloned.1.call-done = bf16[1024,896]{1,0:T(8,128)(2,1)} async-done(((bf16[128,896]{1,0:T(8,128)(2,1)}), bf16[1024,896]{1,0:T(8,128)(2,1)}) %all-gather.3.cloned.1.call-update) | async-done | bytes 1835024 | tf_op jit(solution)/shard_map/all_gather | solution.py:557
  61.5 1.5 collective-permute-start.1
  63.6 21.2 %collective-permute-done.1 = bf16[2,256,1024]{2,1,0:T(8,128)(2,1)} collective-permute-done((bf16[2,256,1024]{2,1,0:T(8,128)(2,1)S(1)}, bf16[2,256,1024]{2,1,0:T(8,128)(2,1)}, u32[]{:S(2)}, u32[]{:S(2)}) %collective-permute-start.1) | collective-permute-done | bytes 1048608 | tf_op jit(solution)/shard_map/ppermute | solution.py:420
  85.8 2.2 fusion.29
  89.3 1.4 constant_dynamic-update-slice_fusion.12
  92.1 1.5 collective-permute-start.7
  96.1 2.0 copy-done.31
  100.4 4.5 fusion.6.q_ref.k_ref.v_ref
  104.9 17.1 %attend.1 = (bf16[2,1024,256]{2,1,0:T(8,128)(2,1)}, bf16[2,1024,128]{2,1,0:T(8,128)(2,1)}, bf16[2,1024,256]{2,1,0:T(8,128)(2,1)}) custom-call(f32[2,1024,512]{2,1,0:T(8,128)} %fusion.6.q_ref.k_ref.v_ref, f32[2,1024,512]{2,1,0:T(8,128)} %fusion.6.q_ref.k_ref.v_ref, f32[2,1024,512]{2,1,0:T(8,128)} %fusion.6.q_ref.k_ref.v_ref, ...), custom_call_target="tpu_custom_call" | custom-call | flops 2147483648 | bytes 8388608 | tf_op jit(solution)/shard_map/attend/pallas_call | solution.py:271
  126.1 3.6 pad_maximum_fusion.1.cot_ref
  130.6 2.1 collective-permute-done.10
  133.1 1.5 collective-permute-start.11
  134.7 24.0 %collective-permute-done.11 = bf16[2,256,1024]{2,1,0:T(8,128)(2,1)S(1)} collective-permute-done((bf16[2,256,1024]{2,1,0:T(8,128)(2,1)S(1)}, bf16[2,256,1024]{2,1,0:T(8,128)(2,1)S(1)}, u32[]{:S(2)}, u32[]{:S(2)}) %collective-permute-start.11) | collective-permute-done | bytes 1048608 | tf_op jit(solution)/shard_map/ppermute | solution.py:420
  160.6 1.5 collective-permute-start.14
  162.1 1.4 collective-permute-done.12
  164.4 2.8 pad_maximum_fusion.4.two_ref
  167.2 4.0 all-gather.5.cloned.1.call-done.gate_w.up_w
  171.2 1.8 slice.228
  173.0 1.6 slice.229
  176.5 3.2 pad_maximum_fusion.3
  179.7 22.1 %ffn.2 = (bf16[2048,1152]{1,0:T(8,128)(2,1)}, bf16[2048,1152]{1,0:T(8,128)(2,1)}, bf16[2048,1152]{1,0:T(8,128)(2,1)}, bf16[1024,1024]{1,0:T(8,128)(2,1)}, bf16[1024,1024]{1,0:T(8,128)(2,1)}) custom-call(bf16[1024,1024]{1,0:T(8,128)(2,1)} %pad_maximum_fusion.4.two_ref, bf16[2048,1024]{1,0:T(8,128)(2,1)} %pad_maximum_fusion.1.cot_ref, ...), custom_call_target="tpu_custom_call" | custom-call | flops 14495514624 | bytes 22544384 | tf_op jit(solution)/shard_map/ffn/pallas_call | solution.py:374
  202.0 2.9 collective-permute-done.15
  205.8 2.8 pad_maximum_fusion.5.two_ref
  208.6 22.2 %ffn.3 = (bf16[2048,1152]{1,0:T(8,128)(2,1)}, bf16[2048,1152]{1,0:T(8,128)(2,1)}, bf16[2048,1152]{1,0:T(8,128)(2,1)}, bf16[1024,1024]{1,0:T(8,128)(2,1)}, bf16[1024,1024]{1,0:T(8,128)(2,1)}) custom-call(bf16[1024,1024]{1,0:T(8,128)(2,1)} %pad_maximum_fusion.5.two_ref, ...), custom_call_target="tpu_custom_call", output_to_operand_aliasing={{0}: (5, {}), {1}: (6, {}), {2}: (7, {})} | custom-call | flops 14495514624 | bytes 22544384 | tf_op jit(solution)/shard_map/ffn/pallas_call | solution.py:374
  230.8 1.9 fusion.38
  232.9 2.5 collective-permute-done.16
  235.4 1.4 fusion.15
  236.8 1.5 collective-permute-start.17
  238.3 7.8 %convolution_convert_fusion.2 = bf16[1024,1152]{1,0:T(8,128)(2,1)S(1)} fusion(bf16[2048,1152]{1,0:T(8,128)(2,1)S(1)} %copy-done.35, bf16[512,1024]{1,0:T(8,128)(2,1)S(1)} %bitcast.229, bf16[512,1024]{1,0:T(8,128)(2,1)} %bitcast.28, bf16[512,1024]{1,0:T(8,128)(2,1)S(1)} %bitcast.225, bf16[512,1024]{1,0:T(8,128)(2,1)} %bitcast.14), kind=kOutput, calls=%fused_computation.13 | convolution fusion | flops 4849795072 | bytes 11272192 | tf_op jit(solution)/shard_map/dot_general | solution.py:509
  246.2 7.4 %convolution_convert_fusion.1 = bf16[1024,1152]{1,0:T(8,128)(2,1)S(1)} fusion(bf16[2048,1152]{1,0:T(8,128)(2,1)S(1)} %bitcast.247, bf16[512,1024]{1,0:T(8,128)(2,1)S(1)} %bitcast.230, bf16[512,1024]{1,0:T(8,128)(2,1)} %bitcast.28, bf16[512,1024]{1,0:T(8,128)(2,1)S(1)} %bitcast.226, bf16[512,1024]{1,0:T(8,128)(2,1)} %bitcast.14), kind=kOutput, calls=%fused_computation.12 | convolution fusion | flops 4849795072 | bytes 11272192 | tf_op jit(solution)/shard_map/dot_general | solution.py:509
  253.6 5.4 %convolution_convert_fusion = bf16[1152,1024]{1,0:T(8,128)(2,1)S(1)} fusion(bf16[2048,1152]{1,0:T(8,128)(2,1)S(1)} %bitcast.245, bf16[2048,1024]{1,0:T(8,128)(2,1)S(1)} %copy-done.17), kind=kOutput, calls=%fused_computation.11 | convolution fusion | flops 4833017856 | bytes 11272192 | tf_op jit(solution)/shard_map/dot_general | solution.py:509
  259.3 3.4 pad_maximum_fusion
  262.8 1.9 fusion.37
  267.4 1.5 collective-permute-done.20
  268.9 4.7 multiply_reduce_fusion
  274.8 4.0 constant_dynamic-update-slice_fusion.6
  278.8 1.9 copy-done.4
  283.2 2.7 multiply_convert_fusion
  285.9 20.3 %collective-permute-done.19 = bf16[2,256,1024]{2,1,0:T(8,128)(2,1)S(1)} collective-permute-done((bf16[2,256,1024]{2,1,0:T(8,128)(2,1)}, bf16[2,256,1024]{2,1,0:T(8,128)(2,1)S(1)}, u32[]{:S(2)}, u32[]{:S(2)}) %collective-permute-start.19) | collective-permute-done | bytes 1048608 | tf_op jit(solution)/shard_map/ppermute | solution.py:420
  306.2 2.3 constant_dynamic-update-slice_fusion.5
  311.6 3.6 fusion.19
  316.5 4.6 convolution_convert_fusion.4
  321.1 26.5 %attend_back.1 = (bf16[2,1024,512]{2,1,0:T(8,128)(2,1)}, f32[8,128]{1,0:T(8,128)}) custom-call(bf16[2,1024,256]{2,1,0:T(8,128)(2,1)} %get-tuple-element.52.low_q_ref, bf16[2,1024,128]{2,1,0:T(8,128)(2,1)} %get-tuple-element.53.low_k_ref, f32[2,1024,512]{2,1,0:T(8,128)} %fusion.6.q_ref.k_ref.v_ref, f32[2,1024,512]{2,1,0:T(8,128)} %fusion.6.q_ref.k_ref.v_ref, ...), custom_call_target="tpu_custom_call" | custom-call | flops 5368709120 | bytes 12582912 | tf_op jit(solution)/shard_map/attend_back/pallas_call | solution.py:306
  350.2 1.6 bitcast_dynamic-update-slice_fusion.4
  355.0 3.0 collective-permute-done.29
  358.7 2.5 add_convert_fusion.1
  361.2 6.2 %fusion.3 = (bf16[1024]{0:T(1024)(128)(2,1)S(1)}, bf16[2048,1024]{1,0:T(8,128)(2,1)}) fusion(bf16[2,1024,1024]{2,1,0:T(8,128)(2,1)S(1)} %copy-done.16, bf16[2048,512]{1,0:T(8,128)(2,1)} %bitcast.242, bf16[1024,896]{1,0:T(8,128)(2,1)} %all-gather.3.cloned.1.call-done), kind=kOutput, calls=%fused_computation.6 | convolution fusion | flops 2155871232 | bytes 11536384 | tf_op jit(solution)/shard_map/dot_general | solution.py:503
  367.6 5.5 %bitcast_convert_fusion = bf16[1024,512]{0,1:T(8,128)(2,1)S(1)} fusion(bf16[2,1024,512]{2,1,0:T(8,128)(2,1)} %get-tuple-element.84, bf16[2,1024,1024]{2,1,0:T(8,128)(2,1)} %copy-done.2, f32[1024]{0:T(1024)S(1)} %get-tuple-element.143, f32[2,1024]{1,0:T(2,128)S(1)} %add_rsqrt_fusion), kind=kOutput, calls=%fused_computation.40 | convolution fusion | flops 2156396544 | bytes 7352320 | tf_op jit(solution)/shard_map/dot_general | solution.py:509
  374.3 2.6 concatenate.103
  376.8 3.6 copy.135
  381.8 3.0 constant_dynamic-slice_fusion.1
  384.8 18.5 %collective-permute-done.30 = bf16[4,144,768]{2,1,0:T(8,128)(2,1)} collective-permute-done((bf16[4,144,768]{2,1,0:T(8,128)(2,1)}, bf16[4,144,768]{2,1,0:T(8,128)(2,1)}, u32[]{:S(2)}, u32[]{:S(2)}) %collective-permute-start.30) | collective-permute-done | bytes 884768 | tf_op jit(solution)/shard_map/ppermute | solution.py:420
  407.2 2.0 add_convert_fusion
  411.5 6.7 %collective-permute-done.31 = bf16[2,144,768]{2,1,0:T(8,128)(2,1)S(1)} collective-permute-done((bf16[2,144,768]{2,1,0:T(8,128)(2,1)}, bf16[2,144,768]{2,1,0:T(8,128)(2,1)S(1)}, u32[]{:S(2)}, u32[]{:S(2)}) %collective-permute-start.31) | collective-permute-done | bytes 442400 | tf_op jit(solution)/shard_map/ppermute | solution.py:420
  418.4 1.8 collective-permute-start.32
  421.7 8.1 %collective-permute-done.32 = bf16[1,144,768]{2,1,0:T(8,128)(2,1)S(1)} collective-permute-done((bf16[1,144,768]{2,1,0:T(8,128)(2,1)S(1)}, bf16[1,144,768]{2,1,0:T(8,128)(2,1)S(1)}, u32[]{:S(2)}, u32[]{:S(2)}) %collective-permute-start.32) | collective-permute-done | bytes 221216 | tf_op jit(solution)/shard_map/ppermute | solution.py:420
  429.8 29.6 %all_gather.12 = bf16[4,144,768]{2,1,0:T(8,128)(2,1)S(1)} all-gather(bf16[1,144,768]{2,1,0:T(8,128)(2,1)S(1)} %add_convert_fusion.3), channel_id=1, replica_groups=mesh['fsdp'=8,'seq'=4] {'seq'}, dimensions={0}, use_global_device_ids=true | all-gather | bytes 1105920 | tf_op jit(solution)/shard_map/all_gather | solution.py:680
  463.6 2.1 fusion.8
  467.2 4.2 fusion.11
  474.9 1.8 bitcast_convert_fusion.1
  478.4 1.7 copy.142
  480.1 1.7 copy.143
  (239 shorter events, 68.3 us)
Async XLA Ops:
  7.2 11.7 %copy-start = (bf16[576,1024]{1,0:T(8,128)(2,1)S(1)}, bf16[576,1024]{1,0:T(8,128)(2,1)}, u32[]{:S(2)}) copy-start(bf16[576,1024]{1,0:T(8,128)(2,1)} %param.19) | copy-start | bytes 3538948
  7.2 54.2 %all-gather.3.cloned.1.call-start = ((), (), s32[]{:S(2)}) async-start(), calls=%async_computation.1 | async-start | bytes 2064384 | tf_op jit(solution)/shard_map/all_gather | solution.py:557
  12.1 159.1 %all-gather.5.cloned.1.call-start = ((), (), s32[]{:S(2)}) async-start(), calls=%async_computation.2 | async-start | bytes 7962624 | tf_op jit(solution)/shard_map/all_gather | solution.py:572
  16.4 45.0 %copy-start.5 = (bf16[2,256,1024]{2,1,0:T(8,128)(2,1)S(1)}, bf16[2,256,1024]{2,1,0:T(8,128)(2,1)}, u32[]{:S(2)}) copy-start(bf16[2,256,1024]{2,1,0:T(8,128)(2,1)} %param.12) | copy-start | bytes 3145732
  16.4 46.6 %copy-start.34 = (bf16[2,64]{1,0:T(2,128)(2,1)S(1)}, bf16[2,64]{1,0:T(2,128)(2,1)}, u32[]{:S(2)}) copy-start(bf16[2,64]{1,0:T(2,128)(2,1)} %param.22) | copy-start | bytes 772
  61.4 342.0 %reduce-scatter.2.cloned.1.call-start = ((), (), s32[]{:S(2)}) async-start(), calls=%async_computation.3 | async-start | bytes 7962624 | tf_op jit(solution)/shard_map/reduce_scatter | solution.py:648
  61.5 23.4 %collective-permute-start.1 = (bf16[2,256,1024]{2,1,0:T(8,128)(2,1)S(1)}, bf16[2,256,1024]{2,1,0:T(8,128)(2,1)}, u32[]{:S(2)}, u32[]{:S(2)}) collective-permute-start(bf16[2,256,1024]{2,1,0:T(8,128)(2,1)S(1)} %copy-done.5), channel_id=1, source_target_pairs={{0,2},{1,3},{2,0},{3,1},{4,6},{5,7},{6,4},{7,5},{8,10},{9,11},{10,... | collective-permute-start | bytes 3145736 | tf_op jit(solution)/shard_map/ppermute | solution.py:420
  63.0 26.3 %collective-permute-start = (bf16[2,256,1024]{2,1,0:T(8,128)(2,1)S(1)}, bf16[2,256,1024]{2,1,0:T(8,128)(2,1)}, u32[]{:S(2)}, u32[]{:S(2)}) collective-permute-start(bf16[2,256,1024]{2,1,0:T(8,128)(2,1)S(1)} %copy-done.5), channel_id=1, source_target_pairs={{0,1},{1,0},{2,3},{3,2},{4,5},{5,4},{6,7},{7,6},{8,9},{9,8},{10,11... | collective-permute-start | bytes 3145736 | tf_op jit(solution)/shard_map/ppermute | solution.py:420
  84.9 7.2 %collective-permute-start.2 = (bf16[2,256,1024]{2,1,0:T(8,128)(2,1)}, bf16[2,256,1024]{2,1,0:T(8,128)(2,1)}, u32[]{:S(2)}, u32[]{:S(2)}) collective-permute-start(bf16[2,256,1024]{2,1,0:T(8,128)(2,1)} %collective-permute-done.1), channel_id=1, source_target_pairs={{0,1},{1,0},{2,3},{3,2},{4,5},{5,4},{6,7},{7,6},{8,9},{9,8},{10,11... | collective-permute-start | bytes 3145736 | tf_op jit(solution)/shard_map/ppermute | solution.py:420
  92.1 30.8 %collective-permute-start.7 = (bf16[2,256,1024]{2,1,0:T(8,128)(2,1)S(1)}, bf16[2,256,1024]{2,1,0:T(8,128)(2,1)}, u32[]{:S(2)}, u32[]{:S(2)}) collective-permute-start(bf16[2,256,1024]{2,1,0:T(8,128)(2,1)S(1)} %copy-done.18), channel_id=1, source_target_pairs={{0,2},{1,3},{2,0},{3,1},{4,6},{5,7},{6,4},{7,5},{8,10},{9,11},{10,... | collective-permute-start | bytes 3145736 | tf_op jit(solution)/shard_map/ppermute | solution.py:420
  93.6 31.3 %collective-permute-start.6 = (bf16[2,256,1024]{2,1,0:T(8,128)(2,1)S(1)}, bf16[2,256,1024]{2,1,0:T(8,128)(2,1)}, u32[]{:S(2)}, u32[]{:S(2)}) collective-permute-start(bf16[2,256,1024]{2,1,0:T(8,128)(2,1)S(1)} %copy-done.18), channel_id=1, source_target_pairs={{0,1},{1,0},{2,3},{3,2},{4,5},{5,4},{6,7},{7,6},{8,9},{9,8},{10,11... | collective-permute-start | bytes 3145736 | tf_op jit(solution)/shard_map/ppermute | solution.py:420
  95.1 5.2 %copy-start.2 = (bf16[2,1024,1024]{2,1,0:T(8,128)(2,1)}, bf16[2,1024,1024]{2,1,0:T(8,128)(2,1)S(1)}, u32[]{:S(2)}) copy-start(bf16[2,1024,1024]{2,1,0:T(8,128)(2,1)S(1)} %constant_dynamic-update-slice_fusion.10) | copy-start | bytes 12582916
  98.1 23.9 %collective-permute-start.3 = (bf16[256,256]{1,0:T(8,128)(2,1)S(1)}, bf16[256,256]{1,0:T(8,128)(2,1)S(1)}, u32[]{:S(2)}, u32[]{:S(2)}) collective-permute-start(bf16[256,256]{1,0:T(8,128)(2,1)S(1)} %get-tuple-element.189), channel_id=1, source_target_pairs={{0,1},{1,0},{2,3},{3,2},{4,5},{5,4},{6,7},{7,6},{8,9},{9,8},{10,11... | collective-permute-start | bytes 393224 | tf_op jit(solution)/shard_map/ppermute | solution.py:420
  98.5 23.6 %collective-permute-start.4 = (bf16[256,256]{1,0:T(8,128)(2,1)S(1)}, bf16[256,256]{1,0:T(8,128)(2,1)S(1)}, u32[]{:S(2)}, u32[]{:S(2)}) collective-permute-start(bf16[256,256]{1,0:T(8,128)(2,1)S(1)} %get-tuple-element.188), channel_id=1, source_target_pairs={{0,2},{1,3},{2,0},{3,1},{4,6},{5,7},{6,4},{7,5},{8,10},{9,11},{10,... | collective-permute-start | bytes 393224 | tf_op jit(solution)/shard_map/ppermute | solution.py:420
  99.0 23.8 %collective-permute-start.5 = (bf16[256,256]{1,0:T(8,128)(2,1)S(1)}, bf16[256,256]{1,0:T(8,128)(2,1)S(1)}, u32[]{:S(2)}, u32[]{:S(2)}) collective-permute-start(bf16[256,256]{1,0:T(8,128)(2,1)S(1)} %get-tuple-element.187), channel_id=1, source_target_pairs={{0,3},{1,2},{2,1},{3,0},{4,7},{5,6},{6,5},{7,4},{8,11},{9,10},{10,... | collective-permute-start | bytes 393224 | tf_op jit(solution)/shard_map/ppermute | solution.py:420
  122.8 3.3 collective-permute-start.8
  130.0 28.7 %copy-start.6 = (bf16[2,256,1024]{2,1,0:T(8,128)(2,1)S(1)}, bf16[2,256,1024]{2,1,0:T(8,128)(2,1)}, u32[]{:S(2)}) copy-start(bf16[2,256,1024]{2,1,0:T(8,128)(2,1)} %param.12) | copy-start | bytes 3145732
  130.0 2.7 collective-permute-start.10
  130.4 4.2 collective-permute-start.9
  133.1 25.5 %collective-permute-start.11 = (bf16[2,256,1024]{2,1,0:T(8,128)(2,1)S(1)}, bf16[2,256,1024]{2,1,0:T(8,128)(2,1)S(1)}, u32[]{:S(2)}, u32[]{:S(2)}) collective-permute-start(bf16[2,256,1024]{2,1,0:T(8,128)(2,1)S(1)} %add_convert_fusion.2), channel_id=1, source_target_pairs={{0,2},{1,3},{2,0},{3,1},{4,6},{5,7},{6,4},{7,5},{8,10},{9,11},{10,... | collective-permute-start | bytes 3145736 | tf_op jit(solution)/shard_map/ppermute | solution.py:420
  160.6 2.9 collective-permute-start.12
  160.6 41.3 %collective-permute-start.14 = (bf16[2,256,1024]{2,1,0:T(8,128)(2,1)}, bf16[2,256,1024]{2,1,0:T(8,128)(2,1)}, u32[]{:S(2)}, u32[]{:S(2)}) collective-permute-start(bf16[2,256,1024]{2,1,0:T(8,128)(2,1)} %multiply_convert_fusion.1), channel_id=1, source_target_pairs={{0,2},{1,3},{2,0},{3,1},{4,6},{5,7},{6,4},{7,5},{8,10},{9,11},{10,... | collective-permute-start | bytes 3145736 | tf_op jit(solution)/shard_map/ppermute | solution.py:420
  201.9 2.9 collective-permute-start.15
  230.8 7.5 %copy-start.35 = (bf16[2048,1152]{1,0:T(8,128)(2,1)S(1)}, bf16[2048,1152]{1,0:T(8,128)(2,1)}, u32[]{:S(2)}) copy-start(bf16[2048,1152]{1,0:T(8,128)(2,1)} %get-tuple-element.71) | copy-start | bytes 14155780
  232.7 5.6 %copy-start.28 = (bf16[2,256,1024]{2,1,0:T(8,128)(2,1)S(1)}, bf16[2,256,1024]{2,1,0:T(8,128)(2,1)}, u32[]{:S(2)}) copy-start(bf16[2,256,1024]{2,1,0:T(8,128)(2,1)} %copy-done.27) | copy-start | bytes 3145732
  232.7 5.6 %copy-start.30 = (bf16[2,256,1024]{2,1,0:T(8,128)(2,1)S(1)}, bf16[2,256,1024]{2,1,0:T(8,128)(2,1)}, u32[]{:S(2)}) copy-start(bf16[2,256,1024]{2,1,0:T(8,128)(2,1)} %copy-done.29) | copy-start | bytes 3145732
  232.7 2.7 collective-permute-start.16
  235.4 10.7 %slice-start.2 = ((s8[4718592]{0:T(1024)(128)(4,1)}), s8[4194304]{0:T(1024)(128)(4,1)S(1)}, s32[]{:S(2)}) async-start(s8[4718592]{0:T(1024)(128)(4,1)} %bitcast.246), calls=%async_computation.6 | async-start | bytes 8388608
  236.8 25.9 %collective-permute-start.17 = (bf16[2,256,1024]{2,1,0:T(8,128)(2,1)}, bf16[2,256,1024]{2,1,0:T(8,128)(2,1)}, u32[]{:S(2)}, u32[]{:S(2)}) collective-permute-start(bf16[2,256,1024]{2,1,0:T(8,128)(2,1)} %fusion.15), channel_id=1, source_target_pairs={{0,2},{1,3},{2,0},{3,1},{4,6},{5,7},{6,4},{7,5},{8,10},{9,11},{10,... | collective-permute-start | bytes 3145736 | tf_op jit(solution)/shard_map/ppermute | solution.py:420
  238.3 7.9 %slice-start.3 = ((s8[4718592]{0:T(1024)(128)(4,1)}), s8[524288]{0:T(1024)(128)(4,1)S(1)}, s32[]{:S(2)}) async-start(s8[4718592]{0:T(1024)(128)(4,1)} %bitcast.246), calls=%async_computation.7 | async-start | bytes 1048576
  238.3 15.3 %slice-start = ((s8[4718592]{0:T(1024)(128)(4,1)}), s8[4194304]{0:T(1024)(128)(4,1)S(1)}, s32[]{:S(2)}) async-start(s8[4718592]{0:T(1024)(128)(4,1)} %bitcast.244), calls=%async_computation.4 | async-start | bytes 8388608
  246.2 7.4 %copy-start.17 = (bf16[2048,1024]{1,0:T(8,128)(2,1)S(1)}, bf16[2048,1024]{1,0:T(8,128)(2,1)}, u32[]{:S(2)}) copy-start(bf16[2048,1024]{1,0:T(8,128)(2,1)} %pad_maximum_fusion.1.cot_ref) | copy-start | bytes 12582916
  246.2 7.4 %slice-start.1 = ((s8[4718592]{0:T(1024)(128)(4,1)}), s8[524288]{0:T(1024)(128)(4,1)S(1)}, s32[]{:S(2)}) async-start(s8[4718592]{0:T(1024)(128)(4,1)} %bitcast.244), calls=%async_computation.5 | async-start | bytes 1048576
  264.7 2.7 collective-permute-start.13
  265.2 3.7 copy-start.10
  265.2 3.7 collective-permute-start.20
  266.5 15.3 %collective-permute-start.21 = (bf16[2,256,1024]{2,1,0:T(8,128)(2,1)S(1)}, bf16[2,256,1024]{2,1,0:T(8,128)(2,1)S(1)}, u32[]{:S(2)}, u32[]{:S(2)}) collective-permute-start(bf16[2,256,1024]{2,1,0:T(8,128)(2,1)S(1)} %bitcast.227), channel_id=1, source_target_pairs={{0,1},{1,0},{2,3},{3,2},{4,5},{5,4},{6,7},{7,6},{8,9},{9,8},{10,11... | collective-permute-start | bytes 3145736 | tf_op jit(solution)/shard_map/ppermute | solution.py:420
  274.8 8.4 %copy-start.3 = (bf16[2,1024,1024]{2,1,0:T(8,128)(2,1)S(1)}, bf16[2,1024,1024]{2,1,0:T(8,128)(2,1)}, u32[]{:S(2)}) copy-start(bf16[2,1024,1024]{2,1,0:T(8,128)(2,1)} %copy-done.2) | copy-start | bytes 12582916
  280.8 25.4 %collective-permute-start.19 = (bf16[2,256,1024]{2,1,0:T(8,128)(2,1)}, bf16[2,256,1024]{2,1,0:T(8,128)(2,1)S(1)}, u32[]{:S(2)}, u32[]{:S(2)}) collective-permute-start(bf16[2,256,1024]{2,1,0:T(8,128)(2,1)} %get-tuple-element.147), channel_id=1, source_target_pairs={{0,2},{1,3},{2,0},{3,1},{4,6},{5,7},{6,4},{7,5},{8,10},{9,11},{10,... | collective-permute-start | bytes 3145736 | tf_op jit(solution)/shard_map/ppermute | solution.py:420
  283.2 23.0 %collective-permute-start.18 = (bf16[2,256,1024]{2,1,0:T(8,128)(2,1)}, bf16[2,256,1024]{2,1,0:T(8,128)(2,1)}, u32[]{:S(2)}, u32[]{:S(2)}) collective-permute-start(bf16[2,256,1024]{2,1,0:T(8,128)(2,1)} %get-tuple-element.147), channel_id=1, source_target_pairs={{0,1},{1,0},{2,3},{3,2},{4,5},{5,4},{6,7},{7,6},{8,9},{9,8},{10,11... | collective-permute-start | bytes 3145736 | tf_op jit(solution)/shard_map/ppermute | solution.py:420
  306.2 3.4 collective-permute-start.22
  309.5 49.1 %collective-permute-start.23 = (bf16[2,256,1024]{2,1,0:T(8,128)(2,1)}, bf16[2,256,1024]{2,1,0:T(8,128)(2,1)}, u32[]{:S(2)}, u32[]{:S(2)}) collective-permute-start(bf16[2,256,1024]{2,1,0:T(8,128)(2,1)} %fusion.13), channel_id=1, source_target_pairs={{0,2},{1,3},{2,0},{3,1},{4,6},{5,7},{6,4},{7,5},{8,10},{9,11},{10,... | collective-permute-start | bytes 3145736 | tf_op jit(solution)/shard_map/ppermute | solution.py:420
  311.6 4.9 copy-start.23
  315.5 5.6 %copy-start.26 = (bf16[256,1024]{0,1:T(8,128)(2,1)}, bf16[256,1024]{0,1:T(8,128)(2,1)S(1)}, u32[]{:S(2)}) copy-start(bf16[256,1024]{0,1:T(8,128)(2,1)S(1)} %copy.146) | copy-start | bytes 1572868
  316.3 37.4 %collective-permute-start.27 = (bf16[256,256]{0,1:T(8,128)(2,1)}, bf16[256,256]{0,1:T(8,128)(2,1)S(1)}, u32[]{:S(2)}, u32[]{:S(2)}) collective-permute-start(bf16[256,256]{0,1:T(8,128)(2,1)} %get-tuple-element.186), channel_id=1, source_target_pairs={{0,1},{1,0},{2,3},{3,2},{4,5},{5,4},{6,7},{7,6},{8,9},{9,8},{10,11... | collective-permute-start | bytes 393224 | tf_op jit(solution)/shard_map/ppermute | solution.py:420
  321.1 37.6 %copy-start.9 = (f32[2,256,1024]{2,1,0:T(8,128)S(1)}, f32[2,256,1024]{2,1,0:T(8,128)}, u32[]{:S(2)}) copy-start(f32[2,256,1024]{2,1,0:T(8,128)} %get-tuple-element.161) | copy-start | bytes 6291460
  348.4 5.9 %collective-permute-start.28 = (bf16[256,256]{0,1:T(8,128)(2,1)}, bf16[256,256]{0,1:T(8,128)(2,1)S(1)}, u32[]{:S(2)}, u32[]{:S(2)}) collective-permute-start(bf16[256,256]{0,1:T(8,128)(2,1)} %get-tuple-element.185), channel_id=1, source_target_pairs={{0,2},{1,3},{2,0},{3,1},{4,6},{5,7},{6,4},{7,5},{8,10},{9,11},{10,... | collective-permute-start | bytes 393224 | tf_op jit(solution)/shard_map/ppermute | solution.py:420
  352.3 5.7 %collective-permute-start.29 = (bf16[256,256]{0,1:T(8,128)(2,1)S(1)}, bf16[256,256]{0,1:T(8,128)(2,1)S(1)}, u32[]{:S(2)}, u32[]{:S(2)}) collective-permute-start(bf16[256,256]{0,1:T(8,128)(2,1)S(1)} %get-tuple-element.184), channel_id=1, source_target_pairs={{0,3},{1,2},{2,1},{3,0},{4,7},{5,6},{6,5},{7,4},{8,11},{9,10},{10,... | collective-permute-start | bytes 393224 | tf_op jit(solution)/shard_map/ppermute | solution.py:420
  354.4 6.9 %copy-start.16 = (bf16[2,1024,1024]{2,1,0:T(8,128)(2,1)S(1)}, bf16[2,1024,1024]{2,1,0:T(8,128)(2,1)}, u32[]{:S(2)}) copy-start(bf16[2,1024,1024]{2,1,0:T(8,128)(2,1)} %multiply_convert_fusion) | copy-start | bytes 12582916
  361.2 6.2 %copy-start.33 = (bf16[1024]{0:T(1024)(128)(2,1)S(1)}, bf16[1024]{0:T(1024)(128)(2,1)}, u32[]{:S(2)}) copy-start(bf16[1024]{0:T(1024)(128)(2,1)} %get-tuple-element.140) | copy-start | bytes 6148
  381.4 22.0 %collective-permute-start.30 = (bf16[4,144,768]{2,1,0:T(8,128)(2,1)}, bf16[4,144,768]{2,1,0:T(8,128)(2,1)}, u32[]{:S(2)}, u32[]{:S(2)}) collective-permute-start(bf16[4,144,768]{2,1,0:T(8,128)(2,1)} %fusion.25), channel_id=1, source_target_pairs={{0,4},{4,0},{8,12},{12,8},{16,20},{20,16},{24,28},{28,24},{1,5},{5... | collective-permute-start | bytes 2654216 | tf_op jit(solution)/shard_map/ppermute | solution.py:420
  384.8 22.4 %collective-permute-start.25 = (bf16[2,256,1024]{2,1,0:T(8,128)(2,1)}, bf16[2,256,1024]{2,1,0:T(8,128)(2,1)}, u32[]{:S(2)}, u32[]{:S(2)}) collective-permute-start(bf16[2,256,1024]{2,1,0:T(8,128)(2,1)} %get-tuple-element.154), channel_id=1, source_target_pairs={{0,1},{1,0},{2,3},{3,2},{4,5},{5,4},{6,7},{7,6},{8,9},{9,8},{10,11... | collective-permute-start | bytes 3145736 | tf_op jit(solution)/shard_map/ppermute | solution.py:420
  406.7 11.5 %copy-start.15 = (f32[4,144,768]{2,1,0:T(8,128)S(1)}, f32[4,144,768]{2,1,0:T(8,128)}, u32[]{:S(2)}) copy-start(f32[4,144,768]{2,1,0:T(8,128)} %copy-done.14) | copy-start | bytes 5308420
  406.7 11.5 %collective-permute-start.31 = (bf16[2,144,768]{2,1,0:T(8,128)(2,1)}, bf16[2,144,768]{2,1,0:T(8,128)(2,1)S(1)}, u32[]{:S(2)}, u32[]{:S(2)}) collective-permute-start(bf16[2,144,768]{2,1,0:T(8,128)(2,1)} %fusion.28), channel_id=1, source_target_pairs={{0,8},{4,12},{8,0},{12,4},{16,24},{20,28},{24,16},{28,20},{1,9},{5... | collective-permute-start | bytes 1327112 | tf_op jit(solution)/shard_map/ppermute | solution.py:420
  407.2 55.4 %collective-permute-start.24 = (bf16[2,256,1024]{2,1,0:T(8,128)(2,1)}, bf16[2,256,1024]{2,1,0:T(8,128)(2,1)S(1)}, u32[]{:S(2)}, u32[]{:S(2)}) collective-permute-start(bf16[2,256,1024]{2,1,0:T(8,128)(2,1)} %get-tuple-element.153), channel_id=1, source_target_pairs={{0,1},{1,0},{2,3},{3,2},{4,5},{5,4},{6,7},{7,6},{8,9},{9,8},{10,11... | collective-permute-start | bytes 3145736 | tf_op jit(solution)/shard_map/ppermute | solution.py:420
  409.2 50.2 %collective-permute-start.26 = (bf16[2,256,1024]{2,1,0:T(8,128)(2,1)S(1)}, bf16[2,256,1024]{2,1,0:T(8,128)(2,1)S(1)}, u32[]{:S(2)}, u32[]{:S(2)}) collective-permute-start(bf16[2,256,1024]{2,1,0:T(8,128)(2,1)S(1)} %add_convert_fusion), channel_id=1, source_target_pairs={{0,2},{1,3},{2,0},{3,1},{4,6},{5,7},{6,4},{7,5},{8,10},{9,11},{10,... | collective-permute-start | bytes 3145736 | tf_op jit(solution)/shard_map/ppermute | solution.py:420
  410.5 61.2 %collective-permute-start.33 = (bf16[128,3456]{1,0:T(8,128)(2,1)}, bf16[128,3456]{1,0:T(8,128)(2,1)}, u32[]{:S(2)}, u32[]{:S(2)}) collective-permute-start(bf16[128,3456]{1,0:T(8,128)(2,1)} %reduce-scatter.2.cloned.1.call-done), channel_id=1, source_target_pairs={{0,1},{1,0},{2,3},{3,2},{4,5},{5,4},{6,7},{7,6},{8,9},{9,8},{10,11... | collective-permute-start | bytes 2654216 | tf_op jit(solution)/shard_map/ppermute | solution.py:420
  410.5 60.8 %collective-permute-start.34 = (bf16[128,3456]{1,0:T(8,128)(2,1)}, bf16[128,3456]{1,0:T(8,128)(2,1)}, u32[]{:S(2)}, u32[]{:S(2)}) collective-permute-start(bf16[128,3456]{1,0:T(8,128)(2,1)} %reduce-scatter.2.cloned.1.call-done), channel_id=1, source_target_pairs={{0,2},{1,3},{2,0},{3,1},{4,6},{5,7},{6,4},{7,5},{8,10},{9,11},{10,... | collective-permute-start | bytes 2654216 | tf_op jit(solution)/shard_map/ppermute | solution.py:420
  418.4 11.4 %collective-permute-start.32 = (bf16[1,144,768]{2,1,0:T(8,128)(2,1)S(1)}, bf16[1,144,768]{2,1,0:T(8,128)(2,1)S(1)}, u32[]{:S(2)}, u32[]{:S(2)}) collective-permute-start(bf16[1,144,768]{2,1,0:T(8,128)(2,1)S(1)} %dynamic-slice_convert_fusion.1), channel_id=1, source_target_pairs={{0,16},{4,20},{8,24},{12,28},{16,0},{20,4},{24,8},{28,12},{1,17},{... | collective-permute-start | bytes 663560 | tf_op jit(solution)/shard_map/ppermute | solution.py:420
  421.7 39.6 %copy-start.7 = (bf16[4,128,3456]{2,1,0:T(8,128)(2,1)}, bf16[4,128,3456]{2,1,0:T(8,128)(2,1)S(1)}, u32[]{:S(2)}) copy-start(bf16[4,128,3456]{2,1,0:T(8,128)(2,1)S(1)} %bitcast_dynamic-update-slice_fusion.3) | copy-start | bytes 10616836
  459.5 6.3 %copy-start.21 = (bf16[2,256,1024]{2,1,0:T(8,128)(2,1)}, bf16[2,256,1024]{2,1,0:T(8,128)(2,1)S(1)}, u32[]{:S(2)}) copy-start(bf16[2,256,1024]{2,1,0:T(8,128)(2,1)S(1)} %collective-permute-done.26) | copy-start | bytes 3145732
  462.1 5.0 %copy-start.11 = (f32[2,256,1024]{2,1,0:T(8,128)S(1)}, f32[2,256,1024]{2,1,0:T(8,128)}, u32[]{:S(2)}) copy-start(f32[2,256,1024]{2,1,0:T(8,128)} %get-tuple-element.148) | copy-start | bytes 6291460
  467.1 4.6 copy-start.8
  471.3 2.9 collective-permute-start.35
  (15 other events, 27.9 us)
Sparse Core Ops, SparseCore 0:
  12.2 49.0 all-gather.2
  64.1 106.9 all-gather.4
  262.9 126.8 reduce-scatter.1
